TPU v7x, 32 devices: a whole 2x2x4 slice. The times are simulated.
32 devices in a mesh: dp: 8 (over z, y), mp: 4 (over x, core).
Axes of the slice: x: 2, y: 2, z: 4, core: 2. Of those that a mesh axis runs over, the one named last changes fastest.
Arguments:
- hidden_in: bfloat16 [16384, 1024], P('dp', 'mp'), may hold values from -6 to 6
- cotangent: bfloat16 [16384, 1024], P('dp', 'mp'), may hold values from -6 to 6
- owners: int32 [128], replicated, may hold values from 0 to 7, as said below
- masters: float32 [4, 256, 32, 1024], P('mp', 'dp'), may hold values from -0.1875 to 0.1875
- firsts: float32 [4, 256, 32, 1024], P('mp', 'dp'), may hold values from -6 to 6
- seconds: float32 [4, 256, 32, 1024], P('mp', 'dp'), may hold values from 19.33312 to 77.66016
- width_gains: float32 [3, 1024], P(None, 'mp'), may hold values from 0.1 to 1.6, as said below
- width_first: float32 [3, 1024], P(None, 'mp'), may hold values from -32 to 32
- width_second: float32 [3, 1024], P(None, 'mp'), may hold values from 137.6256 to 552.1408
- hidden_gains: float32 [2, 4096], P(None, 'mp'), may hold values from 0.25 to 1.75
- hidden_first: float32 [2, 4096], P(None, 'mp'), may hold values from -6 to 6
- hidden_second: float32 [2, 4096], P(None, 'mp'), may hold values from 19.33312 to 77.66016
Outputs:
- hidden_out: float32 [16384, 1024], P('dp', 'mp')
- grad_in: float32 [16384, 1024], P('dp', 'mp')
- masters_new: float32 [4, 256, 32, 1024], P('mp', 'dp')
- firsts_new: float32 [4, 256, 32, 1024], P('mp', 'dp')
- seconds_new: float32 [4, 256, 32, 1024], P('mp', 'dp')
- weight_grads: float32 [4, 256, 32, 1024], P('mp', 'dp')
- width_gains_new: float32 [3, 1024], P(None, 'mp')
- width_grads: float32 [3, 1024], P(None, 'mp')
- width_first_new: float32 [3, 1024], P(None, 'mp')
- width_second_new: float32 [3, 1024], P(None, 'mp')
- hidden_gains_new: float32 [2, 4096], P(None, 'mp')
- hidden_grads: float32 [2, 4096], P(None, 'mp')
- hidden_first_new: float32 [2, 4096], P(None, 'mp')
- hidden_second_new: float32 [2, 4096], P(None, 'mp')
Inputs may be any that keep to these rules, and one draw needn't show every extreme that they name: owners[b] is the index of dp that owns row block b; no index owns more than 32 blocks, and some index owns exactly 32. `width_gains`: row 0 lies in 0.8 to 1.6, rows 1 and 2 in 0.1 to 0.8.
All inputs are finite; a program needn't handle non-finite values.
Results may differ from a plain program's by a relative error of at most 0.015.
The roundings to bfloat16 on the way count: a program that leaves them out, or rounds other values in their place, can miss the bound.
Values may be sent and summed in bfloat16 or wider, within the bound.
A program may use at most 256 MiB of HBM per device.

v0:
```python
import math

import jax
import jax.numpy as jnp
from jax import lax
from jax.sharding import PartitionSpec as P

D = 1024
HD = 64
STEP = 7


EPSILON = 1e-06
ADAM_EPSILON = 1e-08
BETA_FIRST = 0.9
BETA_SECOND = 0.95
LEARN_RATE = 0.05
GAIN_RATE = 0.6
WEIGHT_DECAY = 0.1
MASKED_SCORE = -1e30


def rows_times(left_rows, weight):
    return lax.dot_general(
        left_rows, weight, (((1,), (1,)), ((), ())), preferred_element_type=jnp.float32
    )


def across_rows(left_rows, right_rows):
    return lax.dot_general(
        left_rows, right_rows, (((0,), (0,)), ((), ())), preferred_element_type=jnp.float32
    )


def token_sum(values_in):
    return lax.psum(jnp.sum(values_in, axis=-1), "mp")


def widen_rows(stream_part):
    return lax.all_gather(stream_part.astype(jnp.bfloat16), "mp", axis=1, tiled=True)


def settle(partial_value):
    return lax.psum_scatter(partial_value, "mp", scatter_dimension=1, tiled=True)


def normalize(vector):
    inverse = lax.rsqrt(token_sum(vector * vector) / D + EPSILON)[:, None]
    return (vector * inverse, inverse)


def normalize_back(unit_rows, inverse, upstream):
    return inverse * (upstream - unit_rows * (token_sum(unit_rows * upstream) / D)[:, None])


def rope_tables(length, head_size):
    half_size = head_size // 2
    position = jnp.arange(length).astype(jnp.float32)
    frequency = jnp.exp(
        jnp.arange(half_size).astype(jnp.float32) * (-2.0 * math.log(10000.0) / head_size)
    )
    angles = position[:, None] * frequency[None, :]
    return (jnp.cos(angles)[:, None, :], jnp.sin(angles)[:, None, :])


def rotate(vector, cosine_table, sine_table):
    half_size = vector.shape[-1] // 2
    first_half = vector[..., :half_size]
    second_half = vector[..., half_size:]
    return jnp.concatenate(
        [
            first_half * cosine_table - second_half * sine_table,
            first_half * sine_table + second_half * cosine_table,
        ],
        axis=-1,
    )


def rotate_back(upstream, cosine_table, sine_table):
    half_size = upstream.shape[-1] // 2
    first_half = upstream[..., :half_size]
    second_half = upstream[..., half_size:]
    return jnp.concatenate(
        [
            first_half * cosine_table + second_half * sine_table,
            second_half * cosine_table - first_half * sine_table,
        ],
        axis=-1,
    )


def head_unit(vector):
    inverse = lax.rsqrt(jnp.sum(vector * vector, axis=-1, keepdims=True) + EPSILON)
    return (vector * inverse, inverse)


def head_unit_back(unit_rows, inverse, upstream):
    return inverse * (upstream - unit_rows * jnp.sum(unit_rows * upstream, axis=-1, keepdims=True))


def blend_branch(base_rows, branch, branch_rate):
    branch_unit, branch_inv = normalize(branch)
    mixed_rows = base_rows + branch_rate * (branch_unit - base_rows)
    mixed_unit, mixed_inv = normalize(mixed_rows)
    result = (branch_unit, branch_inv, mixed_unit, mixed_inv)
    return result


def blend_back(base_rows, branch_unit, branch_inv, mixed_unit, mixed_inv, branch_rate, upstream):
    d_mixed = normalize_back(mixed_unit, mixed_inv, upstream)
    d_branch = normalize_back(branch_unit, branch_inv, branch_rate * d_mixed)
    return (
        (1.0 - branch_rate) * d_mixed,
        d_branch,
        jnp.sum(d_mixed * (branch_unit - base_rows), axis=0),
    )


def adam_update(params, gradient, first_moment, second_moment, decay_rate, step_rate):
    first_new = BETA_FIRST * first_moment + (1.0 - BETA_FIRST) * gradient
    second_new = BETA_SECOND * second_moment + (1.0 - BETA_SECOND) * gradient * gradient
    corrected = (
        first_new
        / (1.0 - BETA_FIRST**STEP)
        / (jnp.sqrt(second_new / (1.0 - BETA_SECOND**STEP)) + ADAM_EPSILON)
    )
    return (params - step_rate * (corrected + decay_rate * params), first_new, second_new)


def shards(
    hidden_in,
    cotangent,
    owners,
    masters,
    firsts,
    seconds,
    width_gains,
    width_first,
    width_second,
    hidden_gains,
    hidden_first,
    hidden_second,
):
    tokens = hidden_in.shape[0]
    narrow = hidden_in.shape[1]
    slot_count = masters.shape[1]
    block_rows = masters.shape[2]
    blocks = owners.shape[0]
    hidden_local = hidden_gains.shape[1]
    heads_local = narrow // HD
    score_scale = float(HD) ** 0.5
    dp_index = lax.axis_index("dp")
    block_order = jnp.arange(blocks)
    same_owner = owners[:, None] == owners[None, :]
    slot_rank = jnp.sum(
        jnp.logical_and(same_owner, block_order[None, :] < block_order[:, None]).astype(jnp.int32),
        axis=1,
    )
    owned_mask = owners == dp_index
    in_use = jnp.arange(slot_count) < jnp.sum(owned_mask.astype(jnp.int32))
    spread_blocks = (
        jnp.take(masters[0], slot_rank, axis=0) * owned_mask.astype(jnp.float32)[:, None, None]
    ).astype(jnp.bfloat16)
    stacked = lax.psum(spread_blocks, "dp").astype(jnp.float32).astype(jnp.bfloat16)
    stacked = stacked.reshape(blocks * block_rows, D)
    w_query = stacked[0:narrow]
    w_key = stacked[narrow : 2 * narrow]
    w_value = stacked[2 * narrow : 3 * narrow]
    w_out = stacked[3 * narrow : 4 * narrow]
    offset = 4 * narrow
    w_up = stacked[offset : offset + hidden_local]
    w_gate = stacked[offset + hidden_local : offset + 2 * hidden_local]
    w_down = stacked[offset + 2 * hidden_local : offset + 3 * hidden_local]
    qk_heads = width_gains[0].reshape(heads_local, HD)
    rate_attn = width_gains[1]
    rate_mlp = width_gains[2]
    up_scale = hidden_gains[0]
    gate_scale = hidden_gains[1]
    stream = hidden_in.astype(jnp.float32)
    start_unit, start_inv = normalize(stream)
    operand = widen_rows(start_unit)
    query_raw = rows_times(operand, w_query)
    key_raw = rows_times(operand, w_key)
    value_heads = rows_times(operand, w_value).astype(jnp.bfloat16).reshape(tokens, heads_local, HD)
    cosine_table, sine_table = rope_tables(tokens, HD)
    query_unit, query_inv = head_unit(
        rotate(query_raw.reshape(tokens, heads_local, HD), cosine_table, sine_table)
    )
    key_unit, key_inv = head_unit(
        rotate(key_raw.reshape(tokens, heads_local, HD), cosine_table, sine_table)
    )
    queries = (qk_heads * query_unit).astype(jnp.bfloat16)
    key_rows = (qk_heads * key_unit).astype(jnp.bfloat16)
    block_size = min(512, tokens)
    block_count = tokens // block_size
    columns = jnp.arange(tokens)

    def scores_of(first_row):
        query_part = lax.dynamic_slice_in_dim(queries, first_row, block_size, 0)
        raw_scores = (
            jnp.einsum("qhd,khd->hqk", query_part, key_rows, preferred_element_type=jnp.float32)
            * score_scale
        )
        allowed = (first_row + jnp.arange(block_size))[:, None] >= columns[None, :]
        return (query_part, jnp.where(allowed[None], raw_scores, MASKED_SCORE))

    def attend(block_index):
        query_part, raw_scores = scores_of(block_index * block_size)
        row_top = jnp.max(raw_scores, axis=-1, keepdims=True)
        exp_scores = jnp.exp(raw_scores - row_top)
        row_total = jnp.sum(exp_scores, axis=-1, keepdims=True)
        prob_rows = (exp_scores / row_total).astype(jnp.bfloat16)
        mixed_heads = jnp.einsum(
            "hqk,khd->qhd", prob_rows, value_heads, preferred_element_type=jnp.float32
        )
        return (mixed_heads, (row_top + jnp.log(row_total))[..., 0])

    mixed_all, log_totals = lax.map(attend, jnp.arange(block_count))
    attended = mixed_all.reshape(tokens, narrow).astype(jnp.bfloat16)
    attn_branch = settle(jnp.dot(attended, w_out, preferred_element_type=jnp.float32))
    attn_unit, attn_inv, middle, middle_inv = blend_branch(start_unit, attn_branch, rate_attn)
    middle_rows = widen_rows(middle)
    up_raw = rows_times(middle_rows, w_up)
    gate_raw = rows_times(middle_rows, w_gate)
    up_val = up_scale * up_raw
    gate_val = gate_scale * gate_raw
    sigmoid_gate = jax.nn.sigmoid(gate_val)
    activated = gate_val * sigmoid_gate
    product = (up_val * activated).astype(jnp.bfloat16)
    mlp_branch = settle(jnp.dot(product, w_down, preferred_element_type=jnp.float32))
    mlp_unit, mlp_inv, hidden_out, out_inv = blend_branch(middle, mlp_branch, rate_mlp)
    grad_out = cotangent.astype(jnp.float32)
    d_middle, d_mlp, g_rate_mlp = blend_back(
        middle, mlp_unit, mlp_inv, hidden_out, out_inv, rate_mlp, grad_out
    )
    grad_rows = widen_rows(d_mlp)
    d_product = rows_times(grad_rows, w_down)
    g_down = across_rows(product, grad_rows)
    d_up = d_product * activated
    d_gate = d_product * up_val * (sigmoid_gate * (1.0 + gate_val * (1.0 - sigmoid_gate)))
    g_up_scale = jnp.sum(d_up * up_raw, axis=0)
    g_gate_scale = jnp.sum(d_gate * gate_raw, axis=0)
    d_up_raw = (d_up * up_scale).astype(jnp.bfloat16)
    d_gate_raw = (d_gate * gate_scale).astype(jnp.bfloat16)
    d_middle = d_middle + settle(
        jnp.dot(d_up_raw, w_up, preferred_element_type=jnp.float32)
        + jnp.dot(d_gate_raw, w_gate, preferred_element_type=jnp.float32)
    )
    g_up = across_rows(d_up_raw, middle_rows)
    g_gate = across_rows(d_gate_raw, middle_rows)
    d_start, d_attn, g_rate_attn = blend_back(
        start_unit, attn_unit, attn_inv, middle, middle_inv, rate_attn, d_middle
    )
    attn_grad_rows = widen_rows(d_attn)
    d_attended = rows_times(attn_grad_rows, w_out).astype(jnp.bfloat16)
    g_out = across_rows(attended, attn_grad_rows)
    d_heads = d_attended.reshape(tokens, heads_local, HD)

    def attend_back(carried, block_index):
        key_acc, value_acc = carried
        first_row = block_index * block_size
        query_part, raw_scores = scores_of(first_row)
        log_total = log_totals[block_index]
        prob_rows = jnp.exp(raw_scores - log_total[..., None])
        d_part = lax.dynamic_slice_in_dim(d_heads, first_row, block_size, 0)
        d_probs = jnp.einsum(
            "qhd,khd->hqk", d_part, value_heads, preferred_element_type=jnp.float32
        )
        d_scores = (
            prob_rows * (d_probs - jnp.sum(prob_rows * d_probs, axis=-1, keepdims=True))
        ).astype(jnp.bfloat16)
        d_query_part = (
            jnp.einsum("hqk,khd->qhd", d_scores, key_rows, preferred_element_type=jnp.float32)
            * score_scale
        )
        key_acc = (
            key_acc
            + jnp.einsum("hqk,qhd->khd", d_scores, query_part, preferred_element_type=jnp.float32)
            * score_scale
        )
        value_acc = value_acc + jnp.einsum(
            "hqk,qhd->khd",
            prob_rows.astype(jnp.bfloat16),
            d_part,
            preferred_element_type=jnp.float32,
        )
        return ((key_acc, value_acc), d_query_part)

    zero_heads = jnp.zeros((tokens, heads_local, HD), jnp.float32)
    (d_keys, d_values), d_query_blocks = lax.scan(
        attend_back, (zero_heads, zero_heads), jnp.arange(block_count)
    )
    d_queries = d_query_blocks.reshape(tokens, heads_local, HD)
    g_qk = jnp.sum(d_queries * query_unit + d_keys * key_unit, axis=0).reshape(narrow)
    d_query_raw = rotate_back(
        head_unit_back(query_unit, query_inv, d_queries * qk_heads), cosine_table, sine_table
    )
    d_key_raw = rotate_back(
        head_unit_back(key_unit, key_inv, d_keys * qk_heads), cosine_table, sine_table
    )
    grads_query = d_query_raw.reshape(tokens, narrow).astype(jnp.bfloat16)
    grads_key = d_key_raw.reshape(tokens, narrow).astype(jnp.bfloat16)
    grads_value = d_values.reshape(tokens, narrow).astype(jnp.bfloat16)
    d_start = d_start + settle(
        jnp.dot(grads_query, w_query, preferred_element_type=jnp.float32)
        + jnp.dot(grads_key, w_key, preferred_element_type=jnp.float32)
        + jnp.dot(grads_value, w_value, preferred_element_type=jnp.float32)
    )
    g_query = across_rows(grads_query, operand)
    g_key = across_rows(grads_key, operand)
    g_value = across_rows(grads_value, operand)
    grad_in = normalize_back(start_unit, start_inv, d_start)
    local_grads = jnp.concatenate(
        [g_query, g_key, g_value, g_out, g_up, g_gate, g_down], axis=0
    ).reshape(blocks, block_rows, D)
    summed = lax.psum(local_grads, "dp")
    target = jnp.where(owned_mask, slot_rank, slot_count)
    owned = (
        jnp.zeros((slot_count + 1, block_rows, D), jnp.float32).at[target].set(summed)[:slot_count]
    )
    width_local = jnp.stack([g_qk, g_rate_attn, g_rate_mlp], axis=0)
    hidden_grads_local = jnp.stack([g_up_scale, g_gate_scale], axis=0)
    width_total, hidden_total = lax.psum((width_local, hidden_grads_local), "dp")
    stepped, firsts_step, seconds_step = adam_update(
        masters[0], owned, firsts[0], seconds[0], WEIGHT_DECAY, LEARN_RATE
    )
    renormed = stepped * lax.rsqrt(jnp.sum(stepped * stepped, axis=-1, keepdims=True) + EPSILON)
    slot_live = in_use[:, None, None]
    masters_new = jnp.where(slot_live, renormed, 0.0)[None]
    firsts_new = jnp.where(slot_live, firsts_step, 0.0)[None]
    seconds_new = jnp.where(slot_live, seconds_step, 0.0)[None]
    weight_grads = jnp.where(slot_live, owned, 0.0)[None]
    width_new, width_first_new, width_second_new = adam_update(
        width_gains, width_total, width_first, width_second, 0.0, GAIN_RATE
    )
    hidden_new, hidden_first_new, hidden_second_new = adam_update(
        hidden_gains, hidden_total, hidden_first, hidden_second, 0.0, GAIN_RATE
    )
    return (
        hidden_out,
        grad_in,
        masters_new,
        firsts_new,
        seconds_new,
        weight_grads,
        width_new,
        width_total,
        width_first_new,
        width_second_new,
        hidden_new,
        hidden_total,
        hidden_first_new,
        hidden_second_new,
    )


def solution(mesh):
    in_specs = (
        P("dp", "mp"),
        P("dp", "mp"),
        P(),
        P("mp", "dp", None, None),
        P("mp", "dp", None, None),
        P("mp", "dp", None, None),
        P(None, "mp"),
        P(None, "mp"),
        P(None, "mp"),
        P(None, "mp"),
        P(None, "mp"),
        P(None, "mp"),
    )
    out_specs = (
        P("dp", "mp"),
        P("dp", "mp"),
        P("mp", "dp", None, None),
        P("mp", "dp", None, None),
        P("mp", "dp", None, None),
        P("mp", "dp", None, None),
        P(None, "mp"),
        P(None, "mp"),
        P(None, "mp"),
        P(None, "mp"),
        P(None, "mp"),
        P(None, "mp"),
        P(None, "mp"),
        P(None, "mp"),
    )
    return jax.shard_map(shards, mesh=mesh, in_specs=in_specs, out_specs=out_specs, check_vma=False)
```

profile of v0, /device:TPU:8, one launch (start us, length us, event | category | flops | bytes accessed | tf_op | source)
XLA Modules:
  0.0 1736.2 jit_solution(8989670986887148688)
XLA Ops:
  10.2 12.0 gather_fusion
  22.2 10.1 multiply_convert_fusion.1
  45.7 256.7 %all-reduce.4.cloned.1.call-done = bf16[128,32,1024]{2,1,0:T(8,128)(2,1)} async-done(((bf16[128,32,1024]{2,1,0:T(8,128)(2,1)}), bf16[128,32,1024]{2,1,0:T(8,128)(2,1)}) %all-reduce.4.cloned.1.call-update) | async-done | bytes 8388624 | tf_op jit(solution)/shard_map/psum | solution.py:164
  314.6 64.2 %while.30 = (s32[]{:T(128)}, bf16[4,512,4,64]{1,3,2,0:T(8,128)(2,1)}, f32[4,4,512]{2,1,0:T(4,128)}, s32[4]{0:T(128)S(1)}, bf16[2048,4,64]{0,2,1:T(8,128)(2,1)S(1...) while((s32[]{:T(128)}, ...), condition=%wide.region_9.10_spmd.clone.clone, body=%wide.region_6.0_spmd.clone.sunk.clone | while | flops 1125120512 | bytes 57480344 | solution.py:218
  387.5 72.4 %reduce-scatter.5.cloned.1.call-done = f32[2048,256]{1,0:T(8,128)} async-done(((f32[2048,1024]{1,0:T(8,128)}), f32[2048,256]{1,0:T(8,128)}) %reduce-scatter.5.cloned.1.call-update) | async-done | bytes 2097168 | tf_op jit(solution)/shard_map/reduce_scatter | solution.py:44
  484.0 29.1 %all-gather.7.cloned.1.call-done = bf16[2048,1024]{1,0:T(8,128)(2,1)} async-done(((bf16[2048,256]{1,0:T(8,128)(2,1)}), bf16[2048,1024]{1,0:T(8,128)(2,1)}) %all-gather.7.cloned.1.call-update) | async-done | bytes 4194320 | tf_op jit(solution)/shard_map/all_gather | solution.py:40
  513.1 10.8 fusion.82
  524.0 10.8 multiply_convert_fusion.4
  543.5 71.7 %reduce-scatter.7.cloned.1.call-done = f32[2048,256]{1,0:T(8,128)} async-done(((f32[2048,1024]{1,0:T(8,128)}), f32[2048,256]{1,0:T(8,128)}) %reduce-scatter.7.cloned.1.call-update) | async-done | bytes 2097168 | tf_op jit(solution)/shard_map/reduce_scatter | solution.py:44
  655.8 35.0 %all-gather.9.cloned.1.call-done = bf16[2048,1024]{1,0:T(8,128)(2,1)} async-done(((bf16[2048,256]{1,0:T(8,128)(2,1)}), bf16[2048,1024]{1,0:T(8,128)(2,1)}) %all-gather.9.cloned.1.call-update) | async-done | bytes 4194320 | tf_op jit(solution)/shard_map/all_gather | solution.py:40
  690.9 16.7 multiply_reduce_fusion.2
  707.6 12.1 fusion.84
  719.6 8.9 convolution_add_fusion
  728.7 71.7 %reduce-scatter.9.cloned.1.call-done = f32[2048,256]{1,0:T(8,128)} async-done(((f32[2048,1024]{1,0:T(8,128)}), f32[2048,256]{1,0:T(8,128)}) %reduce-scatter.9.cloned.1.call-update) | async-done | bytes 2097168 | tf_op jit(solution)/shard_map/reduce_scatter | solution.py:44
  826.4 33.6 %all-gather.11.cloned.1.call-done = bf16[2048,1024]{1,0:T(8,128)(2,1)} async-done(((bf16[2048,256]{1,0:T(8,128)(2,1)}), bf16[2048,1024]{1,0:T(8,128)(2,1)}) %all-gather.11.cloned.1.call-update) | async-done | bytes 4194320 | tf_op jit(solution)/shard_map/all_gather | solution.py:40
  864.5 251.8 %while.31 = (s32[]{:T(128)}, f32[2048,4,64]{0,2,1:T(8,128)}, f32[2048,4,64]{0,2,1:T(8,128)}, f32[4,512,4,64]{1,3,2,0:T(8,128)}, s32[4]{0:T(128)S(1)}, /*index=5*...) while((s32[]{:T(128)}, f32[2048,4,64]{0,2,1:T(8,128)}, ...), condition=%wide.region_31.32_spmd.clone.clone, body=%wide.region_29.31_spmd.clone.sunk.clone | while | flops 2751068672 | bytes 248050624 | solution.py:290
  866.0 9.0 fusion.182
  879.4 15.8 multiply_reduce_fusion.18
  896.5 10.9 multiply_convert_fusion.14
  928.3 9.0 fusion.182
  941.7 15.8 multiply_reduce_fusion.18
  958.9 10.9 multiply_convert_fusion.14
  991.3 9.0 fusion.182
  1004.7 15.8 multiply_reduce_fusion.18
  1021.8 10.9 multiply_convert_fusion.14
  1054.2 9.0 fusion.182
  1067.6 15.8 multiply_reduce_fusion.18
  1084.8 10.9 multiply_convert_fusion.14
  1167.8 36.3 %all-reduce = (f32[3,256]{1,0:T(4,128)S(1)}, f32[2,1024]{1,0:T(2,128)S(1)}) all-reduce(f32[3,256]{1,0:T(4,128)S(1)} %pad_maximum_fusion.3, f32[2,1024]{1,0:T(2,128)S(1)} %pad_maximum_fusion.2), channel_id=1, replica_groups=mesh['dp'=8,'mp'=4] {'dp'}, use_global_device_ids=true, to_apply=%region_44.45 | all-reduce | flops 2816 | bytes 22528 | tf_op jit(solution)/shard_map/psum | solution.py:323
  1205.3 459.5 %all-reduce.6.cloned.1.call-done = f32[128,32,1024]{2,1,0:T(8,128)} async-done(((f32[128,32,1024]{2,1,0:T(8,128)}), f32[128,32,1024]{2,1,0:T(8,128)}) %all-reduce.6.cloned.1.call-update) | async-done | bytes 16777232 | tf_op jit(solution)/shard_map/psum | solution.py:316
  1667.4 31.6 %scatter_fusion = f32[33,32,1024]{2,1,0:T(8,128)} fusion(f32[33,32,1024]{2,1,0:T(8,128)} %broadcast_in_dim.130, s32[128]{0:T(128)S(1)} %get-tuple-element.270, f32[128,32,1024]{2,1,0:T(8,128)} %all-reduce.6.cloned.1.call-done), kind=kCustom, calls=%fused_computation.1 | custom fusion | bytes 50332160 | tf_op jit(solution)/shard_map/scatter | solution.py:319
  1699.0 13.3 multiply_reduce_fusion.3
  (413 shorter events, 370.0 us)
Async XLA Ops:
  8.0 294.3 %all-reduce.4.cloned.1.call-start = ((), (), s32[]{:S(2)}) async-start(), calls=%async_computation.5 | async-start | bytes 16777216 | tf_op jit(solution)/shard_map/psum | solution.py:164
  32.3 272.8 %all-gather.5.cloned.1.call-start = ((), (), s32[]{:S(2)}) async-start(), calls=%async_computation.4 | async-start | bytes 5242880 | tf_op jit(solution)/shard_map/all_gather | solution.py:40
  42.8 417.1 %reduce-scatter.5.cloned.1.call-start = ((), (), s32[]{:S(2)}) async-start(), calls=%async_computation.6 | async-start | bytes 10485760 | tf_op jit(solution)/shard_map/reduce_scatter | solution.py:44
  43.6 268.3 %copy-start.56 = (f32[4,64]{1,0:T(4,128)}, f32[4,64]{1,0:T(4,128)S(1)}, u32[]{:S(2)}) copy-start(f32[4,64]{1,0:T(4,128)S(1)} %mul.806) | copy-start | bytes 3076
  45.7 264.8 %copy-start.29 = (f32[2048,32]{0,1:T(8,128)}, f32[2048,32]{0,1:T(8,128)S(1)}, u32[]{:S(2)}) copy-start(f32[2048,32]{0,1:T(8,128)S(1)} %get-tuple-element.258) | copy-start | bytes 786436
  45.7 264.8 %copy-start.31 = (f32[2048,32]{0,1:T(8,128)}, f32[2048,32]{0,1:T(8,128)S(1)}, u32[]{:S(2)}) copy-start(f32[2048,32]{0,1:T(8,128)S(1)} %get-tuple-element.259) | copy-start | bytes 786436
  387.5 80.6 %copy-start.54 = (f32[2048]{0:T(1024)S(1)}, f32[2048]{0:T(1024)}, u32[]{:S(2)}) copy-start(f32[2048]{0:T(1024)} %copy-done.53) | copy-start | bytes 24580
  387.5 80.6 %copy-start.61 = (f32[1,256]{1,0:T(1,128)S(1)}, f32[1,256]{1,0:T(1,128)}, u32[]{:S(2)}) copy-start(f32[1,256]{1,0:T(1,128)} %get-tuple-element.265) | copy-start | bytes 3076
  387.5 125.6 %all-gather.7.cloned.1.call-start = ((), (), s32[]{:S(2)}) async-start(), calls=%async_computation.7 | async-start | bytes 5242880 | tf_op jit(solution)/shard_map/all_gather | solution.py:40
  477.6 137.6 %reduce-scatter.7.cloned.1.call-start = ((), (), s32[]{:S(2)}) async-start(), calls=%async_computation.8 | async-start | bytes 10485760 | tf_op jit(solution)/shard_map/reduce_scatter | solution.py:44
  478.1 241.5 %copy-start.51 = (f32[1,1024]{1,0:T(1,128)}, f32[1,1024]{1,0:T(1,128)S(1)}, u32[]{:S(2)}) copy-start(f32[1,1024]{1,0:T(1,128)S(1)} %get-tuple-element.260) | copy-start | bytes 12292
  543.4 79.9 %copy-start.60 = (f32[1,256]{1,0:T(1,128)S(1)}, f32[1,256]{1,0:T(1,128)}, u32[]{:S(2)}) copy-start(f32[1,256]{1,0:T(1,128)} %get-tuple-element.266) | copy-start | bytes 3076
  543.5 147.4 %all-gather.9.cloned.1.call-start = ((), (), s32[]{:S(2)}) async-start(), calls=%async_computation.9 | async-start | bytes 5242880 | tf_op jit(solution)/shard_map/all_gather | solution.py:40
  655.8 144.6 %reduce-scatter.9.cloned.1.call-start = ((), (), s32[]{:S(2)}) async-start(), calls=%async_computation.10 | async-start | bytes 10485760 | tf_op jit(solution)/shard_map/reduce_scatter | solution.py:44
  690.9 16.7 copy-start.38
  728.6 71.8 %copy-start.64 = (f32[1,256]{1,0:T(1,128)S(1)}, f32[1,256]{1,0:T(1,128)}, u32[]{:S(2)}) copy-start(f32[1,256]{1,0:T(1,128)} %get-tuple-element.263) | copy-start | bytes 3076
  728.6 131.3 %all-gather.11.cloned.1.call-start = ((), (), s32[]{:S(2)}) async-start(), calls=%async_computation.11 | async-start | bytes 5242880 | tf_op jit(solution)/shard_map/all_gather | solution.py:40
  824.1 840.7 %all-reduce.6.cloned.1.call-start = ((), (), s32[]{:S(2)}) async-start(), calls=%async_computation.13 | async-start | bytes 33554432 | tf_op jit(solution)/shard_map/psum | solution.py:316
  879.4 15.8 slice-start.2
  879.4 17.1 slice-start.3
  941.7 17.1 slice-start.3
  1004.7 17.1 slice-start.3
  1067.6 17.1 slice-start.3
  1156.6 555.8 %reduce-scatter.11.cloned.1.call-start = ((), (), s32[]{:S(2)}) async-start(), calls=%async_computation.12 | async-start | bytes 10485760 | tf_op jit(solution)/shard_map/reduce_scatter | solution.py:44
  1165.7 38.3 %copy-start.63 = (f32[3,256]{1,0:T(4,128)S(1)}, f32[3,256]{1,0:T(4,128)}, u32[]{:S(2)}) copy-start(f32[3,256]{1,0:T(4,128)} %param.22) | copy-start | bytes 9220
  1165.7 38.3 %copy-start.71 = (f32[3,256]{1,0:T(4,128)S(1)}, f32[3,256]{1,0:T(4,128)}, u32[]{:S(2)}) copy-start(f32[3,256]{1,0:T(4,128)} %param.23) | copy-start | bytes 9220
  1165.7 38.3 %copy-start.72 = (f32[3,256]{1,0:T(4,128)S(1)}, f32[3,256]{1,0:T(4,128)}, u32[]{:S(2)}) copy-start(f32[3,256]{1,0:T(4,128)} %param.24) | copy-start | bytes 9220
  1165.8 38.9 %copy-start.59 = (f32[2,1024]{1,0:T(2,128)S(1)}, f32[2,1024]{1,0:T(2,128)}, u32[]{:S(2)}) copy-start(f32[2,1024]{1,0:T(2,128)} %param.25) | copy-start | bytes 24580
  1165.8 38.9 %copy-start.66 = (f32[2,1024]{1,0:T(2,128)S(1)}, f32[2,1024]{1,0:T(2,128)}, u32[]{:S(2)}) copy-start(f32[2,1024]{1,0:T(2,128)} %param.26) | copy-start | bytes 24580
  1165.8 38.9 %copy-start.67 = (f32[2,1024]{1,0:T(2,128)S(1)}, f32[2,1024]{1,0:T(2,128)}, u32[]{:S(2)}) copy-start(f32[2,1024]{1,0:T(2,128)} %param.27) | copy-start | bytes 24580
  1204.0 494.9 %copy-start.68 = (f32[2,1024]{1,0:T(2,128)}, f32[2,1024]{1,0:T(2,128)S(1)}, u32[]{:S(2)}) copy-start(f32[2,1024]{1,0:T(2,128)S(1)} %get-tuple-element.213) | copy-start | bytes 24580
  1204.0 494.9 %copy-start.73 = (f32[3,256]{1,0:T(4,128)}, f32[3,256]{1,0:T(4,128)S(1)}, u32[]{:S(2)}) copy-start(f32[3,256]{1,0:T(4,128)S(1)} %get-tuple-element.212) | copy-start | bytes 9220
  (94 other events, 540.5 us)
Sparse Core Ops, SparseCore 0:
  32.4 269.8 all-reduce.3
  1156.7 508.0 all-reduce.5
Sparse Core Ops, SparseCore 1:
  42.9 35.1 all-gather.4
  387.6 72.3 reduce-scatter.4
  477.7 35.4 all-gather.6
  543.6 71.6 reduce-scatter.6
  655.8 35.0 all-gather.8
  728.7 71.6 reduce-scatter.8
  824.2 35.7 all-gather.10
  1165.9 71.8 reduce-scatter.10
where the time goes:
time: 1750 us; the launch traced here: 1740 us
  waiting for transfers between devices  1030 us (59%)
  matrix products  328 us (19%)
  other arithmetic  154 us (9%)
  blocking collectives  99.1 us (6%)
  local copies, waits for them, and re-layouts  93.8 us (5%)
    psum x1, waiting for transfers between devices, shards(): summed = lax.psum(local_grads, 'dp')  460 us
    psum x1, waiting for transfers between devices, shards(): lax.psum(spread_blocks, 'dp').astype(jnp.float32).astype(jnp.bfloat16)  257 us
    reduce_scatter x4, waiting for transfers between devices, settle(): lax.psum_scatter(partial_value, 'mp', scatter_dimension=1, tiled=True)  216 us
    all_gather x4, waiting for transfers between devices, widen_rows(): lax.all_gather(stream_part.astype(jnp.bfloat16), 'mp', axis=1, tiled=True)  97.7 us
    dot_general x4, matrix products, attend_back(): jnp.einsum('qhd,khd->hqk', d_part, value_heads, preferred_element_type=jn...  63 us
    psum x10, blocking collectives, token_sum(): return lax.psum(jnp.sum(values_in, axis=-1), 'mp')  62.8 us
    dot_general x7, matrix products, rows_times(): lax.dot_general(left_rows, weight, (((1,), (1,)), ((), ())), preferred_el...  49.4 us
    dot_general x8, matrix products, scores_of(): jnp.einsum('qhd,khd->hqk', query_part, key_rows, preferred_element_type=j...  49.1 us
  transfers between devices with their start and end apart: 10, of which 8 were waited for; matrix products, arithmetic and copies ran while one was open for 4% of the time, Pallas kernels for 0%

commit v1 on v0

v1 whole, which is shorter than its diff:
```python
import functools
import math

import jax
import jax.numpy as jnp
from jax import lax
from jax.experimental import pallas as pl
from jax.experimental.pallas import tpu as pltpu
from jax.sharding import PartitionSpec as P

D = 1024
HD = 64
STEP = 7
LANES = 128
STEPS = 4

EPSILON = 1e-06
ADAM_EPSILON = 1e-08
BETA_FIRST = 0.9
BETA_SECOND = 0.95
LEARN_RATE = 0.05
GAIN_RATE = 0.6
WEIGHT_DECAY = 0.1
SCORE_SCALE = float(HD) ** 0.5

f32 = jnp.float32
bf16 = jnp.bfloat16


def nn(left, right):
    return jnp.dot(left, right, preferred_element_type=f32)


def nt(left, right):
    return lax.dot_general(left, right, (((1,), (1,)), ((), ())), preferred_element_type=f32)


def tn(left, right):
    return lax.dot_general(left, right, (((0,), (0,)), ((), ())), preferred_element_type=f32)


def normalize(vector):
    inverse = lax.rsqrt(jnp.sum(vector * vector, axis=-1, keepdims=True) / D + EPSILON)
    return (vector * inverse, inverse)


def normalize_back(unit_rows, inverse, upstream):
    return inverse * (upstream - unit_rows * (jnp.sum(unit_rows * upstream, axis=-1, keepdims=True) / D))


def blend_branch(base_rows, branch, branch_rate):
    branch_unit, branch_inv = normalize(branch)
    mixed_unit, mixed_inv = normalize(base_rows + branch_rate * (branch_unit - base_rows))
    return (branch_unit, branch_inv, mixed_unit, mixed_inv)


def blend_back(base_rows, branch_unit, branch_inv, mixed_unit, mixed_inv, branch_rate, upstream):
    d_mixed = normalize_back(mixed_unit, mixed_inv, upstream)
    d_branch = normalize_back(branch_unit, branch_inv, branch_rate * d_mixed)
    return (
        (1.0 - branch_rate) * d_mixed,
        d_branch,
        jnp.sum(d_mixed * (branch_unit - base_rows), axis=0),
    )


def adam_update(params, gradient, first_moment, second_moment, decay_rate, step_rate):
    first_new = BETA_FIRST * first_moment + (1.0 - BETA_FIRST) * gradient
    second_new = BETA_SECOND * second_moment + (1.0 - BETA_SECOND) * gradient * gradient
    corrected = (
        first_new
        / (1.0 - BETA_FIRST**STEP)
        / (jnp.sqrt(second_new / (1.0 - BETA_SECOND**STEP)) + ADAM_EPSILON)
    )
    return (params - step_rate * (corrected + decay_rate * params), first_new, second_new)


def swap_halves(pair, lane):
    return jnp.where(
        lane % HD < HD // 2, pltpu.roll(pair, LANES - HD // 2, 1), pltpu.roll(pair, HD // 2, 1)
    )


def head_sums(values):
    width = values.shape[1]
    row = lax.broadcasted_iota(jnp.int32, (width, width), 0) // HD
    column = lax.broadcasted_iota(jnp.int32, (width, width), 1) // HD
    same = jnp.where(row == column, 1.0, 0.0).astype(bf16)
    high = values.astype(bf16)
    rest = values - high.astype(f32)
    middle = rest.astype(bf16)
    low = (rest - middle.astype(f32)).astype(bf16)
    return nn(high, same) + nn(middle, same) + nn(low, same)


def project_kernel(
    narrow, x_ref, w_ref, gain_ref, cos_ref, sin_ref, op_ref, q_ref, k_ref, v_ref, qr_ref, kr_ref
):
    rows = x_ref.shape[1]
    x = jnp.concatenate([x_ref[d] for d in range(x_ref.shape[0])], axis=1).astype(f32)
    operand = (x * lax.rsqrt(jnp.sum(x * x, axis=1, keepdims=True) / D + EPSILON)).astype(bf16)
    op_ref[...] = operand
    lane = lax.broadcasted_iota(jnp.int32, (rows, LANES), 1)
    cosine, sine = cos_ref[...], sin_ref[...]
    raw = nt(operand, w_ref[...])
    pairs = range(narrow // LANES)
    for which in range(2):
        out_ref, rot_ref = ((q_ref, qr_ref), (k_ref, kr_ref))[which]
        fill = (0.0, 1.0)[which]
        turned = []
        for pair in pairs:
            here = raw[:, which * narrow + pair * LANES : which * narrow + (pair + 1) * LANES]
            turned.append(here * cosine + swap_halves(here, lane) * sine)
        turned = jnp.concatenate(turned, axis=1)
        rot_ref[...] = turned
        gained = gain_ref[...] * (turned * lax.rsqrt(head_sums(turned * turned) + EPSILON))
        gained = gained.astype(bf16).astype(f32)
        if which == 0:
            gained = gained * SCORE_SCALE
        for pair in pairs:
            here = gained[:, pair * LANES : (pair + 1) * LANES]
            out_ref[2 * pair] = jnp.where(lane < HD, here, fill).astype(bf16)
            out_ref[2 * pair + 1] = jnp.where(lane < HD, pltpu.roll(here, HD, 1), fill).astype(bf16)
    for pair in range(narrow // LANES):
        here = raw[:, 2 * narrow + pair * LANES : 2 * narrow + (pair + 1) * LANES]
        v_ref[2 * pair] = jnp.where(lane < HD, here, 1.0).astype(bf16)
        v_ref[2 * pair + 1] = jnp.where(lane < HD, pltpu.roll(here, HD, 1), 1.0).astype(bf16)


def project(x_all, weights, gain, cosine, sine):
    size, tokens, narrow = x_all.shape
    heads = narrow // HD
    rows = min(512, tokens)
    head_spec = pl.BlockSpec((heads, rows, LANES), lambda i: (0, i, 0))
    row_spec = lambda width: pl.BlockSpec((rows, width), lambda i: (i, 0))
    whole = lambda a: pl.BlockSpec(a.shape, lambda i: (0, 0))
    return pl.pallas_call(
        functools.partial(project_kernel, narrow),
        grid=(tokens // rows,),
        in_specs=[pl.BlockSpec((size, rows, narrow), lambda i: (0, i, 0)), pl.BlockSpec((3 * narrow, D), lambda i: (0, 0)), whole(gain), row_spec(LANES), row_spec(LANES)],
        out_specs=[row_spec(D), head_spec, head_spec, head_spec, row_spec(narrow), row_spec(narrow)],
        out_shape=[jax.ShapeDtypeStruct((tokens, D), bf16)]
        + [jax.ShapeDtypeStruct((heads, tokens, LANES), bf16)] * 3
        + [jax.ShapeDtypeStruct((tokens, narrow), f32)] * 2,
        cost_estimate=pl.CostEstimate(
            flops=2 * tokens * D * 3 * narrow, bytes_accessed=tokens * D * 8, transcendentals=0
        ),
        name="project",
    )(x_all, weights, gain, cosine, sine)


def attend_kernel(block, q_ref, k_ref, v_ref, att_ref, o_ref):
    i = pl.program_id(1)
    lane = lax.broadcasted_iota(jnp.int32, (block, LANES), 1)
    queries = [q_ref[h] for h in range(2)]

    def step(j, sums, diagonal):
        rows = pl.ds(pl.multiple_of(j * block, block), block)
        new = []
        for h in range(2):
            weight = jnp.exp(nt(queries[h], k_ref[h, rows, :]))
            if diagonal:
                row = lax.broadcasted_iota(jnp.int32, weight.shape, 0)
                column = lax.broadcasted_iota(jnp.int32, weight.shape, 1)
                weight = jnp.where(row >= column, weight, 0.0)
            new.append(sums[h] + nn(weight.astype(bf16), v_ref[h, rows, :]))
        return tuple(new)

    zero = jnp.zeros((block, LANES), f32)
    sums = lax.fori_loop(0, i, lambda j, s: step(j, s, False), (zero, zero))
    sums = step(i, sums, True)
    mixed = []
    for h in range(2):
        total = pltpu.roll(sums[h], HD, 1)
        o_ref[h] = jnp.where(lane < HD, sums[h] / total, jnp.log(sums[h]))
        mixed.append(o_ref[h])
    att_ref[...] = jnp.where(lane < HD, mixed[0], pltpu.roll(mixed[1], HD, 1)).astype(bf16)


def attend(queries, keys, values):
    heads, tokens, _ = queries.shape
    block = min(512, tokens)
    part = pl.BlockSpec((2, block, LANES), lambda p, i: (p, i, 0))
    whole = pl.BlockSpec((2, tokens, LANES), lambda p, i: (p, 0, 0))
    return pl.pallas_call(
        functools.partial(attend_kernel, block),
        grid=(heads // 2, tokens // block),
        in_specs=[part, whole, whole],
        out_specs=[pl.BlockSpec((block, LANES), lambda p, i: (i, p)), part],
        out_shape=[
            jax.ShapeDtypeStruct((tokens, heads * HD), bf16),
            jax.ShapeDtypeStruct((heads, tokens, LANES), f32),
        ],
        cost_estimate=pl.CostEstimate(
            flops=heads * tokens * tokens * LANES * 4,
            bytes_accessed=heads * tokens * LANES * 10,
            transcendentals=heads * tokens * tokens // 2,
        ),
        name="attend",
    )(queries, keys, values)


def with_parts(lane, base, value):
    high = value.astype(bf16).astype(f32)
    rest = value - high
    middle = rest.astype(bf16).astype(f32)
    low = rest - middle
    tail = jnp.where(lane == HD, high, jnp.where(lane == HD + 1, middle, jnp.where(lane == HD + 2, low, 0.0)))
    return jnp.where(lane < HD, base, tail).astype(bf16)


def attend_back_kernel(
    block, q_ref, k_ref, v_ref, o_ref, do_ref, dq_ref, dk_ref, dv_ref, dk_sum, dv_sum
):
    i = pl.program_id(1)
    count = pl.num_programs(1)
    lane = lax.broadcasted_iota(jnp.int32, (block, LANES), 1)

    @pl.when(i == 0)
    def _():
        dk_sum[...] = jnp.zeros_like(dk_sum)
        dv_sum[...] = jnp.zeros_like(dv_sum)

    d_pair = do_ref[...].astype(f32)
    d_heads = [d_pair, pltpu.roll(d_pair, HD, 1)]
    queries, upstream = [], []
    for h in range(2):
        mixed = o_ref[h]
        delta = jnp.sum(jnp.where(lane < HD, mixed * d_heads[h], 0.0), axis=1, keepdims=True)
        queries.append(with_parts(lane, q_ref[h].astype(f32), -mixed))
        upstream.append(with_parts(lane, d_heads[h], -jnp.broadcast_to(delta, (block, LANES))))

    def step(j, sums, diagonal):
        rows = pl.ds(pl.multiple_of(j * block, block), block)
        new = []
        for h in range(2):
            keys = k_ref[h, rows, :]
            probs = jnp.exp(nt(keys, queries[h]))
            if diagonal:
                row = lax.broadcasted_iota(jnp.int32, probs.shape, 0)
                column = lax.broadcasted_iota(jnp.int32, probs.shape, 1)
                probs = jnp.where(column >= row, probs, 0.0)
            d_scores = (probs * nt(v_ref[h, rows, :], upstream[h])).astype(bf16)
            dv_sum[h, rows, :] += nn(probs.astype(bf16), upstream[h])
            dk_sum[h, rows, :] += nn(d_scores, queries[h])
            new.append(sums[h] + tn(d_scores, keys))
        return tuple(new)

    zero = jnp.zeros((block, LANES), f32)
    sums = lax.fori_loop(0, i, lambda j, s: step(j, s, False), (zero, zero))
    sums = step(i, sums, True)
    dq_ref[...] = jnp.where(lane < HD, sums[0], pltpu.roll(sums[1], HD, 1)) * SCORE_SCALE

    @pl.when(i == count - 1)
    def _():
        def put(j, carry):
            rows = pl.ds(pl.multiple_of(j * block, block), block)
            dk_ref[rows, :] = jnp.where(lane < HD, dk_sum[0, rows, :], pltpu.roll(dk_sum[1, rows, :], HD, 1))
            dv_ref[rows, :] = jnp.where(lane < HD, dv_sum[0, rows, :], pltpu.roll(dv_sum[1, rows, :], HD, 1))
            return carry

        lax.fori_loop(0, count, put, 0)


def attend_back(queries, keys, values, mixed, d_attended):
    heads, tokens, _ = queries.shape
    block = min(512, tokens)
    part = pl.BlockSpec((2, block, LANES), lambda p, i: (p, i, 0))
    whole = pl.BlockSpec((2, tokens, LANES), lambda p, i: (p, 0, 0))
    pair_part = pl.BlockSpec((block, LANES), lambda p, i: (i, p))
    pair_whole = pl.BlockSpec((tokens, LANES), lambda p, i: (0, p))
    return pl.pallas_call(
        functools.partial(attend_back_kernel, block),
        grid=(heads // 2, tokens // block),
        in_specs=[part, whole, whole, part, pair_part],
        out_specs=[pair_part, pair_whole, pair_whole],
        out_shape=[jax.ShapeDtypeStruct((tokens, heads * HD), f32)] * 3,
        scratch_shapes=[pltpu.VMEM((2, tokens, LANES), f32)] * 2,
        cost_estimate=pl.CostEstimate(
            flops=heads * tokens * tokens * LANES * 10,
            bytes_accessed=heads * tokens * LANES * 20,
            transcendentals=heads * tokens * tokens // 2,
        ),
        name="attend_back",
    )(queries, keys, values, mixed, d_attended)


def project_back_kernel(
    narrow, dq_ref, dk_ref, dv_ref, qr_ref, kr_ref, gain_ref, cos_ref, sin_ref, out_ref, gg_ref
):
    rows = dq_ref.shape[0]
    lane = lax.broadcasted_iota(jnp.int32, (rows, LANES), 1)
    cosine, sine = cos_ref[...], sin_ref[...]

    @pl.when(pl.program_id(0) == 0)
    def _():
        gg_ref[...] = jnp.zeros_like(gg_ref)

    for which in range(2):
        d_ref, rot_ref = ((dq_ref, qr_ref), (dk_ref, kr_ref))[which]
        turned = rot_ref[...]
        inverse = lax.rsqrt(head_sums(turned * turned) + EPSILON)
        unit_rows = turned * inverse
        upstream = d_ref[...]
        gg_ref[...] += jnp.sum(upstream * unit_rows, axis=0, keepdims=True)
        upstream = upstream * gain_ref[...]
        back = inverse * (upstream - unit_rows * head_sums(unit_rows * upstream))
        for pair in range(narrow // LANES):
            here = back[:, pair * LANES : (pair + 1) * LANES]
            here = here * cosine - swap_halves(here, lane) * sine
            out_ref[:, which * narrow + pair * LANES : which * narrow + (pair + 1) * LANES] = here.astype(bf16)
    out_ref[:, 2 * narrow : 3 * narrow] = dv_ref[...].astype(bf16)


def project_back(d_queries, d_keys, d_values, q_turned, k_turned, gain, cosine, sine):
    tokens, narrow = d_queries.shape
    rows = min(512, tokens)
    row_spec = lambda width: pl.BlockSpec((rows, width), lambda i: (i, 0))
    one = pl.BlockSpec((1, narrow), lambda i: (0, 0))
    return pl.pallas_call(
        functools.partial(project_back_kernel, narrow),
        grid=(tokens // rows,),
        in_specs=[row_spec(narrow)] * 5 + [one, row_spec(LANES), row_spec(LANES)],
        out_specs=[row_spec(3 * narrow), one],
        out_shape=[
            jax.ShapeDtypeStruct((tokens, 3 * narrow), bf16),
            jax.ShapeDtypeStruct((1, narrow), f32),
        ],
        cost_estimate=pl.CostEstimate(
            flops=tokens * narrow * 60, bytes_accessed=tokens * narrow * 26, transcendentals=0
        ),
        name="project_back",
    )(d_queries, d_keys, d_values, q_turned, k_turned, gain, cosine, sine)


MESH = pl.DeviceIdType.MESH


class Group:
    def __init__(self, size, steps, tokens):
        self.size, self.steps = size, steps
        self.chips = size // 2
        self.own = tokens // size
        self.rows = self.own // steps
        self.dp, self.me = lax.axis_index("dp"), lax.axis_index("mp")
        self.chip, self.core = self.me // 2, lax.rem(self.me, 2)
        self.partner = self.me + 1 - 2 * self.core

    def other(self, k, core):
        return 2 * lax.rem(self.chip + k, self.chips) + core

    def slot(self, device):
        k = lax.rem(device // 2 - self.chip + self.chips, self.chips)
        return jnp.where(k == 0, 0, 2 * k - 1 + (lax.rem(device, 2) != self.core).astype(jnp.int32))

    def piece(self, ref, index, step):
        return ref.at[index, pl.ds(pl.multiple_of(step * self.rows, self.rows), self.rows), :]

    def copy(self, source, target, send, receive, device):
        return pltpu.make_async_remote_copy(
            src_ref=source,
            dst_ref=target,
            send_sem=send,
            recv_sem=receive,
            device_id=(self.dp, device),
            device_id_type=MESH,
        )

    def meet(self, everyone=False):
        barrier = pltpu.get_barrier_semaphore()
        devices = [self.partner] + [self.other(k, self.core) for k in range(1, self.chips)]
        if everyone:
            devices = [lax.rem(self.me + j, self.size) for j in range(1, self.size)]
        for device in devices:
            pl.semaphore_signal(barrier, inc=1, device_id=(self.dp, device), device_id_type=MESH)
        pl.semaphore_wait(barrier, len(devices))

    def place(self, i, remote_first=False):
        size, steps = self.size, self.steps
        others = steps * (size - 1)
        if remote_first:
            is_own = i >= others
            j = jnp.where(is_own, 0, i)
            s = jnp.where(is_own, i - others, j // (size - 1))
            r = lax.rem(lax.rem(j, size - 1) + 1, size - 1)
        else:
            is_own = i < steps
            j = jnp.where(is_own, 0, i - steps)
            s = jnp.where(is_own, i, j // (size - 1))
            r = lax.rem(j, size - 1)
        other = jnp.logical_not(is_own)
        is_partner = jnp.logical_and(other, r == 0)
        remote = jnp.logical_and(other, r > 0)
        is_first = jnp.logical_and(remote, lax.rem(r, 2) == 1)
        is_second = jnp.logical_and(remote, lax.rem(r, 2) == 0)
        k = jnp.where(remote, (r + 1) // 2, 0)
        core = jnp.where(jnp.logical_or(is_own, is_first), self.core, 1 - self.core)
        return self.other(k, core), s, k, is_own, is_partner, is_first, is_second

    def run(self, compute, gather=None, settle=None, remote_first=False, after=None, ready=(), between=None):
        steps, chips, size = self.steps, self.chips, self.size

        if gather:
            own_ref, all_ref, g_send, g_recv = gather

            def own_piece(s):
                return own_ref.at[pl.ds(pl.multiple_of(s * self.rows, self.rows), self.rows), :]

            def start_own(s, carry):
                for k in range(1, chips):
                    self.copy(own_piece(s), self.piece(all_ref, self.me, s), g_send.at[k, s], g_recv.at[self.me, s], self.other(k, self.core)).start()
                self.copy(own_piece(s), self.piece(all_ref, self.me, s), g_send.at[0, s], g_recv.at[self.me, s], self.partner).start()
                return carry

            lax.fori_loop(0, steps, start_own, 0)
            all_ref[self.me] = own_ref[...]

            def got(device, s):
                here = self.piece(all_ref, device, s)
                self.copy(here, here, g_send.at[0, s], g_recv.at[device, s], self.partner).wait_recv()

            def forward(k, s):
                device = self.other(k, self.core)
                here = self.piece(all_ref, device, s)
                return self.copy(here, here, g_send.at[chips + k - 1, s], g_recv.at[device, s], self.partner)

        if settle:
            out_ref, mine, kept, to_partner, from_partner, to_chip, from_chip, p_send, p_recv, x_send, x_recv = settle

            def to_partner_copy(k, s):
                return self.copy(self.piece(to_partner, k, s), self.piece(from_partner, k, s), p_send.at[k, s], p_recv.at[k, s], self.partner)

            def to_chip_copy(k, s):
                return self.copy(self.piece(to_chip, k - 1, s), self.piece(from_chip, k - 1, s), x_send.at[k - 1, s], x_recv.at[k - 1, s], self.other(k, self.core))

        for copy in ready:
            copy.wait()

        def item(i, carry):
            device, s, k, is_own, is_partner, is_first, is_second = self.place(i, remote_first)
            if gather:

                @pl.when(jnp.logical_not(is_own))
                def _():
                    got(device, s)

                @pl.when(is_first)
                def _():
                    forward(k, s).start()

            term = compute(device, s, i)
            if between:
                between(device, jnp.logical_or(i == steps - 1, jnp.logical_and(is_partner, s == steps - 1)))
            if settle:
                here = pl.ds(pl.multiple_of(s * self.rows, self.rows), self.rows)

                @pl.when(is_own)
                def _():
                    mine[here, :] = term

                @pl.when(is_first)
                def _():
                    kept[...] = term

                @pl.when(jnp.logical_or(is_partner, is_second))
                def _():
                    to_partner[k, here, :] = term.astype(bf16)
                    to_partner_copy(k, s).start()

                @pl.when(is_second)
                def _():
                    to_partner_copy(k, s).wait_recv()
                    to_chip[k - 1, here, :] = (kept[...] + from_partner[k, here, :].astype(f32)).astype(bf16)
                    to_chip_copy(k, s).start()

            return carry

        lax.fori_loop(0, size * steps, item, 0)

        def end(s, carry):
            if settle:
                here = pl.ds(pl.multiple_of(s * self.rows, self.rows), self.rows)
                to_partner_copy(0, s).wait_recv()
                total = mine[here, :] + from_partner[0, here, :].astype(f32)
                for k in range(1, chips):
                    to_chip_copy(k, s).wait_recv()
                    total = total + from_chip[k - 1, here, :].astype(f32)
                out_ref[here, :] = total
                if after:
                    after(s)
                for k in range(chips):
                    to_partner_copy(k, s).wait_send()
                for k in range(1, chips):
                    to_chip_copy(k, s).wait_send()
            if gather:
                for k in range(2 * chips - 1):
                    self.copy(own_piece(s), own_piece(s), g_send.at[k, s], g_recv.at[0, s], self.partner).wait_send()
            return carry

        self.end = lambda first=0, last=steps: lax.fori_loop(first, last, end, 0)


def settle_scratch(size, steps, tokens):
    own, chips = tokens // size, size // 2
    return [
        pltpu.VMEM((own, D), f32),
        pltpu.VMEM((own // steps, D), f32),
        pltpu.VMEM((chips, own, D), bf16),
        pltpu.VMEM((chips, own, D), bf16),
        pltpu.VMEM((chips - 1, own, D), bf16),
        pltpu.VMEM((chips - 1, own, D), bf16),
        pltpu.SemaphoreType.DMA((chips, steps)),
        pltpu.SemaphoreType.DMA((chips, steps)),
        pltpu.SemaphoreType.DMA((chips - 1, steps)),
        pltpu.SemaphoreType.DMA((chips - 1, steps)),
    ]


def gather_sems(size, steps):
    return [pltpu.SemaphoreType.DMA((size - 1, steps)), pltpu.SemaphoreType.DMA((size, steps))]


VMEM_WHOLE = pl.BlockSpec(memory_space=pltpu.VMEM)
ANYWHERE = pl.BlockSpec(memory_space=pl.ANY)
GRANT = 63 << 20


def weight_scratch(rows, count=1):
    return [pltpu.VMEM((rows, D), bf16)] * count + [pltpu.SemaphoreType.DMA((count,))]


def weight_copies(weights, buffers, sem, first):
    copies = []
    for i, buffer in enumerate(buffers):
        copies.append(pltpu.make_async_copy(weights.at[pl.ds(first, buffer.shape[0]), :], buffer, sem.at[i]))
        first += buffer.shape[0]
    return copies


def remote_params(collective_id):
    return pltpu.CompilerParams(
        collective_id=collective_id, has_side_effects=True, vmem_limit_bytes=GRANT
    )


def attention_sum_kernel(
    size, steps, first_row, rows_ref, w_hbm, start_ref, rates_ref,
    out_ref, middle_ref, low_ref, w_ref, w_sem, *scratch
):
    tokens = rows_ref.shape[0]
    group = Group(size, steps, tokens)
    (copy,) = weight_copies(w_hbm, [w_ref], w_sem, first_row)
    copy.start()
    group.meet()
    copy.wait()

    def compute(device, s, i):
        first = pl.multiple_of(device * group.own + s * group.rows, group.rows)
        return nn(rows_ref[pl.ds(first, group.rows), :], w_ref[...])

    def after(s):
        here = pl.ds(pl.multiple_of(s * group.rows, group.rows), group.rows)
        middle = blend_branch(start_ref[here, :], out_ref[here, :], rates_ref[1:2, :])[2]
        middle_ref[here, :] = middle
        low_ref[here, :] = middle.astype(bf16)

    group.run(compute, settle=(out_ref, *scratch), remote_first=True, after=after)
    group.end()


def attention_sum(rows, weights, start_unit, rates, first_row, size, steps, collective_id):
    tokens, depth = rows.shape
    own = jax.ShapeDtypeStruct((tokens // size, D), f32)
    return pl.pallas_call(
        functools.partial(attention_sum_kernel, size, steps, first_row),
        out_shape=[own, own, jax.ShapeDtypeStruct(own.shape, bf16)],
        in_specs=[VMEM_WHOLE, ANYWHERE, VMEM_WHOLE, VMEM_WHOLE],
        out_specs=[VMEM_WHOLE] * 3,
        scratch_shapes=weight_scratch(depth) + settle_scratch(size, steps, tokens),
        compiler_params=remote_params(collective_id),
        cost_estimate=pl.CostEstimate(flops=2 * tokens * depth * D, bytes_accessed=tokens * D * 8, transcendentals=0),
        name="attention_sum",
    )(rows, weights, start_unit, rates)


def mlp_kernel(
    size, steps, own_ref, w_hbm, scale_ref, middle_ref, cot_ref, rates_ref,
    out_ref, rows_ref, ur_hbm, gr_hbm, d_mlp_ref, d_middle_ref, g_rate_ref, branch_ref,
    up_ref, gate_ref, down_ref, w_sem, u_buf, g_buf, b_sem, *scratch
):
    tokens = own_ref.shape[0] * size
    group = Group(size, steps, tokens)
    copies = weight_copies(w_hbm, [up_ref, gate_ref, down_ref], w_sem, scale_ref.shape[1])
    for c in copies:
        c.start()
    group.meet()

    def save(i, device, s):
        slot = lax.rem(i, 2)
        rows = pl.ds(pl.multiple_of(device * group.own + s * group.rows, group.rows), group.rows)
        return (
            pltpu.make_async_copy(u_buf.at[slot], ur_hbm.at[rows, :], b_sem.at[0, slot]),
            pltpu.make_async_copy(g_buf.at[slot], gr_hbm.at[rows, :], b_sem.at[1, slot]),
        )

    def compute(device, s, i):
        slot = lax.rem(i, 2)

        @pl.when(i >= 2)
        def _():
            for c in save(i, device, s):
                c.wait()

        rows = group.piece(rows_ref, device, s)[...]
        up_raw = nt(rows, up_ref[...])
        gate_raw = nt(rows, gate_ref[...])
        u_buf[slot] = up_raw
        g_buf[slot] = gate_raw
        for c in save(i, device, s):
            c.start()
        gate_val = scale_ref[1:2, :] * gate_raw
        product = (scale_ref[0:1, :] * up_raw * (gate_val * jax.nn.sigmoid(gate_val))).astype(bf16)
        return nn(product, down_ref[...])

    g_rate_ref[...] = jnp.zeros_like(g_rate_ref)

    def after(s):
        here = pl.ds(pl.multiple_of(s * group.rows, group.rows), group.rows)
        middle, rate = middle_ref[here, :], rates_ref[2:3, :]
        branch_unit, branch_inv, mixed, mixed_inv = blend_branch(middle, branch_ref[here, :], rate)
        out_ref[here, :] = mixed
        upstream = jnp.concatenate([cot_ref[d, here, :] for d in range(size)], axis=1).astype(f32)
        d_middle, d_branch, g_rate = blend_back(
            middle, branch_unit, branch_inv, mixed, mixed_inv, rate, upstream
        )
        d_middle_ref[here, :] = d_middle
        d_mlp_ref[here, :] = d_branch.astype(bf16)
        g_rate_ref[...] += g_rate[None]

    group.run(
        compute, gather=(own_ref, rows_ref, scratch[0], scratch[1]), settle=(branch_ref, *scratch[2:]), ready=copies, after=after
    )
    for i in range(2):
        for c in save(i, 0, 0):
            c.wait()
    group.end()


def mlp(own, weights, scales, middle, cot_all, rates, size, steps, collective_id):
    hidden = scales.shape[1]
    tokens = own.shape[0] * size
    rows = own.shape[0] // steps
    return pl.pallas_call(
        functools.partial(mlp_kernel, size, steps),
        out_shape=[
            jax.ShapeDtypeStruct((own.shape[0], D), f32),
            jax.ShapeDtypeStruct((size, own.shape[0], D), bf16),
            jax.ShapeDtypeStruct((tokens, hidden), f32),
            jax.ShapeDtypeStruct((tokens, hidden), f32),
            jax.ShapeDtypeStruct((own.shape[0], D), bf16),
            jax.ShapeDtypeStruct((own.shape[0], D), f32),
            jax.ShapeDtypeStruct((1, D), f32),
        ],
        in_specs=[VMEM_WHOLE, ANYWHERE] + [VMEM_WHOLE] * 4,
        out_specs=[VMEM_WHOLE, VMEM_WHOLE, ANYWHERE, ANYWHERE] + [VMEM_WHOLE] * 3,
        scratch_shapes=[pltpu.VMEM((own.shape[0], D), f32)]
        + weight_scratch(hidden, 3)
        + [
            pltpu.VMEM((2, rows, hidden), f32),
            pltpu.VMEM((2, rows, hidden), f32),
            pltpu.SemaphoreType.DMA((2, 2)),
        ]
        + gather_sems(size, steps)
        + settle_scratch(size, steps, tokens),
        compiler_params=remote_params(collective_id),
        cost_estimate=pl.CostEstimate(flops=6 * tokens * hidden * D, bytes_accessed=tokens * D * 12, transcendentals=tokens * hidden),
        name="mlp",
    )(own, weights, scales, middle, cot_all, rates)


def mlp_back_kernel(
    size, steps, own_ref, w_hbm, scale_ref, ur_hbm, gr_hbm, middle_rows_ref, d_middle_hbm, start_hbm, branch_hbm, rates_ref,
    d_attn_ref, d_start_ref, g_rate_ref, gs_ref, wide_hbm, down_hbm,
    stage, stage_sem, late, late_sem,
    sum_ref, rows_ref, product_ref, d_ref, grads_sum,
    up_ref, gate_ref, down_ref, w_sem, u_buf, g_buf, b_sem, *scratch
):
    tokens = own_ref.shape[0] * size
    group = Group(size, steps, tokens)

    def load(i):
        device, s = group.place(i)[:2]
        slot = lax.rem(i, 2)
        rows = pl.ds(pl.multiple_of(device * group.own + s * group.rows, group.rows), group.rows)
        return (
            pltpu.make_async_copy(ur_hbm.at[rows, :], u_buf.at[slot], b_sem.at[0, slot]),
            pltpu.make_async_copy(gr_hbm.at[rows, :], g_buf.at[slot], b_sem.at[1, slot]),
        )

    copies = weight_copies(w_hbm, [up_ref, gate_ref, down_ref], w_sem, scale_ref.shape[1])
    for c in (*load(0), *copies):
        c.start()
    gs_ref[...] = jnp.zeros_like(gs_ref)
    g_rate_ref[...] = jnp.zeros_like(g_rate_ref)
    group.meet()
    hidden = scale_ref.shape[1]
    part = min(256, hidden)

    def weight_grads(device):
        rows = pl.ds(pl.multiple_of(group.slot(device) * group.own, group.own), group.own)

        def one(source, offset, other):
            def column(c, carry):
                first = pl.multiple_of(c * part, part)
                to = pl.ds(pl.multiple_of(offset + first, part), part)
                term = tn(source[rows, pl.ds(first, part)], other[device])
                grads_sum[to, :] += term
                return carry

            lax.fori_loop(0, source.shape[1] // part, column, 0)

        one(d_ref, 0, middle_rows_ref)
        one(product_ref, 2 * hidden, rows_ref)

    def clear(c, carry):
        grads_sum[pl.ds(pl.multiple_of(c * part, part), part), :] = jnp.zeros((part, D), f32)
        return carry

    lax.fori_loop(0, 3 * hidden // part, clear, 0)

    def between(device, done):
        @pl.when(done)
        def _():
            weight_grads(device)

    def late_copies(s):
        here = pl.ds(pl.multiple_of(s * group.rows, group.rows), group.rows)
        return [
            pltpu.make_async_copy(ref.at[here, :], late.at[lax.rem(s, 2), i], late_sem.at[lax.rem(s, 2), i])
            for i, ref in enumerate((start_hbm, branch_hbm, d_middle_hbm))
        ]

    for c in late_copies(0):
        c.start()

    def after(s):
        here = pl.ds(pl.multiple_of(s * group.rows, group.rows), group.rows)
        for c in late_copies(s):
            c.wait()

        @pl.when(s + 1 < steps)
        def _():
            for c in late_copies(s + 1):
                c.start()

        start, branch, d_middle = [late[lax.rem(s, 2), i] for i in range(3)]
        rate = rates_ref[1:2, :]
        branch_unit, branch_inv, middle, middle_inv = blend_branch(start, branch, rate)
        d_start, d_branch, g_rate = blend_back(
            start, branch_unit, branch_inv, middle, middle_inv, rate, d_middle + sum_ref[here, :]
        )
        d_start_ref[here, :] = d_start
        d_attn_ref[here, :] = d_branch.astype(bf16)
        g_rate_ref[...] += g_rate[None]

    def compute(device, s, i):
        slot = lax.rem(i, 2)

        @pl.when(i + 1 < size * steps)
        def _():
            for c in load(i + 1):
                c.start()

        rows = group.piece(rows_ref, device, s)[...]
        d_product = nt(rows, down_ref[...])
        for c in load(i):
            c.wait()
        first = pl.multiple_of(group.slot(device) * group.own + s * group.rows, group.rows)
        here = pl.ds(first, group.rows)
        up_raw, gate_raw = u_buf[slot], g_buf[slot]
        up_val = scale_ref[0:1, :] * up_raw
        gate_val = scale_ref[1:2, :] * gate_raw
        sigmoid = jax.nn.sigmoid(gate_val)
        activated = gate_val * sigmoid
        product_ref[here, :] = (up_val * activated).astype(bf16)
        d_up = d_product * activated
        d_gate = d_product * up_val * (sigmoid * (1.0 + gate_val * (1.0 - sigmoid)))
        gs_ref[0:1, :] += jnp.sum(d_up * up_raw, axis=0, keepdims=True)
        gs_ref[1:2, :] += jnp.sum(d_gate * gate_raw, axis=0, keepdims=True)
        d_up_raw = (d_up * scale_ref[0:1, :]).astype(bf16)
        d_gate_raw = (d_gate * scale_ref[1:2, :]).astype(bf16)
        d_ref[here, :hidden] = d_up_raw
        d_ref[here, hidden:] = d_gate_raw
        return nn(d_up_raw, up_ref[...]) + nn(d_gate_raw, gate_ref[...])

    group.run(
        compute, gather=(own_ref, rows_ref, scratch[0], scratch[1]), settle=(sum_ref, *scratch[2:]), ready=copies,
        after=after, between=between,
    )

    def rest(j, carry):
        weight_grads(group.other(1 + j // 2, lax.rem(j, 2)))
        return carry

    lax.fori_loop(0, size - 2, rest, 0)

    wide_parts = 2 * hidden // part

    def stage_copy(c, ref, first):
        here = pl.ds(pl.multiple_of((c - first) * part, part), part)
        return pltpu.make_async_copy(stage.at[lax.rem(c, 2)], ref.at[here, :], stage_sem.at[lax.rem(c, 2)])

    def put(c, carry):
        @pl.when(c >= 2)
        def _():
            stage_copy(lax.rem(c, 2), wide_hbm, 0).wait()

        stage[lax.rem(c, 2)] = grads_sum[pl.ds(pl.multiple_of(c * part, part), part), :].astype(bf16)

        @pl.when(c < wide_parts)
        def _():
            stage_copy(c, wide_hbm, 0).start()

        @pl.when(c >= wide_parts)
        def _():
            stage_copy(c, down_hbm, wide_parts).start()

        return carry

    parts = 3 * hidden // part
    lax.fori_loop(0, parts, put, 0)
    group.end()
    for c in range(2):
        stage_copy(c, wide_hbm, 0).wait()


def mlp_back(own, weights, scales, up_raw, gate_raw, middle_rows, d_middle, start_unit, branch, rates, size, steps, collective_id):
    tokens, hidden = up_raw.shape
    rows = own.shape[0] // steps
    return pl.pallas_call(
        functools.partial(mlp_back_kernel, size, steps),
        out_shape=[
            jax.ShapeDtypeStruct((own.shape[0], D), bf16),
            jax.ShapeDtypeStruct((own.shape[0], D), f32),
            jax.ShapeDtypeStruct((1, D), f32),
            jax.ShapeDtypeStruct((2, hidden), f32),
            jax.ShapeDtypeStruct((2 * hidden, D), bf16),
            jax.ShapeDtypeStruct((hidden, D), bf16),
        ],
        in_specs=[VMEM_WHOLE, ANYWHERE, VMEM_WHOLE, ANYWHERE, ANYWHERE, VMEM_WHOLE] + [ANYWHERE] * 3 + [VMEM_WHOLE],
        out_specs=[VMEM_WHOLE] * 4 + [ANYWHERE] * 2,
        scratch_shapes=[
            pltpu.VMEM((2, min(256, hidden), D), bf16),
            pltpu.SemaphoreType.DMA((2,)),
            pltpu.VMEM((2, 3, rows, D), f32),
            pltpu.SemaphoreType.DMA((2, 3)),
            pltpu.VMEM((own.shape[0], D), f32),
            pltpu.VMEM((size, own.shape[0], D), bf16),
            pltpu.VMEM((tokens - own.shape[0], hidden), bf16),
            pltpu.VMEM((tokens - own.shape[0], 2 * hidden), bf16),
            pltpu.VMEM((3 * hidden, D), f32),
        ]
        + weight_scratch(hidden, 3)
        + [
            pltpu.VMEM((2, rows, hidden), f32),
            pltpu.VMEM((2, rows, hidden), f32),
            pltpu.SemaphoreType.DMA((2, 2)),
        ]
        + gather_sems(size, steps)
        + settle_scratch(size, steps, tokens),
        compiler_params=remote_params(collective_id),
        cost_estimate=pl.CostEstimate(flops=6 * tokens * hidden * D, bytes_accessed=tokens * D * 24, transcendentals=tokens * hidden),
        name="mlp_back",
    )(own, weights, scales, up_raw, gate_raw, middle_rows, d_middle, start_unit, branch, rates)


def gather_project_kernel(size, steps, first_row, own_ref, w_hbm, out_ref, rows_ref, w_ref, w_sem, *scratch):
    tokens = own_ref.shape[0] * size
    group = Group(size, steps, tokens)
    copies = weight_copies(w_hbm, [w_ref], w_sem, first_row)
    copies[0].start()
    group.meet()

    def compute(device, s, i):
        first = pl.multiple_of(device * group.own + s * group.rows, group.rows)
        out_ref[pl.ds(first, group.rows), :] = nt(group.piece(rows_ref, device, s)[...], w_ref[...]).astype(bf16)

    group.run(compute, gather=(own_ref, rows_ref, scratch[0], scratch[1]), ready=copies)
    group.end()


def gather_project(own, weights, width, first_row, size, steps, collective_id, name):
    tokens = own.shape[0] * size
    return pl.pallas_call(
        functools.partial(gather_project_kernel, size, steps, first_row),
        out_shape=[
            jax.ShapeDtypeStruct((tokens, width), bf16),
            jax.ShapeDtypeStruct((size, own.shape[0], D), bf16),
        ],
        in_specs=[VMEM_WHOLE, ANYWHERE],
        out_specs=[VMEM_WHOLE, VMEM_WHOLE],
        scratch_shapes=weight_scratch(width) + gather_sems(size, steps),
        compiler_params=remote_params(collective_id),
        cost_estimate=pl.CostEstimate(flops=2 * tokens * width * D, bytes_accessed=tokens * D * 4, transcendentals=0),
        name=name,
    )(own, weights)


def start_sum_kernel(
    size, steps, rows_ref, w_hbm, base_ref, unit_ref, inv_ref, operand_hbm, attended_hbm, d_attn_hbm,
    out_ref, grads_ref, operand_ref, attended_ref, d_attn_ref, late_sem, w_ref, w_sem, total_ref, pieces, d_send, d_recv, *scratch
):
    tokens = rows_ref.shape[0]
    narrow = out_ref.shape[2]
    group = Group(size, steps, tokens)
    copies = weight_copies(w_hbm, [w_ref], w_sem, 0)
    copies[0].start()
    late = [
        pltpu.make_async_copy(source, target, late_sem.at[i])
        for i, (source, target) in enumerate(
            ((operand_hbm, operand_ref), (attended_hbm, attended_ref), (d_attn_hbm, d_attn_ref))
        )
    ]
    for copy in late:
        copy.start()
    group.meet(everyone=True)
    copies[0].wait()

    def compute(device, s, i):
        first = pl.multiple_of(device * group.own + s * group.rows, group.rows)
        return nn(rows_ref[pl.ds(first, group.rows), :], w_ref[...])

    def deal(j, s):
        device = lax.rem(group.me + j, size)
        return group.copy(
            group.piece(pieces, device, s), group.piece(out_ref, group.me, s), d_send.at[j - 1, s], d_recv.at[group.me, s], device
        )

    def after(s):
        here = pl.ds(pl.multiple_of(s * group.rows, group.rows), group.rows)
        back = normalize_back(unit_ref[here, :], inv_ref[here, :], base_ref[here, :] + total_ref[here, :])
        for device in range(size):
            pieces[device, here, :] = back[:, device * narrow : (device + 1) * narrow].astype(bf16)
        out_ref[group.me, here, :] = pieces[group.me, here, :]
        for j in range(1, size):
            deal(j, s).start()

    group.run(compute, settle=(total_ref, *scratch), remote_first=True, after=after)

    for copy in late:
        copy.wait()
    for c in range(3):
        here = slice(c * narrow, (c + 1) * narrow)
        grads_ref[here, :] = tn(rows_ref[:, here], operand_ref[...]).astype(bf16)
        group.end(c * steps // 4, (c + 1) * steps // 4)
    out_sum = jnp.zeros((narrow, D), f32)
    for d in range(size):
        out_sum += tn(attended_ref[d * group.own : (d + 1) * group.own, :], d_attn_ref[d])
    grads_ref[3 * narrow :, :] = out_sum.astype(bf16)
    group.end(3 * steps // 4, steps)

    def finish(s, carry):
        for j in range(1, size):
            device = lax.rem(group.me + j, size)
            here = group.piece(out_ref, device, s)
            group.copy(here, here, d_send.at[j - 1, s], d_recv.at[device, s], group.partner).wait_recv()
            deal(j, s).wait_send()
        return carry

    lax.fori_loop(0, steps, finish, 0)


def start_sum(rows, weights, base, unit_rows, inverse, operand, attended, d_attn_rows, size, steps, collective_id):
    tokens, depth = rows.shape
    own, narrow = tokens // size, D // size
    return pl.pallas_call(
        functools.partial(start_sum_kernel, size, steps),
        out_shape=[jax.ShapeDtypeStruct((size, own, narrow), bf16), jax.ShapeDtypeStruct((4 * narrow, D), bf16)],
        in_specs=[VMEM_WHOLE, ANYWHERE] + [VMEM_WHOLE] * 3 + [ANYWHERE] * 3,
        out_specs=[VMEM_WHOLE] * 2,
        scratch_shapes=[
            pltpu.VMEM(operand.shape, bf16),
            pltpu.VMEM(attended.shape, bf16),
            pltpu.VMEM(d_attn_rows.shape, bf16),
            pltpu.SemaphoreType.DMA((3,)),
        ]
        + weight_scratch(depth)
        + [
            pltpu.VMEM((own, D), f32),
            pltpu.VMEM((size, own, narrow), bf16),
            pltpu.SemaphoreType.DMA((size - 1, steps)),
            pltpu.SemaphoreType.DMA((size, steps)),
        ]
        + settle_scratch(size, steps, tokens),
        compiler_params=remote_params(collective_id),
        cost_estimate=pl.CostEstimate(flops=2 * tokens * depth * D, bytes_accessed=tokens * D * 8, transcendentals=0),
        name="start_sum",
    )(rows, weights, base, unit_rows, inverse, operand, attended, d_attn_rows)


def tail_plan(devices, rows):
    lines = min(4, devices)
    columns = devices // lines
    cuts = 2 if rows % (devices * 32) == 0 else 1
    return lines, columns, cuts, rows // (devices * cuts)


def tail_sum_kernel(
    devices, size, late_ref, early_ref, rates_ref, small_ref, late_out, early_out, small_out,
    y_land, y_sum, z_land, rate_parts, rate_land, pack, small_land,
    a_send, a_recv, b_send, b_recv, c_send, c_recv, d_send, d_recv, m_send, m_recv, s_send, s_recv
):
    dp, me = lax.axis_index("dp"), lax.axis_index("mp")
    lines, columns, cuts, rows = tail_plan(devices, late_ref.shape[0])
    a, b = dp // columns, lax.rem(dp, columns)
    span = lines * rows
    narrow = rate_parts.shape[2]
    chunks = [(early_ref, early_out, q) for q in range(cuts)] + [(late_ref, late_out, q) for q in range(cuts)]

    def remote(source, target, send, receive, device):
        return pltpu.make_async_remote_copy(
            src_ref=source, dst_ref=target, send_sem=send, recv_sem=receive, device_id=device, device_id_type=MESH
        )

    def peer(j):
        return lax.rem(dp + j, devices)

    def column(j):
        return lax.rem(b + j, columns)

    def line(j):
        return lax.rem(a + j, lines)

    barrier = pltpu.get_barrier_semaphore()

    def greet(j, carry):
        pl.semaphore_signal(barrier, inc=1, device_id=(peer(j), me), device_id_type=MESH)
        return carry

    lax.fori_loop(1, devices, greet, 0)
    for j in range(1, size):
        pl.semaphore_signal(barrier, inc=1, device_id=(dp, lax.rem(me + j, size)), device_id_type=MESH)
    pl.semaphore_wait(barrier, devices - 1 + size - 1)

    def part(ref, q, col):
        return ref.at[pl.ds(pl.multiple_of((q * columns + col) * span, span), span), :]

    def to_column(c, j):
        ref, _, q = chunks[c]
        return remote(part(ref, q, column(j)), y_land.at[c, b], a_send.at[c, j], a_recv.at[c, b], (a * columns + column(j), me))

    def from_column(c, j):
        here = y_land.at[c, column(j)]
        return remote(here, here, a_send.at[c, j], a_recv.at[c, column(j)], (a * columns + column(j), me))

    def to_line(c, j):
        there = pl.ds(pl.multiple_of(line(j) * rows, rows), rows)
        return remote(y_sum.at[c, there, :], z_land.at[c, a], b_send.at[c, j], b_recv.at[c, a], (line(j) * columns + b, me))

    def from_line(c, j):
        here = z_land.at[c, line(j)]
        return remote(here, here, b_send.at[c, j], b_recv.at[c, line(j)], (line(j) * columns + b, me))

    def sum_of(c, col, row):
        _, out, q = chunks[c]
        return out.at[(q * columns + col) * lines + row]

    def back_line(c, j):
        here = sum_of(c, b, a)
        return remote(here, here, c_send.at[c, j], c_recv.at[c, a], (line(j) * columns + b, me))

    def back_line_got(c, j):
        here = sum_of(c, b, line(j))
        return remote(here, here, c_send.at[c, j], c_recv.at[c, line(j)], (line(j) * columns + b, me))

    def back_column(c, i, j):
        here = sum_of(c, b, line(i))
        return remote(here, here, d_send.at[c, i, j], d_recv.at[c, line(i), b], (a * columns + column(j), me))

    def back_column_got(c, i, j):
        here = sum_of(c, column(j), line(i))
        return remote(here, here, d_send.at[c, i, j], d_recv.at[c, line(i), column(j)], (a * columns + column(j), me))

    def rate_copy(j):
        device = lax.rem(me + j, size)
        return remote(rate_parts.at[device], rate_land.at[me], m_send.at[j - 1], m_recv.at[me], (dp, device))

    for c in range(len(chunks)):
        for j in range(1, columns):
            to_column(c, j).start()
    for d in range(size):
        rate_parts[d, 0:2, :] = rates_ref[:, d * narrow : (d + 1) * narrow]
    for j in range(1, size):
        rate_copy(j).start()

    rates = rate_parts[me]
    for j in range(1, size):
        source = lax.rem(me + j, size)
        remote(rate_land.at[source], rate_land.at[source], m_send.at[j - 1], m_recv.at[source], (dp, source)).wait_recv()
        rates = rates + rate_land[source]
    pack[...] = small_ref[...]
    pack[3:5, :narrow] = rates[0:2, :]

    def small_copy(j):
        return remote(pack, small_land.at[dp], s_send.at[j - 1], s_recv.at[dp], (peer(j), me))

    def small_give(j, carry):
        small_copy(j).start()
        return carry

    lax.fori_loop(1, devices, small_give, 0)

    def settle_column(c):
        ref, _, q = chunks[c]
        for j in range(1, columns):
            from_column(c, j).wait_recv()

        def add(i, carry):
            here = pl.ds(pl.multiple_of(i * rows, rows), rows)
            own = pl.ds(pl.multiple_of((q * columns + b) * span + i * rows, rows), rows)
            total = ref[own, :].astype(f32)
            for j in range(1, columns):
                total = total + y_land[c, column(j), here, :].astype(f32)
            y_sum[c, here, :] = total.astype(bf16)
            return carry

        lax.fori_loop(0, lines, add, 0)
        for j in range(1, lines):
            to_line(c, j).start()

    def settle_line(c):
        for j in range(1, lines):
            from_line(c, j).wait_recv()
        total = y_sum[c, pl.ds(pl.multiple_of(a * rows, rows), rows), :].astype(f32)
        for j in range(1, lines):
            total = total + z_land[c, line(j)].astype(f32)
        sum_of(c, b, a)[...] = total.astype(bf16)
        for j in range(1, lines):
            back_line(c, j).start()
        for j in range(1, columns):
            back_column(c, 0, j).start()

    def pass_on(c):
        for i in range(1, lines):
            back_line_got(c, i).wait_recv()
            for j in range(1, columns):
                back_column(c, i, j).start()

    count = len(chunks)
    for step in range(count + 2):
        if step < count:
            settle_column(step)
        if 1 <= step <= count:
            settle_line(step - 1)
        if step >= 2:
            pass_on(step - 2)

    def small_take(j, total):
        source = peer(j)
        remote(small_land.at[source], small_land.at[source], s_send.at[j - 1], s_recv.at[source], (source, me)).wait_recv()
        return total + small_land[source]

    small_out[...] = lax.fori_loop(1, devices, small_take, pack[...])
    for c in range(count):
        for i in range(lines):
            for j in range(1, columns):
                back_column_got(c, i, j).wait_recv()
                back_column(c, i, j).wait_send()
        for j in range(1, lines):
            back_line(c, j).wait_send()
            to_line(c, j).wait_send()
        for j in range(1, columns):
            to_column(c, j).wait_send()

    def finish(j, carry):
        small_copy(j).wait_send()
        return carry

    lax.fori_loop(1, devices, finish, 0)
    for j in range(1, size):
        rate_copy(j).wait_send()


def tail_sum(late, early, rates, small, devices, size, collective_id):
    lines, columns, cuts, rows = tail_plan(devices, late.shape[0])
    narrow = D // size
    chunks = 2 * cuts
    dma = pltpu.SemaphoreType.DMA
    total = jax.ShapeDtypeStruct((late.shape[0] // rows, rows, D), bf16)
    return pl.pallas_call(
        functools.partial(tail_sum_kernel, devices, size),
        out_shape=[total, total, jax.ShapeDtypeStruct(small.shape, f32)],
        in_specs=[VMEM_WHOLE] * 4,
        out_specs=[VMEM_WHOLE] * 3,
        scratch_shapes=[
            pltpu.VMEM((chunks, columns, lines * rows, D), bf16),
            pltpu.VMEM((chunks, lines * rows, D), bf16),
            pltpu.VMEM((chunks, lines, rows, D), bf16),
            pltpu.VMEM((size, 8, narrow), f32),
            pltpu.VMEM((size, 8, narrow), f32),
            pltpu.VMEM(small.shape, f32),
            pltpu.VMEM((devices, *small.shape), f32),
            dma((chunks, columns)), dma((chunks, columns)),
            dma((chunks, lines)), dma((chunks, lines)),
            dma((chunks, lines)), dma((chunks, lines)),
            dma((chunks, lines, columns)), dma((chunks, lines, columns)),
            dma((size - 1,)), dma((size,)),
            dma((devices - 1,)), dma((devices,)),
        ],
        compiler_params=remote_params(collective_id),
        cost_estimate=pl.CostEstimate(flops=0, bytes_accessed=late.shape[0] * D * 16, transcendentals=0),
        name="tail_sum",
    )(late, early, rates, small)


def optimizer_kernel(
    counts, index_ref, attn_ref, wide_ref, down_ref, m_ref, f_ref, s_ref, mo_ref, fo_ref, so_ref, go_ref
):
    group = m_ref.shape[0]
    for j in range(group):
        slot = pl.program_id(0) * group + j
        block, live = index_ref[slot, 0], index_ref[slot, 1]

        @pl.when(live == 0)
        def _():
            for ref in (mo_ref, fo_ref, so_ref, go_ref):
                ref[j] = jnp.zeros_like(m_ref[j])

        for ref, first, last in (
            (attn_ref, 0, counts[0]),
            (wide_ref, counts[0], counts[0] + counts[1]),
            (down_ref, counts[0] + counts[1], sum(counts)),
        ):

            @pl.when(jnp.logical_and(live == 1, jnp.logical_and(block >= first, block < last)))
            def _():
                gradient = ref[block - first].astype(f32)
                stepped, first_new, second_new = adam_update(
                    m_ref[j], gradient, f_ref[j], s_ref[j], WEIGHT_DECAY, LEARN_RATE
                )
                go_ref[j] = gradient
                fo_ref[j] = first_new
                so_ref[j] = second_new
                mo_ref[j] = stepped * lax.rsqrt(jnp.sum(stepped * stepped, axis=-1, keepdims=True) + EPSILON)


def optimizer(index, attn_grads, wide_grads, down_grads, masters, firsts, seconds):
    slots, height, _ = masters.shape
    group = math.gcd(slots, 4)
    grads = [g.reshape(-1, height, D) for g in (attn_grads, wide_grads, down_grads)]
    block = pl.BlockSpec((group, height, D), lambda i, ref: (i, 0, 0))
    return pl.pallas_call(
        functools.partial(optimizer_kernel, tuple(g.shape[0] for g in grads)),
        grid_spec=pltpu.PrefetchScalarGridSpec(
            num_scalar_prefetch=1,
            grid=(slots // group,),
            in_specs=[pl.BlockSpec(memory_space=pltpu.VMEM)] * 3 + [block] * 3,
            out_specs=[block] * 4,
        ),
        out_shape=[jax.ShapeDtypeStruct(masters.shape, f32)] * 4,
        compiler_params=pltpu.CompilerParams(vmem_limit_bytes=GRANT),
        cost_estimate=pl.CostEstimate(flops=20 * masters.size, bytes_accessed=30 * masters.size, transcendentals=0),
        name="optimizer",
    )(index, *grads, masters, firsts, seconds)


def collect_kernel(count, places_ref, slots_hbm, out_ref, sems):
    def copy(b):
        return pltpu.make_async_copy(slots_hbm.at[places_ref[b]], out_ref.at[b], sems.at[b])

    def start(b, carry):
        copy(b).start()
        return carry

    def wait(b, carry):
        copy(b).wait()
        return carry

    lax.fori_loop(0, count, start, 0)
    lax.fori_loop(0, count, wait, 0)


def collect(places, slots):
    count, shape = places.shape[0], slots.shape[1:]
    return pl.pallas_call(
        functools.partial(collect_kernel, count),
        grid_spec=pltpu.PrefetchScalarGridSpec(
            num_scalar_prefetch=1,
            grid=(1,),
            in_specs=[pl.BlockSpec(memory_space=pl.ANY)],
            out_specs=pl.BlockSpec(memory_space=pltpu.VMEM),
            scratch_shapes=[pltpu.SemaphoreType.DMA((count,))],
        ),
        out_shape=jax.ShapeDtypeStruct((count, *shape), bf16),
        compiler_params=pltpu.CompilerParams(vmem_limit_bytes=GRANT),
        cost_estimate=pl.CostEstimate(flops=0, bytes_accessed=4 * count * math.prod(shape), transcendentals=0),
        name="collect",
    )(places, slots)


def spread_plan(devices, slots):
    lines = min(4, devices)
    columns = devices // lines
    across = slots * 5 // 32 if columns == 2 else 0
    cuts = next(q for q in (9, 3, 2, 1) if (slots - across) % q == 0)
    return lines, columns, across, cuts


def spread_kernel(
    devices, size, slots, height, slots_ref, x_ref, cot_ref, gains_ref,
    all_ref, x_all, cot_all, gains_all, cos_ref, sin_ref, gains_land,
    z_send, z_recv, y_send, y_recv, e_send, e_recv, x_send, x_recv, c_send, c_recv, w_send, w_recv, local_sem
):
    lines, columns, across, cuts = spread_plan(devices, slots)
    dp, me = lax.axis_index("dp"), lax.axis_index("mp")
    a, b = dp // columns, lax.rem(dp, columns)
    chips = size // 2
    chip, core = me // 2, lax.rem(me, 2)
    partner = me + 1 - 2 * core
    tokens, narrow = x_ref.shape
    own = tokens // size
    x_steps = x_recv.shape[1]
    x_rows = tokens // x_steps
    cut_rows = (slots - across) * height // cuts
    has_left, has_right = a > 0, a < lines - 1

    def remote(source, target, send, receive, device):
        return pltpu.make_async_remote_copy(
            src_ref=source, dst_ref=target, send_sem=send, recv_sem=receive, device_id=device, device_id_type=MESH
        )

    def column(j):
        return lax.rem(b + j, columns)

    def other(k, which):
        return 2 * lax.rem(chip + k, chips) + which

    def mp_peer(j):
        return lax.rem(me + j, size)

    barrier = pltpu.get_barrier_semaphore()

    def greet(device):
        pl.semaphore_signal(barrier, inc=1, device_id=device, device_id_type=MESH)

    for j in range(1, columns):
        greet((a * columns + column(j), me))
    for j in range(1, size):
        greet((dp, mp_peer(j)))

    @pl.when(has_left)
    def _():
        greet((dp - columns, me))

    @pl.when(has_right)
    def _():
        greet((dp + columns, me))

    pl.semaphore_wait(
        barrier, columns - 1 + size - 1 + has_left.astype(jnp.int32) + has_right.astype(jnp.int32)
    )

    items = cuts + (columns if across else 0)

    def region(ref, line, c, row=None):
        if c < cuts:
            source, first, count = line * columns + b, across * height + c * cut_rows, cut_rows
        else:
            source, first, count = line * columns + (c - cuts), 0, across * height
        return ref.at[source, pl.ds(first, count), :]

    def own_part(c):
        first, count = (across * height + c * cut_rows, cut_rows) if c < cuts else (0, across * height)
        return slots_ref.at[pl.ds(first, count), :]

    def along(line, c, to_right, source=None):
        here = region(all_ref, line, c)
        side = 1 if to_right else 0
        device = (dp + columns if to_right else dp - columns, me)
        return remote(here if source is None else source, here, z_send.at[line, side, c], z_recv.at[line, c], device)

    def over(line, c, j, source=None):
        here = region(all_ref, line, c)
        return remote(
            here if source is None else source, here, y_send.at[line, j, c], y_recv.at[line, b, c],
            (a * columns + column(j), me),
        )

    def over_got(line, column_from, c):
        first = across * height + c * cut_rows
        here = all_ref.at[line * columns + column_from, pl.ds(first, cut_rows), :]
        return remote(here, here, y_send.at[line, 1, c], y_recv.at[line, column_from, c], (dp, partner))

    def early(j):
        here = all_ref.at[dp, pl.ds(0, across * height), :]
        return remote(own_part(cuts), here, e_send.at[j], e_recv.at[b], (a * columns + column(j), me))

    def early_got(column_from):
        here = all_ref.at[a * columns + column_from, pl.ds(0, across * height), :]
        return remote(here, here, e_send.at[1], e_recv.at[column_from], (dp, partner))

    def x_piece(ref, s):
        return ref.at[pl.ds(s * x_rows, x_rows), :]

    def x_own(s, k):
        device = (dp, partner) if k == 0 else (dp, other(k, core))
        return remote(x_piece(x_ref, s), x_piece(x_all.at[me], s), x_send.at[k, s], x_recv.at[me, s], device)

    def x_forward(s, k):
        source = other(k, core)
        here = x_piece(x_all.at[source], s)
        return remote(here, here, x_send.at[chips + k - 1, s], x_recv.at[source, s], (dp, partner))

    def x_got(s, source):
        here = x_piece(x_all.at[source], s)
        return remote(here, here, x_send.at[0, s], x_recv.at[source, s], (dp, partner))

    def cot_own(j):
        device = mp_peer(j)
        rows = pl.ds(pl.multiple_of(device * own, own), own)
        return remote(cot_ref.at[rows, :], cot_all.at[me], c_send.at[j - 1], c_recv.at[me], (dp, device))

    def cot_got(j):
        here = cot_all.at[mp_peer(j)]
        return remote(here, here, c_send.at[j - 1], c_recv.at[mp_peer(j)], (dp, partner))

    def gains_own(j):
        return remote(gains_ref, gains_land.at[me], w_send.at[j - 1], w_recv.at[me], (dp, mp_peer(j)))

    if across:
        for j in range(1, columns):
            early(j).start()
    for j in range(1, size):
        gains_own(j).start()
    gains_land[me] = gains_ref[...]
    for c in range(cuts):
        for side, there in ((False, has_left), (True, has_right)):

            @pl.when(there)
            def _():
                along(a, c, side, own_part(c)).start()

        for j in range(1, columns):
            over(a, c, j, own_part(c)).start()
    for s in range(x_steps):
        for k in range(chips):
            x_own(s, (k + 1) % chips).start()
    for j in range(1, size):
        cot_own(j).start()
    local = [
        pltpu.make_async_copy(slots_ref, all_ref.at[dp], local_sem.at[0]),
        pltpu.make_async_copy(x_ref, x_all.at[me], local_sem.at[1]),
        pltpu.make_async_copy(
            cot_ref.at[pl.ds(pl.multiple_of(me * own, own), own), :], cot_all.at[me], local_sem.at[2]
        ),
    ]
    for copy in local:
        copy.start()
    if across:
        for j in range(1, columns):
            early_got(column(j)).wait_recv()
        for c in range(cuts, items):
            for side, there in ((False, has_left), (True, has_right)):
                mine = b == c - cuts

                @pl.when(jnp.logical_and(there, mine))
                def _():
                    along(a, c, side, own_part(c)).start()

                @pl.when(jnp.logical_and(there, jnp.logical_not(mine)))
                def _():
                    along(a, c, side).start()

    for s in range(x_steps):
        for k in range(1, chips):
            x_got(s, other(k, core)).wait_recv()
            x_forward(s, k).start()

    rope_rows = min(256, tokens)

    def rope_table(i, carry):
        here = pl.ds(pl.multiple_of(i * rope_rows, rope_rows), rope_rows)
        lane = lax.broadcasted_iota(jnp.int32, (rope_rows, LANES), 1)
        position = (lax.broadcasted_iota(jnp.int32, (rope_rows, LANES), 0) + i * rope_rows).astype(f32)
        j = lane % (HD // 2)
        angle = position * jnp.exp(j.astype(f32) * (-2.0 * math.log(10000.0) / HD))
        cos_ref[here, :] = jnp.cos(angle)
        sin_ref[here, :] = jnp.where(lane % HD < HD // 2, -1.0, 1.0) * jnp.sin(angle)
        return carry

    lax.fori_loop(0, tokens // rope_rows, rope_table, 0)

    for hop in range(1, lines):
        for c in range(items):
            for to_right in (True, False):
                line = a - hop if to_right else a + hop
                there = line >= 0 if to_right else line < lines
                onward = has_right if to_right else has_left

                @pl.when(there)
                def _():
                    along(line, c, to_right).wait_recv()

                    @pl.when(onward)
                    def _():
                        along(line, c, to_right).start()

                    if c < cuts:
                        for j in range(1, columns):
                            over(line, c, j).start()

    for line in range(lines):
        for c in range(cuts):
            for j in range(1, columns):
                over_got(line, column(j), c).wait_recv()
    for s in range(x_steps):
        x_got(s, partner).wait_recv()
        for k in range(1, chips):
            x_got(s, other(k, 1 - core)).wait_recv()
    for j in range(1, size):
        cot_got(j).wait_recv()
        here = gains_land.at[mp_peer(j)]
        remote(here, here, w_send.at[j - 1], w_recv.at[mp_peer(j)], (dp, partner)).wait_recv()
        gains_own(j).wait_send()
    for d in range(size):
        gains_all[:, d * narrow : (d + 1) * narrow] = gains_land[d]
    for copy in local:
        copy.wait()
    if across:
        for j in range(1, columns):
            early(j).wait_send()
    for s in range(x_steps):
        for k in range(chips):
            x_own(s, k).wait_send()
        for k in range(1, chips):
            x_forward(s, k).wait_send()
    for j in range(1, size):
        cot_own(j).wait_send()
    for line in range(lines):
        for c in range(items):
            @pl.when(jnp.logical_and(has_right, line <= a))
            def _():
                along(line, c, True).wait_send()

            @pl.when(jnp.logical_and(has_left, line >= a))
            def _():
                along(line, c, False).wait_send()

            if c < cuts:
                for j in range(1, columns):
                    over(line, c, j).wait_send()


def spread(slots_low, hidden_in, cotangent, gains, devices, size, collective_id):
    slots, height, _ = slots_low.shape
    tokens, narrow = hidden_in.shape
    lines, columns, across, cuts = spread_plan(devices, slots)
    items = cuts + (columns if across else 0)
    chips = size // 2
    x_steps = 4
    dma = pltpu.SemaphoreType.DMA
    return pl.pallas_call(
        functools.partial(spread_kernel, devices, size, slots, height),
        out_shape=[
            jax.ShapeDtypeStruct((devices, slots * height, D), bf16),
            jax.ShapeDtypeStruct((size, tokens, narrow), bf16),
            jax.ShapeDtypeStruct((size, tokens // size, narrow), bf16),
            jax.ShapeDtypeStruct((gains.shape[0], D), f32),
            jax.ShapeDtypeStruct((tokens, LANES), f32),
            jax.ShapeDtypeStruct((tokens, LANES), f32),
        ],
        in_specs=[VMEM_WHOLE] * 4,
        out_specs=[ANYWHERE] * 3 + [VMEM_WHOLE] * 3,
        scratch_shapes=[
            pltpu.VMEM((size, *gains.shape), f32),
            dma((lines, 2, items)),
            dma((lines, items)),
            dma((lines, columns, cuts)),
            dma((lines, columns, cuts)),
            dma((columns,)),
            dma((columns,)),
            dma((2 * chips - 1, x_steps)),
            dma((size, x_steps)),
            dma((size - 1,)),
            dma((size,)),
            dma((size - 1,)),
            dma((size,)),
            dma((3,)),
        ],
        compiler_params=remote_params(collective_id),
        cost_estimate=pl.CostEstimate(flops=0, bytes_accessed=devices * slots * height * D * 4, transcendentals=0),
        name="spread",
    )(slots_low.reshape(slots * height, D), hidden_in, cotangent, gains)


def shards(
    n_dp,
    hidden_in,
    cotangent,
    owners,
    masters,
    firsts,
    seconds,
    width_gains,
    width_first,
    width_second,
    hidden_gains,
    hidden_first,
    hidden_second,
):
    tokens = hidden_in.shape[0]
    narrow = hidden_in.shape[1]
    slot_count = masters.shape[1]
    block_rows = masters.shape[2]
    blocks = owners.shape[0]
    hidden_local = hidden_gains.shape[1]
    dp_index = lax.axis_index("dp")
    mp_index = lax.axis_index("mp")
    own_tokens = tokens // (D // narrow)

    block_order = jnp.arange(blocks)
    same_owner = owners[:, None] == owners[None, :]
    slot_rank = jnp.sum(
        jnp.logical_and(same_owner, block_order[None, :] < block_order[:, None]).astype(jnp.int32),
        axis=1,
    )
    owned_mask = owners == dp_index
    in_use = jnp.arange(slot_count) < jnp.sum(owned_mask.astype(jnp.int32))
    slot_block = jnp.sum(
        jnp.where(
            jnp.logical_and(owned_mask[None, :], slot_rank[None, :] == jnp.arange(slot_count)[:, None]),
            block_order[None, :],
            0,
        ),
        axis=1,
    )

    size = D // narrow
    all_slots, x_all, cot_all, gains, cosine, sine = spread(
        masters[0].astype(bf16), hidden_in, cotangent, width_gains, n_dp, size, 6
    )
    weights = collect(
        owners * slot_count + slot_rank, all_slots.reshape(n_dp * slot_count, block_rows, D)
    ).reshape(blocks * block_rows, D)
    x_own = lax.dynamic_slice_in_dim(x_all, mp_index * own_tokens, own_tokens, 1)
    x_own = x_own.transpose(1, 0, 2).reshape(own_tokens, D).astype(f32)

    gain_qk = width_gains[0:1]

    operand, queries, keys, values, q_turned, k_turned = project(x_all, weights, gain_qk, cosine, sine)
    start_unit, start_inv = normalize(x_own)
    attended, mixed = attend(queries, keys, values)

    attn_branch, middle, middle_low = attention_sum(
        attended, weights, start_unit, gains, 3 * narrow, size, STEPS, 1
    )
    out_rows, middle_rows, up_raw, gate_raw, d_mlp, d_middle, g_rate_mlp = mlp(
        middle_low, weights, hidden_gains, middle, cot_all, gains, size, STEPS, 2
    )
    d_attn, d_start, g_rate_attn, g_scales, g_wide, g_down = mlp_back(
        d_mlp, weights, hidden_gains, up_raw, gate_raw, middle_rows, d_middle, start_unit, attn_branch, gains,
        size, STEPS, 3,
    )
    d_attn, g_wide = lax.optimization_barrier((d_attn, g_wide))
    wide_grads = lax.psum(g_wide.reshape(-1, block_rows, D), "dp")
    d_attended, attn_grad_rows = gather_project(d_attn, weights, narrow, 3 * narrow, size, STEPS, 4, "attention_gather")
    d_attended, out_rows = lax.optimization_barrier((d_attended, out_rows))
    hidden_out = lax.all_to_all(out_rows, "mp", split_axis=1, concat_axis=0, tiled=True)
    d_queries, d_keys, d_values = attend_back(queries, keys, values, mixed, d_attended)
    d_queries, hidden_out = lax.optimization_barrier((d_queries, hidden_out))
    grads_qkv, g_qk = project_back(
        d_queries, d_keys, d_values, q_turned, k_turned, gain_qk, cosine, sine
    )
    grad_in, g_attn = start_sum(
        grads_qkv, weights, d_start, start_unit, start_inv, operand, attended, attn_grad_rows, size, STEPS, 5
    )
    grad_in = grad_in.reshape(tokens, narrow).astype(f32)
    small = jnp.zeros((8, hidden_local), f32)
    small = small.at[0:1, :narrow].set(g_qk).at[1:3, :].set(g_scales)
    attn_grads, down_grads, small = tail_sum(g_attn, g_down, jnp.concatenate([g_rate_attn, g_rate_mlp], axis=0), small, n_dp, size, 7)
    width_total = jnp.concatenate([small[0:1, :narrow], small[3:5, :narrow]], axis=0)
    hidden_total = small[1:3, :]
    index = jnp.stack([slot_block, in_use.astype(jnp.int32)], axis=1)
    masters_new, firsts_new, seconds_new, weight_grads = [
        part[None]
        for part in optimizer(index, attn_grads, wide_grads, down_grads, masters[0], firsts[0], seconds[0])
    ]
    width_new, width_first_new, width_second_new = adam_update(
        width_gains, width_total, width_first, width_second, 0.0, GAIN_RATE
    )
    hidden_new, hidden_first_new, hidden_second_new = adam_update(
        hidden_gains, hidden_total, hidden_first, hidden_second, 0.0, GAIN_RATE
    )
    return (
        hidden_out,
        grad_in,
        masters_new,
        firsts_new,
        seconds_new,
        weight_grads,
        width_new,
        width_total,
        width_first_new,
        width_second_new,
        hidden_new,
        hidden_total,
        hidden_first_new,
        hidden_second_new,
    )


def solution(mesh):
    in_specs = (
        P("dp", "mp"),
        P("dp", "mp"),
        P(),
        P("mp", "dp", None, None),
        P("mp", "dp", None, None),
        P("mp", "dp", None, None),
        P(None, "mp"),
        P(None, "mp"),
        P(None, "mp"),
        P(None, "mp"),
        P(None, "mp"),
        P(None, "mp"),
    )
    out_specs = (
        P("dp", "mp"),
        P("dp", "mp"),
        P("mp", "dp", None, None),
        P("mp", "dp", None, None),
        P("mp", "dp", None, None),
        P("mp", "dp", None, None),
        P(None, "mp"),
        P(None, "mp"),
        P(None, "mp"),
        P(None, "mp"),
        P(None, "mp"),
        P(None, "mp"),
        P(None, "mp"),
        P(None, "mp"),
    )
    return jax.shard_map(functools.partial(shards, mesh.shape["dp"]), mesh=mesh, in_specs=in_specs, out_specs=out_specs, check_vma=False)
```

time: 1750 us -> 699 us (0.40)
  waiting for transfers between devices: 1030 us -> 0.02 us
  Pallas kernels: 0 us -> 648 us
  matrix products: 328 us -> 0 us
  other arithmetic: 154 us -> 17.3 us
  blocking collectives: 99.1 us -> 0 us
  local copies, waits for them, and re-layouts: 93.8 us -> 13 us
    psum x2 -> x1, waiting for transfers between devices: 716 us -> 0.01 us  [shards(): wide_grads = lax.psum(g_wide.reshape(-1, block_rows, D), 'dp')]
    pallas_call x0 -> x13, Pallas kernels: none -> 648 us  [the longest x1 169 us: spread(): pl.pallas_call(functools.partial(spread_kernel, devices, size, slots, hei...]
    dot_general x49 -> x0, matrix products: 328 us -> none  [the longest x4 63 us: attend_back(): jnp.einsum('qhd,khd->hqk', d_part, value_heads, preferred_element_type=jn...]
    reduce_scatter x4 -> x0, waiting for transfers between devices: 216 us -> none  [settle(): lax.psum_scatter(partial_value, 'mp', scatter_dimension=1, tiled=True)]
    psum x11 -> x0, blocking collectives: 99.1 us -> none  [the longest x10 62.8 us: token_sum(): return lax.psum(jnp.sum(values_in, axis=-1), 'mp')]
    all_gather x4 -> x0, waiting for transfers between devices: 97.7 us -> none  [widen_rows(): lax.all_gather(stream_part.astype(jnp.bfloat16), 'mp', axis=1, tiled=True)]
    reduce_sum x19 -> x2, other arithmetic: 60.8 us -> 1.63 us  [the longest x1 1.51 us: normalize(): jnp.sum(vector * vector, axis=-1, keepdims=True) / D + EPSILON]
    convert_element_type x14 -> x3, other arithmetic: 64.2 us -> 7.2 us  [the longest x1 3.85 us: shards(): masters[0].astype(bf16)]
  transfers between devices with their start and end apart: 10 -> 2, of which waited for: 8 -> 0; matrix products, arithmetic and copies ran while one was open for 4% -> 2% of each run, Pallas kernels for 0% -> 37%
where the time goes in v1:
time: 699 us; the launch traced here: 697 us
  Pallas kernels  648 us (93%)
  other arithmetic  17.3 us (2%)
  between operations  14.3 us (2%)
  local copies, waits for them, and re-layouts  13 us (2%)
    pallas_call x1, Pallas kernels, spread(): pl.pallas_call(functools.partial(spread_kernel, devices, size, slots, hei...  169 us
    pallas_call x1, Pallas kernels, tail_sum(): pl.pallas_call(functools.partial(tail_sum_kernel, devices, size), out_sha...  129 us
    pallas_call x1, Pallas kernels, mlp_back(): pl.pallas_call(functools.partial(mlp_back_kernel, size, steps), out_shape...  76.1 us
    pallas_call x1, Pallas kernels, mlp(): pl.pallas_call(functools.partial(mlp_kernel, size, steps), out_shape=[jax...  54.6 us
    pallas_call x1, Pallas kernels, start_sum(): pl.pallas_call(functools.partial(start_sum_kernel, size, steps), out_shap...  46.3 us
    pallas_call x1, Pallas kernels, attend_back(): pl.pallas_call(functools.partial(attend_back_kernel, block), grid=(heads...  41.9 us
    pallas_call x1, Pallas kernels, attention_sum(): pl.pallas_call(functools.partial(attention_sum_kernel, size, steps, first...  31.6 us
    pallas_call x1, Pallas kernels, gather_project(): pl.pallas_call(functools.partial(gather_project_kernel, size, steps, firs...  30 us
  transfers between devices with their start and end apart: 2, of which 0 were waited for; matrix products, arithmetic and copies ran while one was open for 2% of the time, Pallas kernels for 37%

profile of v1, /device:TPU:8, one launch (start us, length us, event | category | flops | bytes accessed | tf_op | source)
XLA Modules:
  0.0 696.7 jit_solution(5873621789426751753)
XLA Ops:
  7.2 3.8 convert_element_type.42
  11.1 1.2 slice.49.gain_ref
  12.3 169.4 %spread.1 = (bf16[8,1024,1024]{2,1,0:T(8,128)(2,1)}, bf16[4,2048,256]{2,1,0:T(8,128)(2,1)}, bf16[4,512,256]{2,1,0:T(8,128)(2,1)}, f32[3,1024]{1,0:T(4,128)}, f32[2048,128]{1,0:T(8,128)}, /*index=5*/f32[2048,128]{1,0:T(8,128)}) custom-call(bf16[1024,1024]{1,0:T(8,128)(2,1)} %bitcast.37, bf16[2048,256]{1,0:T(8,128)(2,1)} %x_ref.1, bf16[2048,256]{1,0:T(8,128)(2,1)} %cot_ref.1, ...), custom_call_target="tpu_custom_call" | custom-call | bytes 33554432 | tf_op jit(solution)/shard_map/spread/pallas_call | solution.py:1562
  181.7 1.4 convert_bitcast_fusion
  183.2 1.5 fusion
  184.9 1.6 copy.42
  186.5 1.1 convert_reduce_fusion.1
  187.7 8.6 %collect.1 = bf16[128,32,1024]{2,1,0:T(8,128)(2,1)} custom-call(s32[128]{0:T(128)} %get-tuple-element.152.places_ref, bf16[256,32,1024]{2,1,0:T(8,128)(2,1)} %bitcast.35), custom_call_target="tpu_custom_call" | custom-call | bytes 16777216 | tf_op jit(solution)/shard_map/collect/pallas_call | solution.py:1285
  196.2 3.1 broadcast_multiply_fusion.start_ref.start_hbm.unit_ref
  199.4 12.1 %project.1 = (bf16[2048,1024]{1,0:T(8,128)(2,1)}, bf16[4,2048,128]{2,1,0:T(8,128)(2,1)}, bf16[4,2048,128]{2,1,0:T(8,128)(2,1)}, bf16[4,2048,128]{2,1,0:T(8,128)(...) custom-call(bf16[4,2048,256]{2,1,0:T(8,128)(2,1)} %get-tuple-element.90.x_ref, bf16[4096,1024]{1,0:T(8,128)(2,1)} %bitcast.29, ...), custom_call_target="tpu_custom_call" | custom-call | flops 3221225472 | bytes 16777216 | tf_op jit(solution)/shard_map/project/pallas_call | solution.py:137
  211.4 19.7 %attend.1 = (bf16[2048,256]{1,0:T(8,128)(2,1)}, f32[4,2048,128]{2,1,0:T(8,128)}) custom-call(bf16[4,2048,128]{2,1,0:T(8,128)(2,1)} %get-tuple-element.94.q_ref, bf16[4,2048,128]{2,1,0:T(8,128)(2,1)} %get-tuple-element.95.k_ref, bf16[4,2048,128]{2,1,0:T(8,128)(2,1)} %get-tuple-element.96.v_ref), custom_call_target="tpu_custom_call" | custom-call | flops 8589934592 | bytes 10485760 | tf_op jit(solution)/shard_map/attend/pallas_call | solution.py:185
  231.1 31.6 %attention_sum.1 = (f32[512,1024]{1,0:T(8,128)}, f32[512,1024]{1,0:T(8,128)}, bf16[512,1024]{1,0:T(8,128)(2,1)}) custom-call(bf16[2048,256]{1,0:T(8,128)(2,1)} %get-tuple-element.98.rows_ref.attended_hbm, bf16[4096,1024]{1,0:T(8,128)(2,1)} %bitcast.30, f32[512,1024]{1,0:T(8,128)} %broadcast_multiply_fusion.start_ref.start_hbm.unit_ref, ...), custom_call_target="tpu_custom_call" | custom-call | flops 1073741824 | bytes 16777216 | tf_op jit(solution)/shard_map/attention_sum/pallas_call | solution.py:574
  262.7 54.6 %mlp.1 = (f32[512,1024]{1,0:T(8,128)}, bf16[4,512,1024]{2,1,0:T(8,128)(2,1)}, f32[2048,1024]{1,0:T(8,128)}, f32[2048,1024]{1,0:T(8,128)}, bf16[512,1024]{1,0:T(8...) custom-call(bf16[512,1024]{1,0:T(8,128)(2,1)} %get-tuple-element.100.own_ref, bf16[4096,1024]{1,0:T(8,128)(2,1)} %bitcast.31, ...), custom_call_target="tpu_custom_call" | custom-call | flops 12884901888 | bytes 25165824 | tf_op jit(solution)/shard_map/mlp/pallas_call | solution.py:653
  317.3 76.1 %mlp_back.1 = (bf16[512,1024]{1,0:T(8,128)(2,1)}, f32[512,1024]{1,0:T(8,128)}, f32[1,1024]{1,0:T(1,128)}, f32[2,1024]{1,0:T(2,128)}, bf16[2048,1024]{1,0:T(8,128)(2,1)}, /*index=5*/bf16[1024,1024]{1,0:T(8,128)(2,1)}) custom-call(bf16[512,1024]{1,0:T(8,128)(2,1)} %get-tuple-element.103.own_ref, bf16[4096,1024]{1,0:T(8,128)(2,1)} %bitcast.32, ...), custom_call_target="tpu_custom_call" | custom-call | flops 12884901888 | bytes 50331648 | tf_op jit(solution)/shard_map/mlp_back/pallas_call | solution.py:840
  393.4 30.0 %attention_gather.1 = (bf16[2048,256]{1,0:T(8,128)(2,1)}, bf16[4,512,1024]{2,1,0:T(8,128)(2,1)}) custom-call(bf16[512,1024]{1,0:T(8,128)(2,1)} %get-tuple-element.111.own_ref, bf16[4096,1024]{1,0:T(8,128)(2,1)} %bitcast.33), custom_call_target="tpu_custom_call" | custom-call | flops 1073741824 | bytes 8388608 | tf_op jit(solution)/shard_map/attention_gather/pallas_call | solution.py:894
  423.4 3.2 copy.44
  426.6 3.7 all-to-all-start
  430.4 0.9 copy.39.inv_ref
  431.2 0.6 compare_convert_fusion
  432.0 0.7 copy.40.index_ref
  433.3 41.9 %attend_back.1 = (f32[2048,256]{1,0:T(8,128)}, f32[2048,256]{1,0:T(8,128)}, f32[2048,256]{1,0:T(8,128)}) custom-call(bf16[4,2048,128]{2,1,0:T(8,128)(2,1)} %get-tuple-element.94.q_ref, bf16[4,2048,128]{2,1,0:T(8,128)(2,1)} %get-tuple-element.95.k_ref, bf16[4,2048,128]{2,1,0:T(8,128)(2,1)} %get-tuple-element.96.v_ref, ...), custom_call_target="tpu_custom_call" | custom-call | flops 21474836480 | bytes 20971520 | tf_op jit(solution)/shard_map/attend_back/pallas_call | solution.py:272
  475.3 11.6 %project_back.1 = (bf16[2048,768]{1,0:T(8,128)(2,1)}, f32[1,256]{1,0:T(1,128)}) custom-call(f32[2048,256]{1,0:T(8,128)} %get-tuple-element.118.dq_ref, f32[2048,256]{1,0:T(8,128)} %get-tuple-element.119.dk_ref, f32[2048,256]{1,0:T(8,128)} %get-tuple-element.120.dv_ref, f32[2048,256]{1,0:T(8,128)} %get-tuple-element.121.qr_ref, ...), custom_call_target="tpu_custom_call" | custom-call | flops 31457280 | bytes 13631488 | tf_op jit(solution)/shard_map/project_back/pallas_call | solution.py:320
  486.9 0.7 scatter.6
  487.8 46.3 %start_sum.1 = (bf16[4,512,256]{2,1,0:T(8,128)(2,1)}, bf16[1024,1024]{1,0:T(8,128)(2,1)}) custom-call(bf16[2048,768]{1,0:T(8,128)(2,1)} %get-tuple-element.123.rows_ref, bf16[4096,1024]{1,0:T(8,128)(2,1)} %bitcast.34, f32[512,1024]{1,0:T(8,128)} %get-tuple-element.124.base_ref, f32[512,1024]{1,0:T(8,128)} %broadcast_multiply_fusion.start_ref.start_hbm.unit_ref, ...), custom_call_target="tpu_custom_call" | custom-call | flops 3221225472 | bytes 16777216 | tf_op jit(solution)/shard_map/start_sum/pallas_call | solution.py:976
  534.2 128.7 %tail_sum.1 = (bf16[16,64,1024]{2,1,0:T(8,128)(2,1)}, bf16[16,64,1024]{2,1,0:T(8,128)(2,1)}, f32[8,1024]{1,0:T(8,128)}) custom-call(bf16[1024,1024]{1,0:T(8,128)(2,1)} %get-tuple-element.128.late_ref, bf16[1024,1024]{1,0:T(8,128)(2,1)} %get-tuple-element.129.early_ref, f32[2,1024]{1,0:T(2,128)} %pad_maximum_fusion.rates_ref, f32[8,1024]{1,0:T(8,128)} %copy-done.1), custom_call_target="tpu_custom_call" | custom-call | bytes 16777216 | tf_op jit(solution)/shard_map/tail_sum/pallas_call | solution.py:1190
  662.9 0.7 slice.51
  663.6 0.7 slice.50
  664.3 0.6 multiply_subtract_fusion.1
  665.0 1.4 multiply_subtract_fusion
  666.4 2.7 bitcast_convert_fusion
  669.1 17.7 %optimizer.1 = (f32[32,32,1024]{2,1,0:T(8,128)}, f32[32,32,1024]{2,1,0:T(8,128)}, f32[32,32,1024]{2,1,0:T(8,128)}, f32[32,32,1024]{2,1,0:T(8,128)}) custom-call(s32[32,2]{1,0:T(8,128)} %copy.40.index_ref, bf16[32,32,1024]{2,1,0:T(8,128)(2,1)} %bitcast.44, bf16[64,32,1024]{2,1,0:T(8,128)(2,1)} %all-reduce.3.cloned.1.call-done.wide_ref, ...), custom_call_target="tpu_custom_call" | custom-call | flops 20971520 | bytes 31457280 | tf_op jit(solution)/shard_map/optimizer/pallas_call | solution.py:1252
  686.8 3.0 copy.48
  (34 shorter events, 1.2 us)
Async XLA Ops:
  7.2 661.9 %all-reduce.3.cloned.1.call-start = ((), (), s32[]{:S(2)}) async-start(), calls=%async_computation.1 | async-start | bytes 8388608 | tf_op jit(solution)/shard_map/psum | solution.py:1665
  181.7 2.9 copy-start.11
  426.6 6.1 copy-start.7
  426.6 6.1 copy-start.8
  426.6 48.6 %all-to-all-start = ((f32[512,4,256]{2,0,1:T(8,128)}), f32[512,4,256]{2,0,1:T(8,128)S(1)}, u32[]{:S(2)}, u32[]{:S(2)}) async-start(f32[512,4,256]{2,0,1:T(8,128)} %bitcast.39), calls=%async_computation | async-start | bytes 4194304 | tf_op jit(solution)/shard_map/all_to_all | solution.py:1668
  475.3 11.6 %copy-start = (f32[512,4,256]{2,0,1:T(8,128)}, f32[512,4,256]{2,0,1:T(8,128)S(1)}, u32[]{:S(2)}) copy-start(f32[512,4,256]{2,0,1:T(8,128)S(1)} %all-to-all-done) | copy-start | bytes 6291460
  475.3 12.3 %copy-start.3 = (f32[2,1024]{1,0:T(2,128)S(1)}, f32[2,1024]{1,0:T(2,128)}, u32[]{:S(2)}) copy-start(f32[2,1024]{1,0:T(2,128)} %get-tuple-element.133) | copy-start | bytes 24580
  487.8 46.3 %copy-start.1 = (f32[8,1024]{1,0:T(8,128)}, f32[8,1024]{1,0:T(8,128)S(1)}, u32[]{:S(2)}) copy-start(f32[8,1024]{1,0:T(8,128)S(1)} %scatter.9.small_ref) | copy-start | bytes 98308
  534.1 130.2 %copy-start.2 = (f32[3,256]{1,0:T(4,128)S(1)}, f32[3,256]{1,0:T(4,128)}, u32[]{:S(2)}) copy-start(f32[3,256]{1,0:T(4,128)} %gains_ref.1) | copy-start | bytes 9220
  534.1 130.2 %copy-start.9 = (f32[3,256]{1,0:T(4,128)S(1)}, f32[3,256]{1,0:T(4,128)}, u32[]{:S(2)}) copy-start(f32[3,256]{1,0:T(4,128)} %param.23) | copy-start | bytes 9220
  534.1 130.2 %copy-start.10 = (f32[3,256]{1,0:T(4,128)S(1)}, f32[3,256]{1,0:T(4,128)}, u32[]{:S(2)}) copy-start(f32[3,256]{1,0:T(4,128)} %param.24) | copy-start | bytes 9220
  534.1 130.8 %copy-start.4 = (f32[2,1024]{1,0:T(2,128)S(1)}, f32[2,1024]{1,0:T(2,128)}, u32[]{:S(2)}) copy-start(f32[2,1024]{1,0:T(2,128)} %scale_ref.3) | copy-start | bytes 24580
  534.1 130.8 %copy-start.5 = (f32[2,1024]{1,0:T(2,128)S(1)}, f32[2,1024]{1,0:T(2,128)}, u32[]{:S(2)}) copy-start(f32[2,1024]{1,0:T(2,128)} %param.26) | copy-start | bytes 24580
  534.1 130.8 %copy-start.6 = (f32[2,1024]{1,0:T(2,128)S(1)}, f32[2,1024]{1,0:T(2,128)}, u32[]{:S(2)}) copy-start(f32[2,1024]{1,0:T(2,128)} %param.27) | copy-start | bytes 24580
Sparse Core Ops, SparseCore 0:
  393.5 157.2 all-reduce.2

commit v2 on v1

--- a/solution.py
+++ b/solution.py
@@ -13,6 +13,8 @@
 STEP = 7
 LANES = 128
 STEPS = 4
+MLP_STEPS = 2
+LATE_PARTS = 2
 
 EPSILON = 1e-06
 ADAM_EPSILON = 1e-08
@@ -113,7 +115,7 @@
             turned.append(here * cosine + swap_halves(here, lane) * sine)
         turned = jnp.concatenate(turned, axis=1)
         rot_ref[...] = turned
-        gained = gain_ref[...] * (turned * lax.rsqrt(head_sums(turned * turned) + EPSILON))
+        gained = gain_ref[0:1, :] * (turned * lax.rsqrt(head_sums(turned * turned) + EPSILON))
         gained = gained.astype(bf16).astype(f32)
         if which == 0:
             gained = gained * SCORE_SCALE
@@ -303,7 +305,7 @@
         unit_rows = turned * inverse
         upstream = d_ref[...]
         gg_ref[...] += jnp.sum(upstream * unit_rows, axis=0, keepdims=True)
-        upstream = upstream * gain_ref[...]
+        upstream = upstream * gain_ref[0:1, :]
         back = inverse * (upstream - unit_rows * head_sums(unit_rows * upstream))
         for pair in range(narrow // LANES):
             here = back[:, pair * LANES : (pair + 1) * LANES]
@@ -317,10 +319,11 @@
     rows = min(512, tokens)
     row_spec = lambda width: pl.BlockSpec((rows, width), lambda i: (i, 0))
     one = pl.BlockSpec((1, narrow), lambda i: (0, 0))
+    whole = pl.BlockSpec(gain.shape, lambda i: (0, 0))
     return pl.pallas_call(
         functools.partial(project_back_kernel, narrow),
         grid=(tokens // rows,),
-        in_specs=[row_spec(narrow)] * 5 + [one, row_spec(LANES), row_spec(LANES)],
+        in_specs=[row_spec(narrow)] * 5 + [whole, row_spec(LANES), row_spec(LANES)],
         out_specs=[row_spec(3 * narrow), one],
         out_shape=[
             jax.ShapeDtypeStruct((tokens, 3 * narrow), bf16),
@@ -425,7 +428,7 @@
                 return self.copy(here, here, g_send.at[chips + k - 1, s], g_recv.at[device, s], self.partner)
 
         if settle:
-            out_ref, mine, kept, to_partner, from_partner, to_chip, from_chip, p_send, p_recv, x_send, x_recv = settle
+            out_ref, kept, to_partner, from_partner, to_chip, from_chip, p_send, p_recv, x_send, x_recv = settle
 
             def to_partner_copy(k, s):
                 return self.copy(self.piece(to_partner, k, s), self.piece(from_partner, k, s), p_send.at[k, s], p_recv.at[k, s], self.partner)
@@ -456,7 +459,7 @@
 
                 @pl.when(is_own)
                 def _():
-                    mine[here, :] = term
+                    out_ref[here, :] = term
 
                 @pl.when(is_first)
                 def _():
@@ -481,7 +484,7 @@
             if settle:
                 here = pl.ds(pl.multiple_of(s * self.rows, self.rows), self.rows)
                 to_partner_copy(0, s).wait_recv()
-                total = mine[here, :] + from_partner[0, here, :].astype(f32)
+                total = out_ref[here, :] + from_partner[0, here, :].astype(f32)
                 for k in range(1, chips):
                     to_chip_copy(k, s).wait_recv()
                     total = total + from_chip[k - 1, here, :].astype(f32)
@@ -503,7 +506,6 @@
 def settle_scratch(size, steps, tokens):
     own, chips = tokens // size, size // 2
     return [
-        pltpu.VMEM((own, D), f32),
         pltpu.VMEM((own // steps, D), f32),
         pltpu.VMEM((chips, own, D), bf16),
         pltpu.VMEM((chips, own, D), bf16),
@@ -522,7 +524,7 @@
 
 VMEM_WHOLE = pl.BlockSpec(memory_space=pltpu.VMEM)
 ANYWHERE = pl.BlockSpec(memory_space=pl.ANY)
-GRANT = 63 << 20
+GRANT = 67043328
 
 
 def weight_scratch(rows, count=1):
@@ -628,7 +630,8 @@
         here = pl.ds(pl.multiple_of(s * group.rows, group.rows), group.rows)
         middle, rate = middle_ref[here, :], rates_ref[2:3, :]
         branch_unit, branch_inv, mixed, mixed_inv = blend_branch(middle, branch_ref[here, :], rate)
-        out_ref[here, :] = mixed
+        for d in range(size):
+            out_ref[d, here, :] = mixed[:, d * (D // size) : (d + 1) * (D // size)]
         upstream = jnp.concatenate([cot_ref[d, here, :] for d in range(size)], axis=1).astype(f32)
         d_middle, d_branch, g_rate = blend_back(
             middle, branch_unit, branch_inv, mixed, mixed_inv, rate, upstream
@@ -653,7 +656,7 @@
     return pl.pallas_call(
         functools.partial(mlp_kernel, size, steps),
         out_shape=[
-            jax.ShapeDtypeStruct((own.shape[0], D), f32),
+            jax.ShapeDtypeStruct((size, own.shape[0], D // size), f32),
             jax.ShapeDtypeStruct((size, own.shape[0], D), bf16),
             jax.ShapeDtypeStruct((tokens, hidden), f32),
             jax.ShapeDtypeStruct((tokens, hidden), f32),
@@ -733,8 +736,10 @@
         def _():
             weight_grads(device)
 
+    late_rows = late.shape[2]
+
     def late_copies(s):
-        here = pl.ds(pl.multiple_of(s * group.rows, group.rows), group.rows)
+        here = pl.ds(pl.multiple_of(s * late_rows, late_rows), late_rows)
         return [
             pltpu.make_async_copy(ref.at[here, :], late.at[lax.rem(s, 2), i], late_sem.at[lax.rem(s, 2), i])
             for i, ref in enumerate((start_hbm, branch_hbm, d_middle_hbm))
@@ -743,12 +748,12 @@
     for c in late_copies(0):
         c.start()
 
-    def after(s):
-        here = pl.ds(pl.multiple_of(s * group.rows, group.rows), group.rows)
+    def after_part(s, carry):
+        here = pl.ds(pl.multiple_of(s * late_rows, late_rows), late_rows)
         for c in late_copies(s):
             c.wait()
 
-        @pl.when(s + 1 < steps)
+        @pl.when(s + 1 < steps * LATE_PARTS)
         def _():
             for c in late_copies(s + 1):
                 c.start()
@@ -762,6 +767,10 @@
         d_start_ref[here, :] = d_start
         d_attn_ref[here, :] = d_branch.astype(bf16)
         g_rate_ref[...] += g_rate[None]
+        return carry
+
+    def after(s):
+        lax.fori_loop(s * LATE_PARTS, (s + 1) * LATE_PARTS, after_part, 0)
 
     def compute(device, s, i):
         slot = lax.rem(i, 2)
@@ -852,7 +861,7 @@
         scratch_shapes=[
             pltpu.VMEM((2, min(256, hidden), D), bf16),
             pltpu.SemaphoreType.DMA((2,)),
-            pltpu.VMEM((2, 3, rows, D), f32),
+            pltpu.VMEM((2, 3, rows // LATE_PARTS, D), f32),
             pltpu.SemaphoreType.DMA((2, 3)),
             pltpu.VMEM((own.shape[0], D), f32),
             pltpu.VMEM((size, own.shape[0], D), bf16),
@@ -908,10 +917,10 @@
 
 def start_sum_kernel(
     size, steps, rows_ref, w_hbm, base_ref, unit_ref, inv_ref, operand_hbm, attended_hbm, d_attn_hbm,
-    out_ref, grads_ref, operand_ref, attended_ref, d_attn_ref, late_sem, w_ref, w_sem, total_ref, pieces, d_send, d_recv, *scratch
+    pieces, grads_ref, operand_ref, attended_ref, d_attn_ref, late_sem, w_ref, w_sem, total_ref, *scratch
 ):
     tokens = rows_ref.shape[0]
-    narrow = out_ref.shape[2]
+    narrow = pieces.shape[2]
     group = Group(size, steps, tokens)
     copies = weight_copies(w_hbm, [w_ref], w_sem, 0)
     copies[0].start()
@@ -923,27 +932,18 @@
     ]
     for copy in late:
         copy.start()
-    group.meet(everyone=True)
+    group.meet()
     copies[0].wait()
 
     def compute(device, s, i):
         first = pl.multiple_of(device * group.own + s * group.rows, group.rows)
         return nn(rows_ref[pl.ds(first, group.rows), :], w_ref[...])
 
-    def deal(j, s):
-        device = lax.rem(group.me + j, size)
-        return group.copy(
-            group.piece(pieces, device, s), group.piece(out_ref, group.me, s), d_send.at[j - 1, s], d_recv.at[group.me, s], device
-        )
-
     def after(s):
         here = pl.ds(pl.multiple_of(s * group.rows, group.rows), group.rows)
-        back = normalize_back(unit_ref[here, :], inv_ref[here, :], base_ref[here, :] + total_ref[here, :])
+        back = normalize_back(unit_ref[here, :], inv_ref[here, 0:1], base_ref[here, :] + total_ref[here, :])
         for device in range(size):
             pieces[device, here, :] = back[:, device * narrow : (device + 1) * narrow].astype(bf16)
-        out_ref[group.me, here, :] = pieces[group.me, here, :]
-        for j in range(1, size):
-            deal(j, s).start()
 
     group.run(compute, settle=(total_ref, *scratch), remote_first=True, after=after)
 
@@ -958,16 +958,6 @@
         out_sum += tn(attended_ref[d * group.own : (d + 1) * group.own, :], d_attn_ref[d])
     grads_ref[3 * narrow :, :] = out_sum.astype(bf16)
     group.end(3 * steps // 4, steps)
-
-    def finish(s, carry):
-        for j in range(1, size):
-            device = lax.rem(group.me + j, size)
-            here = group.piece(out_ref, device, s)
-            group.copy(here, here, d_send.at[j - 1, s], d_recv.at[device, s], group.partner).wait_recv()
-            deal(j, s).wait_send()
-        return carry
-
-    lax.fori_loop(0, steps, finish, 0)
 
 
 def start_sum(rows, weights, base, unit_rows, inverse, operand, attended, d_attn_rows, size, steps, collective_id):
@@ -987,9 +977,6 @@
         + weight_scratch(depth)
         + [
             pltpu.VMEM((own, D), f32),
-            pltpu.VMEM((size, own, narrow), bf16),
-            pltpu.SemaphoreType.DMA((size - 1, steps)),
-            pltpu.SemaphoreType.DMA((size, steps)),
         ]
         + settle_scratch(size, steps, tokens),
         compiler_params=remote_params(collective_id),
@@ -1006,9 +993,10 @@
 
 
 def tail_sum_kernel(
-    devices, size, late_ref, early_ref, rates_ref, small_ref, late_out, early_out, small_out,
+    devices, size, late_ref, early_ref, rates_ref, small_ref, hidden_ref, back_ref,
+    late_out, early_out, small_out, hidden_out, back_out,
     y_land, y_sum, z_land, rate_parts, rate_land, pack, small_land,
-    a_send, a_recv, b_send, b_recv, c_send, c_recv, d_send, d_recv, m_send, m_recv, s_send, s_recv
+    a_send, a_recv, b_send, b_recv, c_send, c_recv, d_send, d_recv, m_send, m_recv, s_send, s_recv, h_send, h_recv, g_send, g_recv
 ):
     dp, me = lax.axis_index("dp"), lax.axis_index("mp")
     lines, columns, cuts, rows = tail_plan(devices, late_ref.shape[0])
@@ -1092,6 +1080,26 @@
         rate_parts[d, 0:2, :] = rates_ref[:, d * narrow : (d + 1) * narrow]
     for j in range(1, size):
         rate_copy(j).start()
+
+    def deal(j):
+        device = lax.rem(me + j, size)
+        return [
+            remote(source.at[device], target.at[me], send.at[j - 1], receive.at[me], (dp, device))
+            for source, target, send, receive in ((hidden_ref, hidden_out, h_send, h_recv), (back_ref, back_out, g_send, g_recv))
+        ]
+
+    def dealt(j):
+        device = lax.rem(me + j, size)
+        return [
+            remote(target.at[device], target.at[device], send.at[j - 1], receive.at[device], (dp, device))
+            for target, send, receive in ((hidden_out, h_send, h_recv), (back_out, g_send, g_recv))
+        ]
+
+    for j in range(1, size):
+        for copy in deal(j):
+            copy.start()
+    hidden_out[me] = hidden_ref[me]
+    back_out[me] = back_ref[me]
 
     rates = rate_parts[me]
     for j in range(1, size):
@@ -1179,9 +1187,13 @@
     lax.fori_loop(1, devices, finish, 0)
     for j in range(1, size):
         rate_copy(j).wait_send()
-
-
-def tail_sum(late, early, rates, small, devices, size, collective_id):
+        for copy in dealt(j):
+            copy.wait_recv()
+        for copy in deal(j):
+            copy.wait_send()
+
+
+def tail_sum(late, early, rates, small, hidden, back, devices, size, collective_id):
     lines, columns, cuts, rows = tail_plan(devices, late.shape[0])
     narrow = D // size
     chunks = 2 * cuts
@@ -1189,9 +1201,9 @@
     total = jax.ShapeDtypeStruct((late.shape[0] // rows, rows, D), bf16)
     return pl.pallas_call(
         functools.partial(tail_sum_kernel, devices, size),
-        out_shape=[total, total, jax.ShapeDtypeStruct(small.shape, f32)],
-        in_specs=[VMEM_WHOLE] * 4,
-        out_specs=[VMEM_WHOLE] * 3,
+        out_shape=[total, total] + [jax.ShapeDtypeStruct(x.shape, x.dtype) for x in (small, hidden, back)],
+        in_specs=[VMEM_WHOLE] * 6,
+        out_specs=[VMEM_WHOLE] * 5,
         scratch_shapes=[
             pltpu.VMEM((chunks, columns, lines * rows, D), bf16),
             pltpu.VMEM((chunks, lines * rows, D), bf16),
@@ -1206,11 +1218,13 @@
             dma((chunks, lines, columns)), dma((chunks, lines, columns)),
             dma((size - 1,)), dma((size,)),
             dma((devices - 1,)), dma((devices,)),
+            dma((size - 1,)), dma((size,)),
+            dma((size - 1,)), dma((size,)),
         ],
         compiler_params=remote_params(collective_id),
         cost_estimate=pl.CostEstimate(flops=0, bytes_accessed=late.shape[0] * D * 16, transcendentals=0),
         name="tail_sum",
-    )(late, early, rates, small)
+    )(late, early, rates, small, hidden, back)
 
 
 def optimizer_kernel(
@@ -1308,7 +1322,7 @@
 
 def spread_kernel(
     devices, size, slots, height, slots_ref, x_ref, cot_ref, gains_ref,
-    all_ref, x_all, cot_all, gains_all, cos_ref, sin_ref, gains_land,
+    all_ref, x_all, cot_all, gains_all, cos_ref, sin_ref, start_ref, inv_ref, gains_land, x_own_ref,
     z_send, z_recv, y_send, y_recv, e_send, e_recv, x_send, x_recv, c_send, c_recv, w_send, w_recv, local_sem
 ):
     lines, columns, across, cuts = spread_plan(devices, slots)
@@ -1509,14 +1523,32 @@
                         for j in range(1, columns):
                             over(line, c, j).start()
 
+    for s in range(x_steps):
+        x_got(s, partner).wait_recv()
+        for k in range(1, chips):
+            x_got(s, other(k, 1 - core)).wait_recv()
+    local[1].wait()
+    mine = pltpu.make_async_copy(
+        x_all.at[:, pl.ds(pl.multiple_of(me * own, own), own), :], x_own_ref, local_sem.at[1]
+    )
+    mine.start()
+    mine.wait()
+    start_rows = min(128, own)
+
+    def start_part(i, carry):
+        here = pl.ds(pl.multiple_of(i * start_rows, start_rows), start_rows)
+        x = jnp.concatenate([x_own_ref[d, here, :] for d in range(size)], axis=1).astype(f32)
+        unit_rows, inverse = normalize(x)
+        start_ref[here, :] = unit_rows
+        inv_ref[here, :] = jnp.broadcast_to(inverse, (start_rows, LANES))
+        return carry
+
+    lax.fori_loop(0, own // start_rows, start_part, 0)
+
     for line in range(lines):
         for c in range(cuts):
             for j in range(1, columns):
                 over_got(line, column(j), c).wait_recv()
-    for s in range(x_steps):
-        x_got(s, partner).wait_recv()
-        for k in range(1, chips):
-            x_got(s, other(k, 1 - core)).wait_recv()
     for j in range(1, size):
         cot_got(j).wait_recv()
         here = gains_land.at[mp_peer(j)]
@@ -1524,8 +1556,8 @@
         gains_own(j).wait_send()
     for d in range(size):
         gains_all[:, d * narrow : (d + 1) * narrow] = gains_land[d]
-    for copy in local:
-        copy.wait()
+    local[0].wait()
+    local[2].wait()
     if across:
         for j in range(1, columns):
             early(j).wait_send()
@@ -1568,11 +1600,14 @@
             jax.ShapeDtypeStruct((gains.shape[0], D), f32),
             jax.ShapeDtypeStruct((tokens, LANES), f32),
             jax.ShapeDtypeStruct((tokens, LANES), f32),
+            jax.ShapeDtypeStruct((tokens // size, D), f32),
+            jax.ShapeDtypeStruct((tokens // size, LANES), f32),
         ],
         in_specs=[VMEM_WHOLE] * 4,
-        out_specs=[ANYWHERE] * 3 + [VMEM_WHOLE] * 3,
+        out_specs=[ANYWHERE] * 3 + [VMEM_WHOLE] * 5,
         scratch_shapes=[
             pltpu.VMEM((size, *gains.shape), f32),
+            pltpu.VMEM((size, tokens // size, narrow), bf16),
             dma((lines, 2, items)),
             dma((lines, items)),
             dma((lines, columns, cuts)),
@@ -1636,19 +1671,13 @@
     )
 
     size = D // narrow
-    all_slots, x_all, cot_all, gains, cosine, sine = spread(
+    all_slots, x_all, cot_all, gains, cosine, sine, start_unit, start_inv = spread(
         masters[0].astype(bf16), hidden_in, cotangent, width_gains, n_dp, size, 6
     )
     weights = collect(
         owners * slot_count + slot_rank, all_slots.reshape(n_dp * slot_count, block_rows, D)
     ).reshape(blocks * block_rows, D)
-    x_own = lax.dynamic_slice_in_dim(x_all, mp_index * own_tokens, own_tokens, 1)
-    x_own = x_own.transpose(1, 0, 2).reshape(own_tokens, D).astype(f32)
-
-    gain_qk = width_gains[0:1]
-
-    operand, queries, keys, values, q_turned, k_turned = project(x_all, weights, gain_qk, cosine, sine)
-    start_unit, start_inv = normalize(x_own)
+    operand, queries, keys, values, q_turned, k_turned = project(x_all, weights, width_gains, cosine, sine)
     attended, mixed = attend(queries, keys, values)
 
     attn_branch, middle, middle_low = attention_sum(
@@ -1659,25 +1688,23 @@
     )
     d_attn, d_start, g_rate_attn, g_scales, g_wide, g_down = mlp_back(
         d_mlp, weights, hidden_gains, up_raw, gate_raw, middle_rows, d_middle, start_unit, attn_branch, gains,
-        size, STEPS, 3,
+        size, MLP_STEPS, 3,
     )
     d_attn, g_wide = lax.optimization_barrier((d_attn, g_wide))
     wide_grads = lax.psum(g_wide.reshape(-1, block_rows, D), "dp")
     d_attended, attn_grad_rows = gather_project(d_attn, weights, narrow, 3 * narrow, size, STEPS, 4, "attention_gather")
-    d_attended, out_rows = lax.optimization_barrier((d_attended, out_rows))
-    hidden_out = lax.all_to_all(out_rows, "mp", split_axis=1, concat_axis=0, tiled=True)
     d_queries, d_keys, d_values = attend_back(queries, keys, values, mixed, d_attended)
-    d_queries, hidden_out = lax.optimization_barrier((d_queries, hidden_out))
     grads_qkv, g_qk = project_back(
-        d_queries, d_keys, d_values, q_turned, k_turned, gain_qk, cosine, sine
-    )
-    grad_in, g_attn = start_sum(
+        d_queries, d_keys, d_values, q_turned, k_turned, width_gains, cosine, sine
+    )
+    grad_pieces, g_attn = start_sum(
         grads_qkv, weights, d_start, start_unit, start_inv, operand, attended, attn_grad_rows, size, STEPS, 5
     )
-    grad_in = grad_in.reshape(tokens, narrow).astype(f32)
     small = jnp.zeros((8, hidden_local), f32)
     small = small.at[0:1, :narrow].set(g_qk).at[1:3, :].set(g_scales)
-    attn_grads, down_grads, small = tail_sum(g_attn, g_down, jnp.concatenate([g_rate_attn, g_rate_mlp], axis=0), small, n_dp, size, 7)
+    attn_grads, down_grads, small, hidden_out, grad_in = tail_sum(g_attn, g_down, jnp.concatenate([g_rate_attn, g_rate_mlp], axis=0), small, out_rows, grad_pieces, n_dp, size, 7)
+    hidden_out = hidden_out.reshape(tokens, narrow)
+    grad_in = grad_in.reshape(tokens, narrow).astype(f32)
     width_total = jnp.concatenate([small[0:1, :narrow], small[3:5, :narrow]], axis=0)
     hidden_total = small[1:3, :]
     index = jnp.stack([slot_block, in_use.astype(jnp.int32)], axis=1)

time: 699 us -> 679 us (0.971)
    pallas_call x1, Pallas kernels: 129 us -> 147 us  [tail_sum(): pl.pallas_call(functools.partial(tail_sum_kernel, devices, size), out_sha...]
    pallas_call x1, Pallas kernels: 76.1 us -> 64.2 us  [mlp_back(): pl.pallas_call(functools.partial(mlp_back_kernel, size, steps), out_shape...]
    pallas_call x1, Pallas kernels: 46.3 us -> 35.3 us  [start_sum(): pl.pallas_call(functools.partial(start_sum_kernel, size, steps), out_shap...]
  transfers between devices with their start and end apart: 2 -> 1, of which waited for: 0 -> 0; matrix products, arithmetic and copies ran while one was open for 2% -> 2% of each run, Pallas kernels for 37% -> 39%
where the time goes in v2:
time: 679 us; the launch traced here: 678 us
  Pallas kernels  643 us (95%)
  between operations  14.2 us (2%)
  other arithmetic  12.7 us (2%)
  local copies, waits for them, and re-layouts  7.86 us (1%)
    pallas_call x1, Pallas kernels, spread(): pl.pallas_call(functools.partial(spread_kernel, devices, size, slots, hei...  170 us
    pallas_call x1, Pallas kernels, tail_sum(): pl.pallas_call(functools.partial(tail_sum_kernel, devices, size), out_sha...  147 us
    pallas_call x1, Pallas kernels, mlp_back(): pl.pallas_call(functools.partial(mlp_back_kernel, size, steps), out_shape...  64.2 us
    pallas_call x1, Pallas kernels, mlp(): pl.pallas_call(functools.partial(mlp_kernel, size, steps), out_shape=[jax...  54.8 us
    pallas_call x1, Pallas kernels, attend_back(): pl.pallas_call(functools.partial(attend_back_kernel, block), grid=(heads...  42.1 us
    pallas_call x1, Pallas kernels, start_sum(): pl.pallas_call(functools.partial(start_sum_kernel, size, steps), out_shap...  35.3 us
    pallas_call x1, Pallas kernels, attention_sum(): pl.pallas_call(functools.partial(attention_sum_kernel, size, steps, first...  31.5 us
    pallas_call x1, Pallas kernels, gather_project(): pl.pallas_call(functools.partial(gather_project_kernel, size, steps, firs...  30.1 us
  transfers between devices with their start and end apart: 1, of which 0 were waited for; matrix products, arithmetic and copies ran while one was open for 2% of the time, Pallas kernels for 39%

profile of v2, /device:TPU:8, one launch (start us, length us, event | category | flops | bytes accessed | tf_op | source)
XLA Modules:
  0.0 677.8 jit_solution(3640641496044762316)
XLA Ops:
  7.2 0.0 all-reduce.3.cloned.1.call-start
  7.2 3.9 convert_element_type.29
  11.1 0.2 convert_reduce_fusion
  11.3 0.0 copy-start.4
  11.3 1.2 convert_reduce_fusion.1
  12.4 170.1 %spread.1 = (bf16[8,1024,1024]{2,1,0:T(8,128)(2,1)}, bf16[4,2048,256]{2,1,0:T(8,128)(2,1)}, bf16[4,512,256]{2,1,0:T(8,128)(2,1)}, f32[3,1024]{1,0:T(4,128)}, f32...) custom-call(bf16[1024,1024]{1,0:T(8,128)(2,1)} %bitcast.26, ...), custom_call_target="tpu_custom_call" | custom-call | bytes 33554432 | tf_op jit(solution)/shard_map/spread/pallas_call | solution.py:1594
  182.6 8.6 %collect.1 = bf16[128,32,1024]{2,1,0:T(8,128)(2,1)} custom-call(s32[128]{0:T(128)} %get-tuple-element.152.places_ref, bf16[256,32,1024]{2,1,0:T(8,128)(2,1)} %bitcast.24), custom_call_target="tpu_custom_call" | custom-call | bytes 16777216 | tf_op jit(solution)/shard_map/collect/pallas_call | solution.py:1299
  191.2 12.1 %project.1 = (bf16[2048,1024]{1,0:T(8,128)(2,1)}, bf16[4,2048,128]{2,1,0:T(8,128)(2,1)}, bf16[4,2048,128]{2,1,0:T(8,128)(2,1)}, bf16[4,2048,128]{2,1,0:T(8,128)(...) custom-call(bf16[4,2048,256]{2,1,0:T(8,128)(2,1)} %get-tuple-element.90.x_ref, bf16[4096,1024]{1,0:T(8,128)(2,1)} %bitcast.18, ...), custom_call_target="tpu_custom_call" | custom-call | flops 3221225472 | bytes 16777216 | tf_op jit(solution)/shard_map/project/pallas_call | solution.py:139
  203.3 19.7 %attend.1 = (bf16[2048,256]{1,0:T(8,128)(2,1)}, f32[4,2048,128]{2,1,0:T(8,128)}) custom-call(bf16[4,2048,128]{2,1,0:T(8,128)(2,1)} %get-tuple-element.94.q_ref, bf16[4,2048,128]{2,1,0:T(8,128)(2,1)} %get-tuple-element.95.k_ref, bf16[4,2048,128]{2,1,0:T(8,128)(2,1)} %get-tuple-element.96.v_ref), custom_call_target="tpu_custom_call" | custom-call | flops 8589934592 | bytes 10485760 | tf_op jit(solution)/shard_map/attend/pallas_call | solution.py:187
  222.9 31.5 %attention_sum.1 = (f32[512,1024]{1,0:T(8,128)}, f32[512,1024]{1,0:T(8,128)}, bf16[512,1024]{1,0:T(8,128)(2,1)}) custom-call(bf16[2048,256]{1,0:T(8,128)(2,1)} %get-tuple-element.98.rows_ref.attended_hbm, bf16[4096,1024]{1,0:T(8,128)(2,1)} %bitcast.19, f32[512,1024]{1,0:T(8,128)} %get-tuple-element.99.start_ref.start_hbm.unit_ref, ...), custom_call_target="tpu_custom_call" | custom-call | flops 1073741824 | bytes 16777216 | tf_op jit(solution)/shard_map/attention_sum/pallas_call | solution.py:576
  254.4 54.8 %mlp.1 = (f32[4,512,256]{2,1,0:T(8,128)}, bf16[4,512,1024]{2,1,0:T(8,128)(2,1)}, f32[2048,1024]{1,0:T(8,128)}, f32[2048,1024]{1,0:T(8,128)}, bf16[512,1024]{1,0:...) custom-call(bf16[512,1024]{1,0:T(8,128)(2,1)} %get-tuple-element.101.own_ref, bf16[4096,1024]{1,0:T(8,128)(2,1)} %bitcast.20, ...), custom_call_target="tpu_custom_call" | custom-call | flops 12884901888 | bytes 25165824 | tf_op jit(solution)/shard_map/mlp/pallas_call | solution.py:656
  309.2 64.2 %mlp_back.1 = (bf16[512,1024]{1,0:T(8,128)(2,1)}, f32[512,1024]{1,0:T(8,128)}, f32[1,1024]{1,0:T(1,128)}, f32[2,1024]{1,0:T(2,128)}, bf16[2048,1024]{1,0:T(8,128)(2,1)}, /*index=5*/bf16[1024,1024]{1,0:T(8,128)(2,1)}) custom-call(bf16[512,1024]{1,0:T(8,128)(2,1)} %get-tuple-element.104.own_ref, bf16[4096,1024]{1,0:T(8,128)(2,1)} %bitcast.21, ...), custom_call_target="tpu_custom_call" | custom-call | flops 12884901888 | bytes 50331648 | tf_op jit(solution)/shard_map/mlp_back/pallas_call | solution.py:849
  373.4 0.0 all-reduce.3.cloned.1.call-update
  373.5 30.1 %attention_gather.1 = (bf16[2048,256]{1,0:T(8,128)(2,1)}, bf16[4,512,1024]{2,1,0:T(8,128)(2,1)}) custom-call(bf16[512,1024]{1,0:T(8,128)(2,1)} %get-tuple-element.112.own_ref, bf16[4096,1024]{1,0:T(8,128)(2,1)} %bitcast.22), custom_call_target="tpu_custom_call" | custom-call | flops 1073741824 | bytes 8388608 | tf_op jit(solution)/shard_map/attention_gather/pallas_call | solution.py:903
  403.6 42.1 %attend_back.1 = (f32[2048,256]{1,0:T(8,128)}, f32[2048,256]{1,0:T(8,128)}, f32[2048,256]{1,0:T(8,128)}) custom-call(bf16[4,2048,128]{2,1,0:T(8,128)(2,1)} %get-tuple-element.94.q_ref, bf16[4,2048,128]{2,1,0:T(8,128)(2,1)} %get-tuple-element.95.k_ref, bf16[4,2048,128]{2,1,0:T(8,128)(2,1)} %get-tuple-element.96.v_ref, ...), custom_call_target="tpu_custom_call" | custom-call | flops 21474836480 | bytes 20971520 | tf_op jit(solution)/shard_map/attend_back/pallas_call | solution.py:274
  445.7 10.8 %project_back.1 = (bf16[2048,768]{1,0:T(8,128)(2,1)}, f32[1,256]{1,0:T(1,128)}) custom-call(f32[2048,256]{1,0:T(8,128)} %get-tuple-element.114.dq_ref, f32[2048,256]{1,0:T(8,128)} %get-tuple-element.115.dk_ref, f32[2048,256]{1,0:T(8,128)} %get-tuple-element.116.dv_ref, f32[2048,256]{1,0:T(8,128)} %get-tuple-element.117.qr_ref, ...), custom_call_target="tpu_custom_call" | custom-call | flops 31457280 | bytes 13631488 | tf_op jit(solution)/shard_map/project_back/pallas_call | solution.py:323
  456.5 1.3 scatter.6
  457.8 1.4 scatter.9.small_ref
  459.2 0.0 copy-done.2
  459.2 0.6 pad_maximum_fusion.rates_ref
  459.8 35.3 %start_sum.1 = (bf16[4,512,256]{2,1,0:T(8,128)(2,1)}, bf16[1024,1024]{1,0:T(8,128)(2,1)}) custom-call(bf16[2048,768]{1,0:T(8,128)(2,1)} %get-tuple-element.119.rows_ref, bf16[4096,1024]{1,0:T(8,128)(2,1)} %bitcast.23, f32[512,1024]{1,0:T(8,128)} %get-tuple-element.120.base_ref, f32[512,1024]{1,0:T(8,128)} %get-tuple-element.99.start_ref.start_hbm.unit_ref, ...), custom_call_target="tpu_custom_call" | custom-call | flops 3221225472 | bytes 16777216 | tf_op jit(solution)/shard_map/start_sum/pallas_call | solution.py:966
  495.1 147.3 %tail_sum.1 = (bf16[16,64,1024]{2,1,0:T(8,128)(2,1)}, bf16[16,64,1024]{2,1,0:T(8,128)(2,1)}, f32[8,1024]{1,0:T(8,128)}, f32[4,512,256]{2,1,0:T(8,128)}, bf16[4,512,256]{2,1,0:T(8,128)(2,1)}) custom-call(bf16[1024,1024]{1,0:T(8,128)(2,1)} %get-tuple-element.124.late_ref, bf16[1024,1024]{1,0:T(8,128)(2,1)} %get-tuple-element.125.early_ref, ...), custom_call_target="tpu_custom_call" | custom-call | bytes 16777216 | tf_op jit(solution)/shard_map/tail_sum/pallas_call | solution.py:1202
  642.3 0.7 slice.47
  643.0 0.7 slice.46
  643.7 0.6 compare_convert_fusion
  644.4 0.8 select_reduce_fusion
  645.2 0.7 copy.28.index_ref
  645.9 1.3 multiply_subtract_fusion.1
  647.2 1.4 multiply_subtract_fusion
  648.7 2.7 bitcast_convert_fusion
  651.4 16.6 %optimizer.1 = (f32[32,32,1024]{2,1,0:T(8,128)}, f32[32,32,1024]{2,1,0:T(8,128)}, f32[32,32,1024]{2,1,0:T(8,128)}, f32[32,32,1024]{2,1,0:T(8,128)}) custom-call(s32[32,2]{1,0:T(8,128)} %copy.28.index_ref, bf16[32,32,1024]{2,1,0:T(8,128)(2,1)} %bitcast.30, bf16[64,32,1024]{2,1,0:T(8,128)(2,1)} %all-reduce.3.cloned.1.call-done.wide_ref, ...), custom_call_target="tpu_custom_call" | custom-call | flops 20971520 | bytes 31457280 | tf_op jit(solution)/shard_map/optimizer/pallas_call | solution.py:1266
  667.9 3.0 copy.32
  (10 shorter events, 0.0 us)
Async XLA Ops:
  7.2 644.2 %all-reduce.3.cloned.1.call-start = ((), (), s32[]{:S(2)}) async-start(), calls=%async_computation | async-start | bytes 8388608 | tf_op jit(solution)/shard_map/psum | solution.py:1694
  7.2 3.9 copy-start.3
  11.3 1.2 copy-start.4
  445.7 12.1 %copy-start = (f32[2,1024]{1,0:T(2,128)S(1)}, f32[2,1024]{1,0:T(2,128)}, u32[]{:S(2)}) copy-start(f32[2,1024]{1,0:T(2,128)} %get-tuple-element.129) | copy-start | bytes 24580
  445.7 13.5 %copy-start.1 = (f32[1,1024]{1,0:T(1,128)S(1)}, f32[1,1024]{1,0:T(1,128)}, u32[]{:S(2)}) copy-start(f32[1,1024]{1,0:T(1,128)} %get-tuple-element.127) | copy-start | bytes 12292
  445.7 13.5 %copy-start.2 = (f32[1,1024]{1,0:T(1,128)S(1)}, f32[1,1024]{1,0:T(1,128)}, u32[]{:S(2)}) copy-start(f32[1,1024]{1,0:T(1,128)} %get-tuple-element.126) | copy-start | bytes 12292
Sparse Core Ops, SparseCore 0:
  373.6 181.7 all-reduce.2

commit v3 on v2

--- a/solution.py
+++ b/solution.py
@@ -683,7 +683,7 @@
 
 def mlp_back_kernel(
     size, steps, own_ref, w_hbm, scale_ref, ur_hbm, gr_hbm, middle_rows_ref, d_middle_hbm, start_hbm, branch_hbm, rates_ref,
-    d_attn_ref, d_start_ref, g_rate_ref, gs_ref, wide_hbm, down_hbm,
+    d_attn_ref, d_start_ref, g_rate_ref, gs_ref, grads_hbm,
     stage, stage_sem, late, late_sem,
     sum_ref, rows_ref, product_ref, d_ref, grads_sum,
     up_ref, gate_ref, down_ref, w_sem, u_buf, g_buf, b_sem, *scratch
@@ -813,34 +813,24 @@
 
     lax.fori_loop(0, size - 2, rest, 0)
 
-    wide_parts = 2 * hidden // part
-
-    def stage_copy(c, ref, first):
-        here = pl.ds(pl.multiple_of((c - first) * part, part), part)
-        return pltpu.make_async_copy(stage.at[lax.rem(c, 2)], ref.at[here, :], stage_sem.at[lax.rem(c, 2)])
+    def stage_copy(c):
+        here = pl.ds(pl.multiple_of(c * part, part), part)
+        return pltpu.make_async_copy(stage.at[lax.rem(c, 2)], grads_hbm.at[here, :], stage_sem.at[lax.rem(c, 2)])
 
     def put(c, carry):
         @pl.when(c >= 2)
         def _():
-            stage_copy(lax.rem(c, 2), wide_hbm, 0).wait()
+            stage_copy(c - 2).wait()
 
         stage[lax.rem(c, 2)] = grads_sum[pl.ds(pl.multiple_of(c * part, part), part), :].astype(bf16)
-
-        @pl.when(c < wide_parts)
-        def _():
-            stage_copy(c, wide_hbm, 0).start()
-
-        @pl.when(c >= wide_parts)
-        def _():
-            stage_copy(c, down_hbm, wide_parts).start()
-
+        stage_copy(c).start()
         return carry
 
     parts = 3 * hidden // part
     lax.fori_loop(0, parts, put, 0)
     group.end()
     for c in range(2):
-        stage_copy(c, wide_hbm, 0).wait()
+        stage_copy(c).wait()
 
 
 def mlp_back(own, weights, scales, up_raw, gate_raw, middle_rows, d_middle, start_unit, branch, rates, size, steps, collective_id):
@@ -853,11 +843,10 @@
             jax.ShapeDtypeStruct((own.shape[0], D), f32),
             jax.ShapeDtypeStruct((1, D), f32),
             jax.ShapeDtypeStruct((2, hidden), f32),
-            jax.ShapeDtypeStruct((2 * hidden, D), bf16),
-            jax.ShapeDtypeStruct((hidden, D), bf16),
+            jax.ShapeDtypeStruct((3 * hidden, D), bf16),
         ],
         in_specs=[VMEM_WHOLE, ANYWHERE, VMEM_WHOLE, ANYWHERE, ANYWHERE, VMEM_WHOLE] + [ANYWHERE] * 3 + [VMEM_WHOLE],
-        out_specs=[VMEM_WHOLE] * 4 + [ANYWHERE] * 2,
+        out_specs=[VMEM_WHOLE] * 4 + [ANYWHERE],
         scratch_shapes=[
             pltpu.VMEM((2, min(256, hidden), D), bf16),
             pltpu.SemaphoreType.DMA((2,)),
@@ -993,17 +982,19 @@
 
 
 def tail_sum_kernel(
-    devices, size, late_ref, early_ref, rates_ref, small_ref, hidden_ref, back_ref,
-    late_out, early_out, small_out, hidden_out, back_out,
+    devices, size, late_ref, home_ref, rates_ref, small_ref, hidden_ref, back_ref,
+    late_out, home_out, small_out, hidden_out, back_out,
     y_land, y_sum, z_land, rate_parts, rate_land, pack, small_land,
-    a_send, a_recv, b_send, b_recv, c_send, c_recv, d_send, d_recv, m_send, m_recv, s_send, s_recv, h_send, h_recv, g_send, g_recv
+    a_send, a_recv, b_send, b_recv, c_send, c_recv, d_send, d_recv, m_send, m_recv, s_send, s_recv, h_send, h_recv, g_send, g_recv, e_send, e_recv, f_send, f_recv, local_sem
 ):
     dp, me = lax.axis_index("dp"), lax.axis_index("mp")
     lines, columns, cuts, rows = tail_plan(devices, late_ref.shape[0])
     a, b = dp // columns, lax.rem(dp, columns)
     span = lines * rows
     narrow = rate_parts.shape[2]
-    chunks = [(early_ref, early_out, q) for q in range(cuts)] + [(late_ref, late_out, q) for q in range(cuts)]
+    chunks = [(late_ref, late_out, q) for q in range(cuts)]
+    pieces = e_send.shape[0]
+    height = home_ref.shape[0] // pieces
 
     def remote(source, target, send, receive, device):
         return pltpu.make_async_remote_copy(
@@ -1069,6 +1060,33 @@
         here = sum_of(c, column(j), line(i))
         return remote(here, here, d_send.at[c, i, j], d_recv.at[c, line(i), column(j)], (a * columns + column(j), me))
 
+    def home(col, row, p):
+        return home_out.at[row * columns + col, pl.ds(p * height, height), :]
+
+    def home_line(p, j):
+        return remote(
+            home_ref.at[pl.ds(p * height, height), :], home(b, a, p), e_send.at[p, j], e_recv.at[p, a], (line(j) * columns + b, me)
+        )
+
+    def home_line_got(p, j):
+        here = home(b, line(j), p)
+        return remote(here, here, e_send.at[p, j], e_recv.at[p, line(j)], (line(j) * columns + b, me))
+
+    def home_column(p, i, j):
+        here = home(b, line(i), p)
+        source = here if i else home_ref.at[pl.ds(p * height, height), :]
+        return remote(source, here, f_send.at[p, i, j], f_recv.at[p, line(i), b], (a * columns + column(j), me))
+
+    def home_column_got(p, i, j):
+        here = home(column(j), line(i), p)
+        return remote(here, here, f_send.at[p, i, j], f_recv.at[p, line(i), column(j)], (a * columns + column(j), me))
+
+    def home_pass(p):
+        for i in range(1, lines):
+            home_line_got(p, i).wait_recv()
+            for j in range(1, columns):
+                home_column(p, i, j).start()
+
     def rate_copy(j):
         device = lax.rem(me + j, size)
         return remote(rate_parts.at[device], rate_land.at[me], m_send.at[j - 1], m_recv.at[me], (dp, device))
@@ -1076,6 +1094,19 @@
     for c in range(len(chunks)):
         for j in range(1, columns):
             to_column(c, j).start()
+    for p in range(pieces):
+        for j in range(1, lines):
+            home_line(p, j).start()
+        for j in range(1, columns):
+            home_column(p, 0, j).start()
+    stay = [
+        pltpu.make_async_copy(source, target, local_sem.at[i])
+        for i, (source, target) in enumerate(
+            ((home_ref, home_out.at[dp]), (hidden_ref.at[me], hidden_out.at[me]), (back_ref.at[me], back_out.at[me]))
+        )
+    ]
+    for copy in stay:
+        copy.start()
     for d in range(size):
         rate_parts[d, 0:2, :] = rates_ref[:, d * narrow : (d + 1) * narrow]
     for j in range(1, size):
@@ -1098,8 +1129,6 @@
     for j in range(1, size):
         for copy in deal(j):
             copy.start()
-    hidden_out[me] = hidden_ref[me]
-    back_out[me] = back_ref[me]
 
     rates = rate_parts[me]
     for j in range(1, size):
@@ -1155,11 +1184,15 @@
                 back_column(c, i, j).start()
 
     count = len(chunks)
+    for c in range(count):
+        settle_column(c)
+    for p in range(pieces - 1):
+        home_pass(p)
     for step in range(count + 2):
-        if step < count:
-            settle_column(step)
         if 1 <= step <= count:
             settle_line(step - 1)
+        if step == 1:
+            home_pass(pieces - 1)
         if step >= 2:
             pass_on(step - 2)
 
@@ -1179,6 +1212,13 @@
             to_line(c, j).wait_send()
         for j in range(1, columns):
             to_column(c, j).wait_send()
+    for p in range(pieces):
+        for i in range(lines):
+            for j in range(1, columns):
+                home_column_got(p, i, j).wait_recv()
+                home_column(p, i, j).wait_send()
+        for j in range(1, lines):
+            home_line(p, j).wait_send()
 
     def finish(j, carry):
         small_copy(j).wait_send()
@@ -1191,19 +1231,23 @@
             copy.wait_recv()
         for copy in deal(j):
             copy.wait_send()
-
-
-def tail_sum(late, early, rates, small, hidden, back, devices, size, collective_id):
+    for copy in stay:
+        copy.wait()
+
+
+def tail_sum(late, home, rates, small, hidden, back, devices, size, collective_id):
     lines, columns, cuts, rows = tail_plan(devices, late.shape[0])
     narrow = D // size
-    chunks = 2 * cuts
+    chunks = cuts
+    pieces = next(p for p in (4, 3, 1) if home.shape[0] % (16 * p) == 0)
     dma = pltpu.SemaphoreType.DMA
     total = jax.ShapeDtypeStruct((late.shape[0] // rows, rows, D), bf16)
+    homes = jax.ShapeDtypeStruct((devices, *home.shape), bf16)
     return pl.pallas_call(
         functools.partial(tail_sum_kernel, devices, size),
-        out_shape=[total, total] + [jax.ShapeDtypeStruct(x.shape, x.dtype) for x in (small, hidden, back)],
+        out_shape=[total, homes] + [jax.ShapeDtypeStruct(x.shape, x.dtype) for x in (small, hidden, back)],
         in_specs=[VMEM_WHOLE] * 6,
-        out_specs=[VMEM_WHOLE] * 5,
+        out_specs=[VMEM_WHOLE, ANYWHERE, VMEM_WHOLE, ANYWHERE, ANYWHERE],
         scratch_shapes=[
             pltpu.VMEM((chunks, columns, lines * rows, D), bf16),
             pltpu.VMEM((chunks, lines * rows, D), bf16),
@@ -1220,15 +1264,18 @@
             dma((devices - 1,)), dma((devices,)),
             dma((size - 1,)), dma((size,)),
             dma((size - 1,)), dma((size,)),
+            dma((pieces, lines)), dma((pieces, lines)),
+            dma((pieces, lines, columns)), dma((pieces, lines, columns)),
+            dma((3,)),
         ],
         compiler_params=remote_params(collective_id),
         cost_estimate=pl.CostEstimate(flops=0, bytes_accessed=late.shape[0] * D * 16, transcendentals=0),
         name="tail_sum",
-    )(late, early, rates, small, hidden, back)
+    )(late, home, rates, small, hidden, back)
 
 
 def optimizer_kernel(
-    counts, index_ref, attn_ref, wide_ref, down_ref, m_ref, f_ref, s_ref, mo_ref, fo_ref, so_ref, go_ref
+    counts, index_ref, attn_ref, mlp_ref, m_ref, f_ref, s_ref, mo_ref, fo_ref, so_ref, go_ref
 ):
     group = m_ref.shape[0]
     for j in range(group):
@@ -1242,8 +1289,7 @@
 
         for ref, first, last in (
             (attn_ref, 0, counts[0]),
-            (wide_ref, counts[0], counts[0] + counts[1]),
-            (down_ref, counts[0] + counts[1], sum(counts)),
+            (mlp_ref, counts[0], sum(counts)),
         ):
 
             @pl.when(jnp.logical_and(live == 1, jnp.logical_and(block >= first, block < last)))
@@ -1258,17 +1304,17 @@
                 mo_ref[j] = stepped * lax.rsqrt(jnp.sum(stepped * stepped, axis=-1, keepdims=True) + EPSILON)
 
 
-def optimizer(index, attn_grads, wide_grads, down_grads, masters, firsts, seconds):
+def optimizer(index, attn_grads, mlp_grads, masters, firsts, seconds):
     slots, height, _ = masters.shape
     group = math.gcd(slots, 4)
-    grads = [g.reshape(-1, height, D) for g in (attn_grads, wide_grads, down_grads)]
+    grads = [g.reshape(-1, height, D) for g in (attn_grads, mlp_grads)]
     block = pl.BlockSpec((group, height, D), lambda i, ref: (i, 0, 0))
     return pl.pallas_call(
         functools.partial(optimizer_kernel, tuple(g.shape[0] for g in grads)),
         grid_spec=pltpu.PrefetchScalarGridSpec(
             num_scalar_prefetch=1,
             grid=(slots // group,),
-            in_specs=[pl.BlockSpec(memory_space=pltpu.VMEM)] * 3 + [block] * 3,
+            in_specs=[pl.BlockSpec(memory_space=pltpu.VMEM)] * 2 + [block] * 3,
             out_specs=[block] * 4,
         ),
         out_shape=[jax.ShapeDtypeStruct(masters.shape, f32)] * 4,
@@ -1686,12 +1732,12 @@
     out_rows, middle_rows, up_raw, gate_raw, d_mlp, d_middle, g_rate_mlp = mlp(
         middle_low, weights, hidden_gains, middle, cot_all, gains, size, STEPS, 2
     )
-    d_attn, d_start, g_rate_attn, g_scales, g_wide, g_down = mlp_back(
+    d_attn, d_start, g_rate_attn, g_scales, g_mlp = mlp_back(
         d_mlp, weights, hidden_gains, up_raw, gate_raw, middle_rows, d_middle, start_unit, attn_branch, gains,
         size, MLP_STEPS, 3,
     )
-    d_attn, g_wide = lax.optimization_barrier((d_attn, g_wide))
-    wide_grads = lax.psum(g_wide.reshape(-1, block_rows, D), "dp")
+    d_attn, g_mlp = lax.optimization_barrier((d_attn, g_mlp))
+    mlp_home = lax.psum_scatter(g_mlp, "dp", scatter_dimension=0, tiled=True)
     d_attended, attn_grad_rows = gather_project(d_attn, weights, narrow, 3 * narrow, size, STEPS, 4, "attention_gather")
     d_queries, d_keys, d_values = attend_back(queries, keys, values, mixed, d_attended)
     grads_qkv, g_qk = project_back(
@@ -1702,7 +1748,7 @@
     )
     small = jnp.zeros((8, hidden_local), f32)
     small = small.at[0:1, :narrow].set(g_qk).at[1:3, :].set(g_scales)
-    attn_grads, down_grads, small, hidden_out, grad_in = tail_sum(g_attn, g_down, jnp.concatenate([g_rate_attn, g_rate_mlp], axis=0), small, out_rows, grad_pieces, n_dp, size, 7)
+    attn_grads, mlp_grads, small, hidden_out, grad_in = tail_sum(g_attn, mlp_home, jnp.concatenate([g_rate_attn, g_rate_mlp], axis=0), small, out_rows, grad_pieces, n_dp, size, 7)
     hidden_out = hidden_out.reshape(tokens, narrow)
     grad_in = grad_in.reshape(tokens, narrow).astype(f32)
     width_total = jnp.concatenate([small[0:1, :narrow], small[3:5, :narrow]], axis=0)
@@ -1710,7 +1756,7 @@
     index = jnp.stack([slot_block, in_use.astype(jnp.int32)], axis=1)
     masters_new, firsts_new, seconds_new, weight_grads = [
         part[None]
-        for part in optimizer(index, attn_grads, wide_grads, down_grads, masters[0], firsts[0], seconds[0])
+        for part in optimizer(index, attn_grads, mlp_grads, masters[0], firsts[0], seconds[0])
     ]
     width_new, width_first_new, width_second_new = adam_update(
         width_gains, width_total, width_first, width_second, 0.0, GAIN_RATE

time: 679 us -> 669 us (0.985)
  Pallas kernels: 643 us -> 635 us
    pallas_call x1, Pallas kernels: 147 us -> 138 us  [tail_sum(): pl.pallas_call(functools.partial(tail_sum_kernel, devices, size), out_sha...]
  transfers between devices with their start and end apart: 1 -> 1, of which waited for: 0 -> 0; matrix products, arithmetic and copies ran while one was open for 2% -> 1% of each run, Pallas kernels for 39% -> 18%
where the time goes in v3:
time: 669 us; the launch traced here: 668 us
  Pallas kernels  635 us (95%)
  between operations  14.3 us (2%)
  other arithmetic  11.3 us (2%)
  local copies, waits for them, and re-layouts  7.92 us (1%)
    pallas_call x1, Pallas kernels, spread(): pl.pallas_call(functools.partial(spread_kernel, devices, size, slots, hei...  170 us
    pallas_call x1, Pallas kernels, tail_sum(): pl.pallas_call(functools.partial(tail_sum_kernel, devices, size), out_sha...  138 us
    pallas_call x1, Pallas kernels, mlp_back(): pl.pallas_call(functools.partial(mlp_back_kernel, size, steps), out_shape...  64.2 us
    pallas_call x1, Pallas kernels, mlp(): pl.pallas_call(functools.partial(mlp_kernel, size, steps), out_shape=[jax...  54.6 us
    pallas_call x1, Pallas kernels, attend_back(): pl.pallas_call(functools.partial(attend_back_kernel, block), grid=(heads...  42 us
    pallas_call x1, Pallas kernels, start_sum(): pl.pallas_call(functools.partial(start_sum_kernel, size, steps), out_shap...  35.8 us
    pallas_call x1, Pallas kernels, attention_sum(): pl.pallas_call(functools.partial(attention_sum_kernel, size, steps, first...  31.5 us
    pallas_call x1, Pallas kernels, gather_project(): pl.pallas_call(functools.partial(gather_project_kernel, size, steps, firs...  30.1 us
  transfers between devices with their start and end apart: 1, of which 0 were waited for; matrix products, arithmetic and copies ran while one was open for 1% of the time, Pallas kernels for 18%

profile of v3, /device:TPU:8, one launch (start us, length us, event | category | flops | bytes accessed | tf_op | source)
XLA Modules:
  0.0 668.1 jit_solution(15885390946984415885)
XLA Ops:
  7.2 0.0 reduce-scatter.2.cloned.1.call-start
  7.2 3.9 convert_element_type.29
  11.1 0.2 convert_reduce_fusion
  11.3 0.0 copy-start.10
  11.3 1.2 convert_reduce_fusion.1
  12.4 170.2 %spread.1 = (bf16[8,1024,1024]{2,1,0:T(8,128)(2,1)}, bf16[4,2048,256]{2,1,0:T(8,128)(2,1)}, bf16[4,512,256]{2,1,0:T(8,128)(2,1)}, f32[3,1024]{1,0:T(4,128)}, f32...) custom-call(bf16[1024,1024]{1,0:T(8,128)(2,1)} %bitcast.25, ...), custom_call_target="tpu_custom_call" | custom-call | bytes 33554432 | tf_op jit(solution)/shard_map/spread/pallas_call | solution.py:1640
  182.7 8.6 %collect.1 = bf16[128,32,1024]{2,1,0:T(8,128)(2,1)} custom-call(s32[128]{0:T(128)} %get-tuple-element.150.places_ref, bf16[256,32,1024]{2,1,0:T(8,128)(2,1)} %bitcast.23), custom_call_target="tpu_custom_call" | custom-call | bytes 16777216 | tf_op jit(solution)/shard_map/collect/pallas_call | solution.py:1345
  191.3 12.1 %project.1 = (bf16[2048,1024]{1,0:T(8,128)(2,1)}, bf16[4,2048,128]{2,1,0:T(8,128)(2,1)}, bf16[4,2048,128]{2,1,0:T(8,128)(2,1)}, bf16[4,2048,128]{2,1,0:T(8,128)(...) custom-call(bf16[4,2048,256]{2,1,0:T(8,128)(2,1)} %get-tuple-element.89.x_ref, bf16[4096,1024]{1,0:T(8,128)(2,1)} %bitcast.17, ...), custom_call_target="tpu_custom_call" | custom-call | flops 3221225472 | bytes 16777216 | tf_op jit(solution)/shard_map/project/pallas_call | solution.py:139
  203.4 19.7 %attend.1 = (bf16[2048,256]{1,0:T(8,128)(2,1)}, f32[4,2048,128]{2,1,0:T(8,128)}) custom-call(bf16[4,2048,128]{2,1,0:T(8,128)(2,1)} %get-tuple-element.93.q_ref, bf16[4,2048,128]{2,1,0:T(8,128)(2,1)} %get-tuple-element.94.k_ref, bf16[4,2048,128]{2,1,0:T(8,128)(2,1)} %get-tuple-element.95.v_ref), custom_call_target="tpu_custom_call" | custom-call | flops 8589934592 | bytes 10485760 | tf_op jit(solution)/shard_map/attend/pallas_call | solution.py:187
  223.0 31.5 %attention_sum.1 = (f32[512,1024]{1,0:T(8,128)}, f32[512,1024]{1,0:T(8,128)}, bf16[512,1024]{1,0:T(8,128)(2,1)}) custom-call(bf16[2048,256]{1,0:T(8,128)(2,1)} %get-tuple-element.97.rows_ref.attended_hbm, bf16[4096,1024]{1,0:T(8,128)(2,1)} %bitcast.18, f32[512,1024]{1,0:T(8,128)} %get-tuple-element.98.start_ref.start_hbm.unit_ref, ...), custom_call_target="tpu_custom_call" | custom-call | flops 1073741824 | bytes 16777216 | tf_op jit(solution)/shard_map/attention_sum/pallas_call | solution.py:576
  254.5 54.6 %mlp.1 = (f32[4,512,256]{2,1,0:T(8,128)}, bf16[4,512,1024]{2,1,0:T(8,128)(2,1)}, f32[2048,1024]{1,0:T(8,128)}, f32[2048,1024]{1,0:T(8,128)}, bf16[512,1024]{1,0:...) custom-call(bf16[512,1024]{1,0:T(8,128)(2,1)} %get-tuple-element.100.own_ref, bf16[4096,1024]{1,0:T(8,128)(2,1)} %bitcast.19, ...), custom_call_target="tpu_custom_call" | custom-call | flops 12884901888 | bytes 25165824 | tf_op jit(solution)/shard_map/mlp/pallas_call | solution.py:656
  309.1 64.2 %mlp_back.1 = (bf16[512,1024]{1,0:T(8,128)(2,1)}, f32[512,1024]{1,0:T(8,128)}, f32[1,1024]{1,0:T(1,128)}, f32[2,1024]{1,0:T(2,128)}, bf16[3072,1024]{1,0:T(8,128)(2,1)}) custom-call(bf16[512,1024]{1,0:T(8,128)(2,1)} %get-tuple-element.103.own_ref, bf16[4096,1024]{1,0:T(8,128)(2,1)} %bitcast.20, f32[2,1024]{1,0:T(2,128)} %scale_ref.3, ...), custom_call_target="tpu_custom_call" | custom-call | flops 12884901888 | bytes 50331648 | tf_op jit(solution)/shard_map/mlp_back/pallas_call | solution.py:839
  373.3 0.0 reduce-scatter.2.cloned.1.call-update
  373.4 0.7 compare_convert_fusion
  374.0 0.1 select_reduce_fusion
  374.2 0.7 copy.28.index_ref
  374.9 30.1 %attention_gather.1 = (bf16[2048,256]{1,0:T(8,128)(2,1)}, bf16[4,512,1024]{2,1,0:T(8,128)(2,1)}) custom-call(bf16[512,1024]{1,0:T(8,128)(2,1)} %get-tuple-element.111.own_ref, bf16[4096,1024]{1,0:T(8,128)(2,1)} %bitcast.21), custom_call_target="tpu_custom_call" | custom-call | flops 1073741824 | bytes 8388608 | tf_op jit(solution)/shard_map/attention_gather/pallas_call | solution.py:892
  405.0 42.0 %attend_back.1 = (f32[2048,256]{1,0:T(8,128)}, f32[2048,256]{1,0:T(8,128)}, f32[2048,256]{1,0:T(8,128)}) custom-call(bf16[4,2048,128]{2,1,0:T(8,128)(2,1)} %get-tuple-element.93.q_ref, bf16[4,2048,128]{2,1,0:T(8,128)(2,1)} %get-tuple-element.94.k_ref, bf16[4,2048,128]{2,1,0:T(8,128)(2,1)} %get-tuple-element.95.v_ref, ...), custom_call_target="tpu_custom_call" | custom-call | flops 21474836480 | bytes 20971520 | tf_op jit(solution)/shard_map/attend_back/pallas_call | solution.py:274
  447.0 10.8 %project_back.1 = (bf16[2048,768]{1,0:T(8,128)(2,1)}, f32[1,256]{1,0:T(1,128)}) custom-call(f32[2048,256]{1,0:T(8,128)} %get-tuple-element.113.dq_ref, f32[2048,256]{1,0:T(8,128)} %get-tuple-element.114.dk_ref, f32[2048,256]{1,0:T(8,128)} %get-tuple-element.115.dv_ref, f32[2048,256]{1,0:T(8,128)} %get-tuple-element.116.qr_ref, ...), custom_call_target="tpu_custom_call" | custom-call | flops 31457280 | bytes 13631488 | tf_op jit(solution)/shard_map/project_back/pallas_call | solution.py:323
  457.8 1.3 scatter.6
  459.1 1.4 scatter.9.small_ref
  460.5 0.6 pad_maximum_fusion.rates_ref
  461.1 35.8 %start_sum.1 = (bf16[4,512,256]{2,1,0:T(8,128)(2,1)}, bf16[1024,1024]{1,0:T(8,128)(2,1)}) custom-call(bf16[2048,768]{1,0:T(8,128)(2,1)} %get-tuple-element.118.rows_ref, bf16[4096,1024]{1,0:T(8,128)(2,1)} %bitcast.22, f32[512,1024]{1,0:T(8,128)} %get-tuple-element.119.base_ref, f32[512,1024]{1,0:T(8,128)} %get-tuple-element.98.start_ref.start_hbm.unit_ref, ...), custom_call_target="tpu_custom_call" | custom-call | flops 3221225472 | bytes 16777216 | tf_op jit(solution)/shard_map/start_sum/pallas_call | solution.py:955
  496.9 0.0 reduce-scatter.2.cloned.1.call-done.home_ref
  496.9 137.7 %tail_sum.1 = (bf16[16,64,1024]{2,1,0:T(8,128)(2,1)}, bf16[8,384,1024]{2,1,0:T(8,128)(2,1)}, f32[8,1024]{1,0:T(8,128)}, f32[4,512,256]{2,1,0:T(8,128)}, bf16[4,512,256]{2,1,0:T(8,128)(2,1)}) custom-call(bf16[1024,1024]{1,0:T(8,128)(2,1)} %get-tuple-element.123.late_ref, bf16[384,1024]{1,0:T(8,128)(2,1)} %reduce-scatter.2.cloned.1.call-done.home_ref, ...), custom_call_target="tpu_custom_call" | custom-call | bytes 16777216 | tf_op jit(solution)/shard_map/tail_sum/pallas_call | solution.py:1246
  634.7 0.7 slice.47
  635.4 0.7 slice.46
  636.1 2.7 bitcast_convert_fusion
  638.8 1.4 multiply_subtract_fusion
  640.2 0.6 multiply_subtract_fusion.1
  640.9 17.3 %optimizer.1 = (f32[32,32,1024]{2,1,0:T(8,128)}, f32[32,32,1024]{2,1,0:T(8,128)}, f32[32,32,1024]{2,1,0:T(8,128)}, f32[32,32,1024]{2,1,0:T(8,128)}) custom-call(s32[32,2]{1,0:T(8,128)} %copy.28.index_ref, bf16[32,32,1024]{2,1,0:T(8,128)(2,1)} %bitcast.29, bf16[96,32,1024]{2,1,0:T(8,128)(2,1)} %bitcast.26, f32[32,32,1024]{2,1,0:T(8,128)} %bitcast.24, ...), custom_call_target="tpu_custom_call" | custom-call | flops 20971520 | bytes 31457280 | tf_op jit(solution)/shard_map/optimizer/pallas_call | solution.py:1312
  658.2 3.0 copy.31
  (26 shorter events, 0.1 us)
Async XLA Ops:
  7.2 489.7 %reduce-scatter.2.cloned.1.call-start = ((), (), s32[]{:S(2)}) async-start(), calls=%async_computation.1 | async-start | bytes 7077888 | tf_op jit(solution)/shard_map/reduce_scatter | solution.py:1740
  7.2 3.9 copy-start.9
  11.3 1.2 copy-start.10
  373.3 0.7 copy-start.11
  373.3 0.7 copy-start.12
  447.0 12.1 %copy-start.1 = (f32[2,1024]{1,0:T(2,128)S(1)}, f32[2,1024]{1,0:T(2,128)}, u32[]{:S(2)}) copy-start(f32[2,1024]{1,0:T(2,128)} %get-tuple-element.128) | copy-start | bytes 24580
  447.0 13.5 %copy-start.5 = (f32[1,1024]{1,0:T(1,128)S(1)}, f32[1,1024]{1,0:T(1,128)}, u32[]{:S(2)}) copy-start(f32[1,1024]{1,0:T(1,128)} %get-tuple-element.126) | copy-start | bytes 12292
  447.0 13.5 %copy-start.6 = (f32[1,1024]{1,0:T(1,128)S(1)}, f32[1,1024]{1,0:T(1,128)}, u32[]{:S(2)}) copy-start(f32[1,1024]{1,0:T(1,128)} %get-tuple-element.125) | copy-start | bytes 12292
  634.6 4.2 copy-start.2
  634.6 4.2 copy-start.3
  634.6 4.2 copy-start.4
  634.7 5.6 copy-start
  634.7 5.6 copy-start.7
  634.7 5.6 copy-start.8
Sparse Core Ops, SparseCore 0:
  373.5 117.2 reduce-scatter.1

commit v4 on v3

--- a/solution.py
+++ b/solution.py
@@ -154,34 +154,38 @@
 def attend_kernel(block, q_ref, k_ref, v_ref, att_ref, o_ref):
     i = pl.program_id(1)
     lane = lax.broadcasted_iota(jnp.int32, (block, LANES), 1)
-    queries = [q_ref[h] for h in range(2)]
-
-    def step(j, sums, diagonal):
-        rows = pl.ds(pl.multiple_of(j * block, block), block)
-        new = []
-        for h in range(2):
-            weight = jnp.exp(nt(queries[h], k_ref[h, rows, :]))
-            if diagonal:
-                row = lax.broadcasted_iota(jnp.int32, weight.shape, 0)
-                column = lax.broadcasted_iota(jnp.int32, weight.shape, 1)
-                weight = jnp.where(row >= column, weight, 0.0)
-            new.append(sums[h] + nn(weight.astype(bf16), v_ref[h, rows, :]))
-        return tuple(new)
-
-    zero = jnp.zeros((block, LANES), f32)
-    sums = lax.fori_loop(0, i, lambda j, s: step(j, s, False), (zero, zero))
-    sums = step(i, sums, True)
-    mixed = []
-    for h in range(2):
-        total = pltpu.roll(sums[h], HD, 1)
-        o_ref[h] = jnp.where(lane < HD, sums[h] / total, jnp.log(sums[h]))
-        mixed.append(o_ref[h])
-    att_ref[...] = jnp.where(lane < HD, mixed[0], pltpu.roll(mixed[1], HD, 1)).astype(bf16)
+    width = min(256, block)
+
+    def head(h, carry):
+        queries = q_ref[h]
+
+        def step(j, total):
+            rows = pl.ds(pl.multiple_of(j * block, block), block)
+            return total + nn(jnp.exp(nt(queries, k_ref[h, rows, :])).astype(bf16), v_ref[h, rows, :])
+
+        total = jnp.zeros((block, LANES), f32)
+        if block < k_ref.shape[1]:
+            total = lax.fori_loop(0, i, step, total)
+        parts = [total[first : first + width] for first in range(0, block, width)]
+        for c in range(len(parts)):
+            rows = pl.ds(pl.multiple_of(i * block + c * width, width), width)
+            weight = jnp.exp(nt(queries[c * width :], k_ref[h, rows, :]))
+            row = lax.broadcasted_iota(jnp.int32, weight.shape, 0)
+            column = lax.broadcasted_iota(jnp.int32, weight.shape, 1)
+            term = nn(jnp.where(row >= column, weight, 0.0).astype(bf16), v_ref[h, rows, :])
+            for r in range(c, len(parts)):
+                parts[r] = parts[r] + term[(r - c) * width : (r - c + 1) * width]
+        total = jnp.concatenate(parts, axis=0)
+        o_ref[h] = jnp.where(lane < HD, total / pltpu.roll(total, HD, 1), jnp.log(total))
+        return carry
+
+    lax.fori_loop(0, 2, head, 0)
+    att_ref[...] = jnp.where(lane < HD, o_ref[0], pltpu.roll(o_ref[1], HD, 1)).astype(bf16)
 
 
 def attend(queries, keys, values):
     heads, tokens, _ = queries.shape
-    block = min(512, tokens)
+    block = min(2048, tokens)
     part = pl.BlockSpec((2, block, LANES), lambda p, i: (p, i, 0))
     whole = pl.BlockSpec((2, tokens, LANES), lambda p, i: (p, 0, 0))
     return pl.pallas_call(
@@ -193,6 +197,7 @@
             jax.ShapeDtypeStruct((tokens, heads * HD), bf16),
             jax.ShapeDtypeStruct((heads, tokens, LANES), f32),
         ],
+        compiler_params=pltpu.CompilerParams(vmem_limit_bytes=56 << 20),
         cost_estimate=pl.CostEstimate(
             flops=heads * tokens * tokens * LANES * 4,
             bytes_accessed=heads * tokens * LANES * 10,
@@ -587,7 +592,7 @@
 
 def mlp_kernel(
     size, steps, own_ref, w_hbm, scale_ref, middle_ref, cot_ref, rates_ref,
-    out_ref, rows_ref, ur_hbm, gr_hbm, d_mlp_ref, d_middle_ref, g_rate_ref, branch_ref,
+    out_ref, rows_hbm, ur_hbm, gr_hbm, d_mlp_ref, d_middle_ref, g_rate_ref, branch_ref, rows_ref, r_sem,
     up_ref, gate_ref, down_ref, w_sem, u_buf, g_buf, b_sem, *scratch
 ):
     tokens = own_ref.shape[0] * size
@@ -643,10 +648,13 @@
     group.run(
         compute, gather=(own_ref, rows_ref, scratch[0], scratch[1]), settle=(branch_ref, *scratch[2:]), ready=copies, after=after
     )
+    keep = pltpu.make_async_copy(rows_ref, rows_hbm, r_sem.at[0])
+    keep.start()
     for i in range(2):
         for c in save(i, 0, 0):
             c.wait()
     group.end()
+    keep.wait()
 
 
 def mlp(own, weights, scales, middle, cot_all, rates, size, steps, collective_id):
@@ -665,8 +673,12 @@
             jax.ShapeDtypeStruct((1, D), f32),
         ],
         in_specs=[VMEM_WHOLE, ANYWHERE] + [VMEM_WHOLE] * 4,
-        out_specs=[VMEM_WHOLE, VMEM_WHOLE, ANYWHERE, ANYWHERE] + [VMEM_WHOLE] * 3,
-        scratch_shapes=[pltpu.VMEM((own.shape[0], D), f32)]
+        out_specs=[VMEM_WHOLE, ANYWHERE, ANYWHERE, ANYWHERE] + [VMEM_WHOLE] * 3,
+        scratch_shapes=[
+            pltpu.VMEM((own.shape[0], D), f32),
+            pltpu.VMEM((size, own.shape[0], D), bf16),
+            pltpu.SemaphoreType.DMA((1,)),
+        ]
         + weight_scratch(hidden, 3)
         + [
             pltpu.VMEM((2, rows, hidden), f32),
@@ -982,7 +994,7 @@
 
 
 def tail_sum_kernel(
-    devices, size, late_ref, home_ref, rates_ref, small_ref, hidden_ref, back_ref,
+    devices, size, late_ref, home_ref, rate_attn_ref, rate_mlp_ref, gain_ref, scale_ref, hidden_ref, back_ref,
     late_out, home_out, small_out, hidden_out, back_out,
     y_land, y_sum, z_land, rate_parts, rate_land, pack, small_land,
     a_send, a_recv, b_send, b_recv, c_send, c_recv, d_send, d_recv, m_send, m_recv, s_send, s_recv, h_send, h_recv, g_send, g_recv, e_send, e_recv, f_send, f_recv, local_sem
@@ -1108,7 +1120,8 @@
     for copy in stay:
         copy.start()
     for d in range(size):
-        rate_parts[d, 0:2, :] = rates_ref[:, d * narrow : (d + 1) * narrow]
+        rate_parts[d, 0:1, :] = rate_attn_ref[:, d * narrow : (d + 1) * narrow]
+        rate_parts[d, 1:2, :] = rate_mlp_ref[:, d * narrow : (d + 1) * narrow]
     for j in range(1, size):
         rate_copy(j).start()
 
@@ -1135,7 +1148,9 @@
         source = lax.rem(me + j, size)
         remote(rate_land.at[source], rate_land.at[source], m_send.at[j - 1], m_recv.at[source], (dp, source)).wait_recv()
         rates = rates + rate_land[source]
-    pack[...] = small_ref[...]
+    pack[...] = jnp.zeros_like(pack)
+    pack[0:1, :narrow] = gain_ref[...]
+    pack[1:3, :] = scale_ref[...]
     pack[3:5, :narrow] = rates[0:2, :]
 
     def small_copy(j):
@@ -1235,9 +1250,10 @@
         copy.wait()
 
 
-def tail_sum(late, home, rates, small, hidden, back, devices, size, collective_id):
+def tail_sum(late, home, rate_attn, rate_mlp, gain, scales, hidden, back, devices, size, collective_id):
     lines, columns, cuts, rows = tail_plan(devices, late.shape[0])
     narrow = D // size
+    small = jax.ShapeDtypeStruct((8, scales.shape[1]), f32)
     chunks = cuts
     pieces = next(p for p in (4, 3, 1) if home.shape[0] % (16 * p) == 0)
     dma = pltpu.SemaphoreType.DMA
@@ -1246,7 +1262,7 @@
     return pl.pallas_call(
         functools.partial(tail_sum_kernel, devices, size),
         out_shape=[total, homes] + [jax.ShapeDtypeStruct(x.shape, x.dtype) for x in (small, hidden, back)],
-        in_specs=[VMEM_WHOLE] * 6,
+        in_specs=[VMEM_WHOLE] * 8,
         out_specs=[VMEM_WHOLE, ANYWHERE, VMEM_WHOLE, ANYWHERE, ANYWHERE],
         scratch_shapes=[
             pltpu.VMEM((chunks, columns, lines * rows, D), bf16),
@@ -1271,13 +1287,11 @@
         compiler_params=remote_params(collective_id),
         cost_estimate=pl.CostEstimate(flops=0, bytes_accessed=late.shape[0] * D * 16, transcendentals=0),
         name="tail_sum",
-    )(late, home, rates, small, hidden, back)
-
-
-def optimizer_kernel(
-    counts, index_ref, attn_ref, mlp_ref, m_ref, f_ref, s_ref, mo_ref, fo_ref, so_ref, go_ref
-):
-    group = m_ref.shape[0]
+    )(late, home, rate_attn, rate_mlp, gain, scales, hidden, back)
+
+
+def optimizer_kernel(counts, group, index_ref, *refs):
+    grads, (m_ref, f_ref, s_ref, mo_ref, fo_ref, so_ref, go_ref) = refs[: 2 * group], refs[2 * group :]
     for j in range(group):
         slot = pl.program_id(0) * group + j
         block, live = index_ref[slot, 0], index_ref[slot, 1]
@@ -1287,46 +1301,56 @@
             for ref in (mo_ref, fo_ref, so_ref, go_ref):
                 ref[j] = jnp.zeros_like(m_ref[j])
 
-        for ref, first, last in (
-            (attn_ref, 0, counts[0]),
-            (mlp_ref, counts[0], sum(counts)),
-        ):
-
-            @pl.when(jnp.logical_and(live == 1, jnp.logical_and(block >= first, block < last)))
-            def _():
-                gradient = ref[block - first].astype(f32)
-                stepped, first_new, second_new = adam_update(
-                    m_ref[j], gradient, f_ref[j], s_ref[j], WEIGHT_DECAY, LEARN_RATE
-                )
-                go_ref[j] = gradient
-                fo_ref[j] = first_new
-                so_ref[j] = second_new
-                mo_ref[j] = stepped * lax.rsqrt(jnp.sum(stepped * stepped, axis=-1, keepdims=True) + EPSILON)
+        @pl.when(live == 1)
+        def _():
+            gradient = jnp.where(block < counts[0], grads[2 * j][0].astype(f32), grads[2 * j + 1][0].astype(f32))
+            stepped, first_new, second_new = adam_update(
+                m_ref[j], gradient, f_ref[j], s_ref[j], WEIGHT_DECAY, LEARN_RATE
+            )
+            go_ref[j] = gradient
+            fo_ref[j] = first_new
+            so_ref[j] = second_new
+            mo_ref[j] = stepped * lax.rsqrt(jnp.sum(stepped * stepped, axis=-1, keepdims=True) + EPSILON)
 
 
 def optimizer(index, attn_grads, mlp_grads, masters, firsts, seconds):
     slots, height, _ = masters.shape
     group = math.gcd(slots, 4)
     grads = [g.reshape(-1, height, D) for g in (attn_grads, mlp_grads)]
+    counts = tuple(g.shape[0] for g in grads)
     block = pl.BlockSpec((group, height, D), lambda i, ref: (i, 0, 0))
+
+    def attn_block(j):
+        return pl.BlockSpec(
+            (1, height, D), lambda i, ref: (jnp.minimum(ref[i * group + j, 0], counts[0] - 1), 0, 0)
+        )
+
+    def mlp_block(j):
+        return pl.BlockSpec(
+            (1, height, D), lambda i, ref: (jnp.maximum(ref[i * group + j, 0] - counts[0], 0), 0, 0)
+        )
+
     return pl.pallas_call(
-        functools.partial(optimizer_kernel, tuple(g.shape[0] for g in grads)),
+        functools.partial(optimizer_kernel, counts, group),
         grid_spec=pltpu.PrefetchScalarGridSpec(
             num_scalar_prefetch=1,
             grid=(slots // group,),
-            in_specs=[pl.BlockSpec(memory_space=pltpu.VMEM)] * 2 + [block] * 3,
+            in_specs=[spec(j) for j in range(group) for spec in (attn_block, mlp_block)] + [block] * 3,
             out_specs=[block] * 4,
         ),
         out_shape=[jax.ShapeDtypeStruct(masters.shape, f32)] * 4,
         compiler_params=pltpu.CompilerParams(vmem_limit_bytes=GRANT),
         cost_estimate=pl.CostEstimate(flops=20 * masters.size, bytes_accessed=30 * masters.size, transcendentals=0),
         name="optimizer",
-    )(index, *grads, masters, firsts, seconds)
-
-
-def collect_kernel(count, places_ref, slots_hbm, out_ref, sems):
+    )(index, *(grads * group), masters, firsts, seconds)
+
+
+def collect_kernel(count, places_ref, slots_hbm, out_hbm, held, sems, out_sems):
+    chunks = out_sems.shape[0]
+    each = count // chunks
+
     def copy(b):
-        return pltpu.make_async_copy(slots_hbm.at[places_ref[b]], out_ref.at[b], sems.at[b])
+        return pltpu.make_async_copy(slots_hbm.at[places_ref[b]], held.at[b], sems.at[b])
 
     def start(b, carry):
         copy(b).start()
@@ -1336,8 +1360,16 @@
         copy(b).wait()
         return carry
 
+    def out(c):
+        here = pl.ds(c * each, each)
+        return pltpu.make_async_copy(held.at[here], out_hbm.at[here], out_sems.at[c])
+
     lax.fori_loop(0, count, start, 0)
-    lax.fori_loop(0, count, wait, 0)
+    for c in range(chunks):
+        lax.fori_loop(c * each, (c + 1) * each, wait, 0)
+        out(c).start()
+    for c in range(chunks):
+        out(c).wait()
 
 
 def collect(places, slots):
@@ -1348,8 +1380,12 @@
             num_scalar_prefetch=1,
             grid=(1,),
             in_specs=[pl.BlockSpec(memory_space=pl.ANY)],
-            out_specs=pl.BlockSpec(memory_space=pltpu.VMEM),
-            scratch_shapes=[pltpu.SemaphoreType.DMA((count,))],
+            out_specs=pl.BlockSpec(memory_space=pl.ANY),
+            scratch_shapes=[
+                pltpu.VMEM((count, *shape), bf16),
+                pltpu.SemaphoreType.DMA((count,)),
+                pltpu.SemaphoreType.DMA((math.gcd(count, 8),)),
+            ],
         ),
         out_shape=jax.ShapeDtypeStruct((count, *shape), bf16),
         compiler_params=pltpu.CompilerParams(vmem_limit_bytes=GRANT),
@@ -1746,9 +1782,7 @@
     grad_pieces, g_attn = start_sum(
         grads_qkv, weights, d_start, start_unit, start_inv, operand, attended, attn_grad_rows, size, STEPS, 5
     )
-    small = jnp.zeros((8, hidden_local), f32)
-    small = small.at[0:1, :narrow].set(g_qk).at[1:3, :].set(g_scales)
-    attn_grads, mlp_grads, small, hidden_out, grad_in = tail_sum(g_attn, mlp_home, jnp.concatenate([g_rate_attn, g_rate_mlp], axis=0), small, out_rows, grad_pieces, n_dp, size, 7)
+    attn_grads, mlp_grads, small, hidden_out, grad_in = tail_sum(g_attn, mlp_home, g_rate_attn, g_rate_mlp, g_qk, g_scales, out_rows, grad_pieces, n_dp, size, 7)
     hidden_out = hidden_out.reshape(tokens, narrow)
     grad_in = grad_in.reshape(tokens, narrow).astype(f32)
     width_total = jnp.concatenate([small[0:1, :narrow], small[3:5, :narrow]], axis=0)

time: 669 us -> 658 us (0.984)
  Pallas kernels: 635 us -> 626 us
  transfers between devices with their start and end apart: 1 -> 1, of which waited for: 0 -> 0; matrix products, arithmetic and copies ran while one was open for 1% -> 0% of each run, Pallas kernels for 18% -> 18%
where the time goes in v4:
time: 658 us; the launch traced here: 656 us
  Pallas kernels  626 us (95%)
  between operations  14.2 us (2%)
  other arithmetic  10.7 us (2%)
    pallas_call x1, Pallas kernels, spread(): pl.pallas_call(functools.partial(spread_kernel, devices, size, slots, hei...  170 us
    pallas_call x1, Pallas kernels, tail_sum(): pl.pallas_call(functools.partial(tail_sum_kernel, devices, size), out_sha...  138 us
    pallas_call x1, Pallas kernels, mlp_back(): pl.pallas_call(functools.partial(mlp_back_kernel, size, steps), out_shape...  64.2 us
    pallas_call x1, Pallas kernels, mlp(): pl.pallas_call(functools.partial(mlp_kernel, size, steps), out_shape=[jax...  53.4 us
    pallas_call x1, Pallas kernels, attend_back(): pl.pallas_call(functools.partial(attend_back_kernel, block), grid=(heads...  42.1 us
    pallas_call x1, Pallas kernels, start_sum(): pl.pallas_call(functools.partial(start_sum_kernel, size, steps), out_shap...  35.8 us
    pallas_call x1, Pallas kernels, attention_sum(): pl.pallas_call(functools.partial(attention_sum_kernel, size, steps, first...  31.5 us
    pallas_call x1, Pallas kernels, gather_project(): pl.pallas_call(functools.partial(gather_project_kernel, size, steps, firs...  30.1 us
  transfers between devices with their start and end apart: 1, of which 0 were waited for; matrix products, arithmetic and copies ran while one was open for 0% of the time, Pallas kernels for 18%

profile of v4, /device:TPU:8, one launch (start us, length us, event | category | flops | bytes accessed | tf_op | source)
XLA Modules:
  0.0 656.3 jit_solution(7078181343500952220)
XLA Ops:
  7.2 0.0 reduce-scatter.2.cloned.1.call-start
  7.2 3.9 convert_element_type.29
  11.1 0.2 convert_reduce_fusion
  11.3 0.0 copy-start.7
  11.3 1.2 convert_reduce_fusion.1
  12.4 170.2 %spread.1 = (bf16[8,1024,1024]{2,1,0:T(8,128)(2,1)}, bf16[4,2048,256]{2,1,0:T(8,128)(2,1)}, bf16[4,512,256]{2,1,0:T(8,128)(2,1)}, f32[3,1024]{1,0:T(4,128)}, f32...) custom-call(bf16[1024,1024]{1,0:T(8,128)(2,1)} %bitcast.33, ...), custom_call_target="tpu_custom_call" | custom-call | bytes 33554432 | tf_op jit(solution)/shard_map/spread/pallas_call | solution.py:1676
  182.6 8.4 %collect.1 = bf16[128,32,1024]{2,1,0:T(8,128)(2,1)} custom-call(s32[128]{0:T(128)} %get-tuple-element.126.places_ref, bf16[256,32,1024]{2,1,0:T(8,128)(2,1)} %bitcast.31), custom_call_target="tpu_custom_call" | custom-call | bytes 16777216 | tf_op jit(solution)/shard_map/collect/pallas_call | solution.py:1377
  191.0 12.1 %project.1 = (bf16[2048,1024]{1,0:T(8,128)(2,1)}, bf16[4,2048,128]{2,1,0:T(8,128)(2,1)}, bf16[4,2048,128]{2,1,0:T(8,128)(2,1)}, bf16[4,2048,128]{2,1,0:T(8,128)(...) custom-call(bf16[4,2048,256]{2,1,0:T(8,128)(2,1)} %get-tuple-element.65.x_ref, bf16[4096,1024]{1,0:T(8,128)(2,1)} %bitcast.17, ...), custom_call_target="tpu_custom_call" | custom-call | flops 3221225472 | bytes 16777216 | tf_op jit(solution)/shard_map/project/pallas_call | solution.py:139
  203.1 14.8 %attend.1 = (bf16[2048,256]{1,0:T(8,128)(2,1)}, f32[4,2048,128]{2,1,0:T(8,128)}) custom-call(bf16[4,2048,128]{2,1,0:T(8,128)(2,1)} %get-tuple-element.69.q_ref, bf16[4,2048,128]{2,1,0:T(8,128)(2,1)} %get-tuple-element.70.k_ref, bf16[4,2048,128]{2,1,0:T(8,128)(2,1)} %get-tuple-element.71.v_ref), custom_call_target="tpu_custom_call" | custom-call | flops 8589934592 | bytes 10485760 | tf_op jit(solution)/shard_map/attend/pallas_call | solution.py:191
  217.9 31.5 %attention_sum.1 = (f32[512,1024]{1,0:T(8,128)}, f32[512,1024]{1,0:T(8,128)}, bf16[512,1024]{1,0:T(8,128)(2,1)}) custom-call(bf16[2048,256]{1,0:T(8,128)(2,1)} %get-tuple-element.73.rows_ref.attended_hbm, bf16[4096,1024]{1,0:T(8,128)(2,1)} %bitcast.18, f32[512,1024]{1,0:T(8,128)} %get-tuple-element.74.start_ref.start_hbm.unit_ref, ...), custom_call_target="tpu_custom_call" | custom-call | flops 1073741824 | bytes 16777216 | tf_op jit(solution)/shard_map/attention_sum/pallas_call | solution.py:581
  249.4 53.4 %mlp.1 = (f32[4,512,256]{2,1,0:T(8,128)}, bf16[4,512,1024]{2,1,0:T(8,128)(2,1)}, f32[2048,1024]{1,0:T(8,128)}, f32[2048,1024]{1,0:T(8,128)}, bf16[512,1024]{1,0:...) custom-call(bf16[512,1024]{1,0:T(8,128)(2,1)} %get-tuple-element.76.own_ref, bf16[4096,1024]{1,0:T(8,128)(2,1)} %bitcast.19, ...), custom_call_target="tpu_custom_call" | custom-call | flops 12884901888 | bytes 25165824 | tf_op jit(solution)/shard_map/mlp/pallas_call | solution.py:664
  302.8 64.2 %mlp_back.1 = (bf16[512,1024]{1,0:T(8,128)(2,1)}, f32[512,1024]{1,0:T(8,128)}, f32[1,1024]{1,0:T(1,128)}, f32[2,1024]{1,0:T(2,128)}, bf16[3072,1024]{1,0:T(8,128)(2,1)}) custom-call(bf16[512,1024]{1,0:T(8,128)(2,1)} %get-tuple-element.79.own_ref, bf16[4096,1024]{1,0:T(8,128)(2,1)} %bitcast.20, f32[2,1024]{1,0:T(2,128)} %scale_ref.3, ...), custom_call_target="tpu_custom_call" | custom-call | flops 12884901888 | bytes 50331648 | tf_op jit(solution)/shard_map/mlp_back/pallas_call | solution.py:851
  367.0 0.0 copy-start.8
  367.1 0.0 reduce-scatter.2.cloned.1.call-update
  367.1 0.7 compare_convert_fusion
  367.8 0.1 select_reduce_fusion
  367.9 0.7 copy.28.index_ref
  368.6 30.1 %attention_gather.1 = (bf16[2048,256]{1,0:T(8,128)(2,1)}, bf16[4,512,1024]{2,1,0:T(8,128)(2,1)}) custom-call(bf16[512,1024]{1,0:T(8,128)(2,1)} %get-tuple-element.87.own_ref, bf16[4096,1024]{1,0:T(8,128)(2,1)} %bitcast.21), custom_call_target="tpu_custom_call" | custom-call | flops 1073741824 | bytes 8388608 | tf_op jit(solution)/shard_map/attention_gather/pallas_call | solution.py:904
  398.7 42.1 %attend_back.1 = (f32[2048,256]{1,0:T(8,128)}, f32[2048,256]{1,0:T(8,128)}, f32[2048,256]{1,0:T(8,128)}) custom-call(bf16[4,2048,128]{2,1,0:T(8,128)(2,1)} %get-tuple-element.69.q_ref, bf16[4,2048,128]{2,1,0:T(8,128)(2,1)} %get-tuple-element.70.k_ref, bf16[4,2048,128]{2,1,0:T(8,128)(2,1)} %get-tuple-element.71.v_ref, ...), custom_call_target="tpu_custom_call" | custom-call | flops 21474836480 | bytes 20971520 | tf_op jit(solution)/shard_map/attend_back/pallas_call | solution.py:279
  440.8 10.7 %project_back.1 = (bf16[2048,768]{1,0:T(8,128)(2,1)}, f32[1,256]{1,0:T(1,128)}) custom-call(f32[2048,256]{1,0:T(8,128)} %get-tuple-element.89.dq_ref, f32[2048,256]{1,0:T(8,128)} %get-tuple-element.90.dk_ref, f32[2048,256]{1,0:T(8,128)} %get-tuple-element.91.dv_ref, f32[2048,256]{1,0:T(8,128)} %get-tuple-element.92.qr_ref, ...), custom_call_target="tpu_custom_call" | custom-call | flops 31457280 | bytes 13631488 | tf_op jit(solution)/shard_map/project_back/pallas_call | solution.py:328
  451.5 35.8 %start_sum.1 = (bf16[4,512,256]{2,1,0:T(8,128)(2,1)}, bf16[1024,1024]{1,0:T(8,128)(2,1)}) custom-call(bf16[2048,768]{1,0:T(8,128)(2,1)} %get-tuple-element.94.rows_ref, bf16[4096,1024]{1,0:T(8,128)(2,1)} %bitcast.22, f32[512,1024]{1,0:T(8,128)} %get-tuple-element.95.base_ref, f32[512,1024]{1,0:T(8,128)} %get-tuple-element.74.start_ref.start_hbm.unit_ref, ...), custom_call_target="tpu_custom_call" | custom-call | flops 3221225472 | bytes 16777216 | tf_op jit(solution)/shard_map/start_sum/pallas_call | solution.py:967
  487.3 0.0 reduce-scatter.2.cloned.1.call-done.home_ref
  487.3 137.8 %tail_sum.1 = (bf16[16,64,1024]{2,1,0:T(8,128)(2,1)}, bf16[8,384,1024]{2,1,0:T(8,128)(2,1)}, f32[8,1024]{1,0:T(8,128)}, f32[4,512,256]{2,1,0:T(8,128)}, bf16[4,512,256]{2,1,0:T(8,128)(2,1)}) custom-call(bf16[1024,1024]{1,0:T(8,128)(2,1)} %get-tuple-element.99.late_ref, bf16[384,1024]{1,0:T(8,128)(2,1)} %reduce-scatter.2.cloned.1.call-done.home_ref, ...), custom_call_target="tpu_custom_call" | custom-call | bytes 16777216 | tf_op jit(solution)/shard_map/tail_sum/pallas_call | solution.py:1262
  625.1 0.0 copy-start.2
  625.1 0.0 copy-start.3
  625.2 0.7 slice.10
  625.9 0.7 slice.9
  626.6 2.7 bitcast_convert_fusion
  629.3 1.4 multiply_subtract_fusion
  630.7 0.6 multiply_subtract_fusion.1
  631.4 15.0 %optimizer.1 = (f32[32,32,1024]{2,1,0:T(8,128)}, f32[32,32,1024]{2,1,0:T(8,128)}, f32[32,32,1024]{2,1,0:T(8,128)}, f32[32,32,1024]{2,1,0:T(8,128)}) custom-call(s32[32,2]{1,0:T(8,128)} %copy.28.index_ref, bf16[32,32,1024]{2,1,0:T(8,128)(2,1)} %bitcast.27, bf16[96,32,1024]{2,1,0:T(8,128)(2,1)} %bitcast.23, bf16[32,32,1024]{2,1,0:T(8,128)(2,1)} %bitcast.28, ...), custom_call_target="tpu_custom_call" | custom-call | flops 20971520 | bytes 31457280 | tf_op jit(solution)/shard_map/optimizer/pallas_call | solution.py:1333
  646.4 3.0 copy.30
  (17 shorter events, 0.1 us)
Async XLA Ops:
  7.2 480.2 %reduce-scatter.2.cloned.1.call-start = ((), (), s32[]{:S(2)}) async-start(), calls=%async_computation.1 | async-start | bytes 7077888 | tf_op jit(solution)/shard_map/reduce_scatter | solution.py:1776
  7.2 3.9 copy-start.6
  11.3 1.2 copy-start.7
  367.0 0.7 copy-start.8
  367.1 0.7 copy-start.9
  625.1 4.2 copy-start.1
  625.1 4.2 copy-start.2
  625.1 4.2 copy-start.3
  625.2 5.6 copy-start
  625.2 5.6 copy-start.4
  625.2 5.6 copy-start.5
Sparse Core Ops, SparseCore 0:
  367.2 117.2 reduce-scatter.1
